TPU v7x, 32 devices: a whole 2x2x4 slice. The times are simulated.
32 devices in a mesh: groups: 2 (over x), lon: 16 (over z, y, core).
Axes of the slice: x: 2, y: 2, z: 4, core: 2. Of those that a mesh axis runs over, the one named last changes fastest.
Arguments:
- input_field: bfloat16 [96, 512, 512], P('groups', 'lon'), parts along dimension 0, may hold values from -8 to 8
- expand_weight: bfloat16 [512, 2048], replicated, may hold values from -0.25 to 0.25
- expand_bias: float32 [2048], replicated, may hold values from -3 to 3
- depth_weight: float32 [9, 2048], replicated, may hold values from -2 to 2
- depth_bias: float32 [2048], replicated, may hold values from -3 to 3
- squeeze_down: bfloat16 [2048, 128], replicated, may hold values from -0.125 to 0.125
- squeeze_up: bfloat16 [128, 2048], replicated, may hold values from -3 to 3
- project_weight: bfloat16 [2048, 512], replicated, may hold values from -0.125 to 0.125
- block_gain: float32 [512], replicated, may hold values from 0.1 to 1.9
- block_in_weight: bfloat16 [512, 1536], replicated, may hold values from -4 to 4
- block_out_weight: bfloat16 [512, 512], replicated, may hold values from -0.25 to 0.25
- block_table: float32 [225, 16], replicated, may hold values from -5 to 5
- grid_gain: float32 [512], replicated, may hold values from 0.1 to 1.9
- grid_in_weight: bfloat16 [512, 1536], replicated, may hold values from -4 to 4
- grid_out_weight: bfloat16 [512, 512], replicated, may hold values from -0.25 to 0.25
- grid_table: float32 [225, 16], replicated, may hold values from -5 to 5
Outputs:
- output_field: bfloat16 [96, 512, 512], P('groups', 'lon'), parts along dimension 0
There are 2 independent parts, one for each index of `groups`. A program takes and returns all parts, laid end to end along the dimension named above; an argument that names none is the same for every part. Nothing has to cross between parts.
All inputs are finite; a program needn't handle non-finite values.
Results may differ from a plain program's by a relative error of at most 0.012.
Values may be sent and summed in bfloat16 or wider, within the bound.
No kernel may reach another device: no remote copies, remote signals or barrier semaphores. Data moves between devices by JAX's collectives and lax.ppermute only.
A program may use at most 128 MiB of HBM per device.

v0:
```python
import jax
import jax.numpy as jnp
from jax import lax
from jax.sharding import PartitionSpec as P

HEADS = 16
HEAD_DIM = 32


def extended(cells, sides, width):
    for axis, dim in sides:
        count = lax.axis_size(axis)
        head = lax.slice_in_dim(cells, 0, width, axis=dim)
        tail = lax.slice_in_dim(cells, cells.shape[dim] - width, cells.shape[dim], axis=dim)
        cells = jnp.concatenate(
            [
                lax.ppermute(tail, axis, [(i, (i + 1) % count) for i in range(count)]),
                cells,
                lax.ppermute(head, axis, [((i + 1) % count, i) for i in range(count)]),
            ],
            axis=dim,
        )
    return cells


def relative_bias(pos_table):
    position = jnp.arange(64)
    win_row = position // 8
    win_col = position % 8
    rel_index = (win_row[:, None] - win_row[None, :] + 7) * 15 + (
        win_col[:, None] - win_col[None, :] + 7
    )
    one_hot = (rel_index[:, :, None] == jnp.arange(225)[None, None, :]).astype(jnp.float32)
    return jnp.einsum("ijr,rh->hij", one_hot, pos_table, precision=lax.Precision.HIGHEST)


def layer_normed(stream, gain):
    widened = stream.astype(jnp.float32)
    average = jnp.mean(widened, axis=-1, keepdims=True)
    centred = widened - average
    variance = jnp.mean(centred * centred, axis=-1, keepdims=True)
    return (centred * lax.rsqrt(variance + 1e-05) * gain).astype(jnp.bfloat16)


def attend_windows(mixed, rel_bias):
    scores = jnp.einsum(
        "nqhd,nkhd->nhqk", mixed[:, :, 0], mixed[:, :, 1], preferred_element_type=jnp.float32
    )
    scores = scores * HEAD_DIM ** (-0.5) + rel_bias[None]
    scores = scores - jnp.max(scores, axis=-1, keepdims=True)
    exponent = jnp.exp(scores)
    probabilities = (exponent / jnp.sum(exponent, axis=-1, keepdims=True)).astype(jnp.bfloat16)
    return jnp.einsum(
        "nhqk,nkhd->nqhd", probabilities, mixed[:, :, 2], preferred_element_type=jnp.float32
    ).astype(jnp.bfloat16)


def expand_cells(cells, expand_weight, expand_bias):
    row_count, col_count, channels = cells.shape
    hidden = (
        jnp.dot(cells.reshape(-1, channels), expand_weight, preferred_element_type=jnp.float32)
        + expand_bias
    )
    return (
        jax.nn.gelu(hidden, approximate=False)
        .astype(jnp.bfloat16)
        .reshape(row_count, col_count, -1)
    )


def mbconv_block(
    input_field,
    expand_weight,
    expand_bias,
    depth_weight,
    depth_bias,
    squeeze_down,
    squeeze_up,
    project_weight,
):
    row_count, col_count, channels = input_field.shape
    hidden = expand_cells(input_field, expand_weight, expand_bias)
    rimmed = extended(hidden, (("lon", 1),), 1)
    padded = jnp.pad(rimmed, ((1, 1), (0, 0), (0, 0)))
    summed = depth_bias + jnp.zeros((row_count, col_count, depth_bias.shape[0]), jnp.float32)
    for row_off in range(3):
        for col_off in range(3):
            summed = (
                summed
                + padded[row_off : row_off + row_count, col_off : col_off + col_count].astype(
                    jnp.float32
                )
                * depth_weight[row_off * 3 + col_off]
            )
    active = jax.nn.gelu(summed, approximate=False).astype(jnp.bfloat16)
    partial_sum = jnp.sum(active, axis=(0, 1), dtype=jnp.float32)
    pooled = lax.psum(partial_sum, "lon") / (row_count * col_count * lax.axis_size("lon"))
    squeezed = jax.nn.silu(
        jnp.dot(pooled, squeeze_down.astype(jnp.float32), precision=lax.Precision.HIGHEST)
    )
    gate_value = jax.nn.sigmoid(
        jnp.dot(squeezed, squeeze_up.astype(jnp.float32), precision=lax.Precision.HIGHEST)
    )
    gated_act = (active * gate_value).astype(jnp.bfloat16)
    result = jnp.dot(
        gated_act.reshape(-1, gated_act.shape[-1]),
        project_weight,
        preferred_element_type=jnp.float32,
    )
    result = result + input_field.reshape(-1, channels).astype(jnp.float32)
    return result.astype(jnp.bfloat16).reshape(row_count, col_count, channels)


def block_attention(stream, gain, in_weight, out_weight, pos_table):
    row_count, col_count, channels = stream.shape
    normed = layer_normed(stream, gain)
    mixed = jnp.dot(
        normed.reshape(-1, channels), in_weight, preferred_element_type=jnp.float32
    ).astype(jnp.bfloat16)
    mixed = mixed.reshape(row_count // 8, 8, col_count // 8, 8, 3 * channels).transpose(
        0, 2, 1, 3, 4
    )
    mixed = mixed.reshape(-1, 64, 3, HEADS, HEAD_DIM)
    heads_out = attend_windows(mixed, relative_bias(pos_table))
    heads_out = (
        heads_out.reshape(row_count // 8, col_count // 8, 8, 8, channels)
        .transpose(0, 2, 1, 3, 4)
        .reshape(-1, channels)
    )
    merged = jnp.dot(heads_out, out_weight, preferred_element_type=jnp.float32) + stream.reshape(
        -1, channels
    ).astype(jnp.float32)
    return merged.astype(jnp.bfloat16).reshape(row_count, col_count, channels)


def grid_windows(tensor):
    row_count, items, lon_count, channels = tensor.shape
    shaped = tensor.reshape(8, row_count // 8, items, 8, lon_count // 8, channels)
    return shaped.transpose(1, 2, 4, 0, 3, 5).reshape(-1, 64, channels)


def grid_restore(windows, row_count, items, lon_count):
    channels = windows.shape[-1]
    shaped = windows.reshape(row_count // 8, items, lon_count // 8, 8, 8, channels)
    return shaped.transpose(3, 0, 1, 4, 2, 5).reshape(row_count, items, lon_count, channels)


def grid_attend(mixed, rel_bias):
    row_count, items, lon_count, triple_width = mixed.shape
    windows = grid_windows(mixed).reshape(-1, 64, 3, HEADS, HEAD_DIM)
    heads_out = attend_windows(windows, rel_bias).reshape(-1, 64, triple_width // 3)
    return grid_restore(heads_out, row_count, items, lon_count)


def grid_attention(stream, gain, in_weight, out_weight, pos_table):
    row_count, col_count, channels = stream.shape
    lon_count = lax.axis_size("lon")
    items = col_count // lon_count
    rel_bias = relative_bias(pos_table)
    normed = layer_normed(stream, gain)
    mixed = jnp.dot(
        normed.reshape(-1, channels), in_weight, preferred_element_type=jnp.float32
    ).astype(jnp.bfloat16)
    mixed = mixed.reshape(row_count, items, lon_count, 3 * channels)
    heads_out = grid_attend(
        lax.all_to_all(mixed, "lon", split_axis=2, concat_axis=2, tiled=True), rel_bias
    )
    returned = lax.all_to_all(heads_out, "lon", split_axis=2, concat_axis=2, tiled=True)
    merged = jnp.dot(returned.reshape(-1, channels), out_weight, preferred_element_type=jnp.float32)
    merged = merged + stream.reshape(-1, channels).astype(jnp.float32)
    return merged.astype(jnp.bfloat16).reshape(row_count, col_count, channels)


def per_device(
    input_field,
    expand_weight,
    expand_bias,
    depth_weight,
    depth_bias,
    squeeze_down,
    squeeze_up,
    project_weight,
    block_gain,
    block_in_weight,
    block_out_weight,
    block_table,
    grid_gain,
    grid_in_weight,
    grid_out_weight,
    grid_table,
):
    first_stream = mbconv_block(
        input_field,
        expand_weight,
        expand_bias,
        depth_weight,
        depth_bias,
        squeeze_down,
        squeeze_up,
        project_weight,
    )
    second_stream = block_attention(
        first_stream, block_gain, block_in_weight, block_out_weight, block_table
    )
    return grid_attention(second_stream, grid_gain, grid_in_weight, grid_out_weight, grid_table)


def solution(mesh):
    return jax.shard_map(
        per_device,
        mesh=mesh,
        in_specs=(
            P("groups", "lon", None),
            P(),
            P(),
            P(),
            P(),
            P(),
            P(),
            P(),
            P(),
            P(),
            P(),
            P(),
            P(),
            P(),
            P(),
            P(),
        ),
        out_specs=P("groups", "lon", None),
        check_vma=False,
    )
```

profile of v0, /device:TPU:0, one launch (start us, length us, event | category | flops | bytes accessed | tf_op | source)
XLA Modules:
  0.0 534.7 jit_solution(4356687229449048533)
XLA Ops:
  1.6 30.8 %fusion.6 = bf16[1536,2048]{1,0:T(8,128)(2,1)S(1)} fusion(bf16[1536,512]{1,0:T(8,128)(2,1)} %bitcast.114, bf16[512,2048]{1,0:T(8,128)(2,1)S(1)} %copy-done, f32[2048]{0:T(1024)} %param.18), kind=kOutput, calls=%fused_computation.12 | convolution fusion | flops 3428843520 | bytes 9969664 | tf_op jit(solution)/shard_map/dot_general | solution.py:61
  53.3 48.9 %convert_reduce_fusion = (f32[2048]{0:T(1024)S(1)}, bf16[48,32,2048]{2,1,0:T(8,128)(2,1)}) fusion(f32[2048]{0:T(1024)S(1)} %bitcast.110, bf16[50,34,2048]{2,1,0:T(8,128)(2,1)S(1)} %fusion.30, f32[2048]{0:T(1024)S(1)} %bitcast.111, f32[2048]{0:T(1024)S(1)} %bitcast.104, f32[2048]{0:T(1024)S(1)} %bitcast.105, ...), kind=kLoop, calls=%fused_computation.8 | loop fusion | flops 314570752 | bytes 50814976 | tf_op jit(solution)/shard_map/reduce_sum | solution.py:96
  102.2 35.0 %psum.7 = f32[2048]{0:T(1024)S(1)} all-reduce(f32[2048]{0:T(1024)S(1)} %get-tuple-element.5), channel_id=1, replica_groups=mesh['groups'=2,'lon'=16] {'lon'}, use_global_device_ids=true, to_apply=%region_1.2 | all-reduce | flops 2048 | bytes 16384 | tf_op jit(solution)/shard_map/psum | solution.py:97
  154.2 21.1 %reshape.215 = bf16[24,64,3,16,32]{4,3,2,1,0:T(8,128)(2,1)} reshape(bf16[6,4,8,8,1536]{4,3,2,1,0:T(8,128)(2,1)} %bitcast.94) | data formatting | bytes 9437184 | tf_op jit(solution)/shard_map/reshape | solution.py:123
  175.4 14.3 %fusion.88 = (bf16[24,64,1,16,32]{4,3,2,1,0:T(8,128)(2,1)}, bf16[24,64,1,16,32]{4,3,2,1,0:T(8,128)(2,1)}, bf16[24,64,1,16,32]{4,3,2,1,0:T(8,128)(2,1)}) fusion(bf16[24,64,3,16,32]{4,3,2,1,0:T(8,128)(2,1)} %reshape.215), kind=kLoop, calls=%fused_computation.139 | loop fusion | bytes 9437184 | tf_op jit(solution)/shard_map/slice | solution.py:54
  189.7 8.0 %copy.79 = bf16[24,64,1,16,32]{1,4,3,0,2:T(8,128)(2,1)} copy(bf16[24,64,1,16,32]{4,3,2,1,0:T(8,128)(2,1)} %get-tuple-element.11) | data formatting | bytes 3145728
  197.7 8.0 %copy.80 = bf16[24,64,1,16,32]{1,4,3,0,2:T(8,128)(2,1)} copy(bf16[24,64,1,16,32]{4,3,2,1,0:T(8,128)(2,1)} %get-tuple-element.12) | data formatting | bytes 3145728
  205.7 8.0 %copy.78 = bf16[24,64,1,16,32]{1,4,3,0,2:T(8,128)(2,1)} copy(bf16[24,64,1,16,32]{4,3,2,1,0:T(8,128)(2,1)} %get-tuple-element.10) | data formatting | bytes 3145728
  218.5 8.2 %fusion.91 = (f32[24,16,64]{2,1,0:T(8,128)S(1)}, f32[24,16,64,64]{2,3,1,0:T(8,128)}) fusion(f32[24,16,64,64]{2,3,1,0:T(8,128)S(1)} %fusion.53, f32[16,64,64]{1,2,0:T(8,128)S(1)} %copy.58), kind=kOutput, calls=%fused_computation.142 | output fusion | flops 9437247 | bytes 12943360 | tf_op jit(solution)/shard_map/sub | solution.py:50
  226.7 9.0 %convert_bitcast_fusion.1 = bf16[24,64,16,32]{1,3,2,0:T(8,128)(2,1)} fusion(f32[24,16,64,64]{2,3,1,0:T(8,128)} %get-tuple-element.27, f32[24,16,64]{2,1,0:T(8,128)S(1)} %get-tuple-element.26, bf16[24,64,1,16,32]{1,4,3,0,2:T(8,128)(2,1)} %copy.78), kind=kOutput, calls=%fused_computation.100 | convolution fusion | flops 104595456 | bytes 9535488 | tf_op jit(solution)/shard_map/nhqk,nkhd->nqhd/dot_general | solution.py:53
  235.7 7.9 %copy.60 = bf16[24,64,16,32]{3,2,1,0:T(8,128)(2,1)} copy(bf16[24,64,16,32]{1,3,2,0:T(8,128)(2,1)} %convert_bitcast_fusion.1) | data formatting | bytes 3145728 | tf_op jit(solution)/shard_map/convert_element_type | solution.py:55
  243.6 8.4 %reshape.216 = bf16[6,4,8,8,512]{4,3,2,1,0:T(8,128)(2,1)S(1)} reshape(bf16[24,64,16,32]{3,2,1,0:T(8,128)(2,1)} %copy.60) | data formatting | bytes 3145728 | tf_op jit(solution)/shard_map/reshape | solution.py:126
  261.6 9.4 %copy.62 = bf16[48,2,16,1536]{3,1,0,2:T(2,128)(2,1)} copy(bf16[48,2,16,1536]{3,2,1,0:T(8,128)(2,1)} %bitcast.100) | data formatting | bytes 9437184 | tf_op jit(solution)/shard_map/reshape | solution.py:164
  279.2 83.2 %all-to-all-done = bf16[48,2,16,1536]{3,1,0,2:T(2,128)(2,1)} async-done(((bf16[48,2,16,1536]{3,1,0,2:T(2,128)(2,1)}), bf16[48,2,16,1536]{3,1,0,2:T(2,128)(2,1)}, u32[]{:S(2)}, u32[]{:S(2)}) %all-to-all-start) | async-done | bytes 4718624 | tf_op jit(solution)/shard_map/all_to_all | solution.py:166
  369.5 21.1 %reshape_reshape.6 = bf16[24,64,3,16,32]{4,3,2,1,0:T(8,128)(2,1)} reshape(bf16[6,2,2,8,8,1536]{5,4,3,2,1,0:T(8,128)(2,1)} %copy.64) | data formatting | bytes 9437184 | tf_op jit(solution)/shard_map/reshape;reshape | solution.py:150
  390.7 14.3 %fusion.87 = (bf16[24,64,1,16,32]{4,3,2,1,0:T(8,128)(2,1)}, bf16[24,64,1,16,32]{4,3,2,1,0:T(8,128)(2,1)}, bf16[24,64,1,16,32]{4,3,2,1,0:T(8,128)(2,1)}) fusion(bf16[24,64,3,16,32]{4,3,2,1,0:T(8,128)(2,1)} %reshape_reshape.6), kind=kLoop, calls=%fused_computation.138 | loop fusion | bytes 9437184 | tf_op jit(solution)/shard_map/slice | solution.py:54
  405.0 8.0 %copy.82 = bf16[24,64,1,16,32]{1,4,3,0,2:T(8,128)(2,1)} copy(bf16[24,64,1,16,32]{4,3,2,1,0:T(8,128)(2,1)} %get-tuple-element.8) | data formatting | bytes 3145728
  413.0 8.0 %copy.83 = bf16[24,64,1,16,32]{1,4,3,0,2:T(8,128)(2,1)} copy(bf16[24,64,1,16,32]{4,3,2,1,0:T(8,128)(2,1)} %get-tuple-element.9) | data formatting | bytes 3145728
  421.0 8.0 %copy.81 = bf16[24,64,1,16,32]{1,4,3,0,2:T(8,128)(2,1)} copy(bf16[24,64,1,16,32]{4,3,2,1,0:T(8,128)(2,1)} %get-tuple-element.7) | data formatting | bytes 3145728
  433.8 8.3 %fusion.92 = (f32[24,16,64]{2,1,0:T(8,128)S(1)}, f32[24,16,64,64]{2,3,1,0:T(8,128)}) fusion(f32[24,16,64,64]{2,3,1,0:T(8,128)S(1)} %fusion.49, f32[16,64,64]{1,2,0:T(8,128)S(1)} %copy.68), kind=kOutput, calls=%fused_computation.143 | output fusion | flops 9437247 | bytes 12943360 | tf_op jit(solution)/shard_map/sub | solution.py:50
  442.1 9.0 %convert_bitcast_fusion = bf16[24,64,16,32]{1,3,2,0:T(8,128)(2,1)} fusion(f32[24,16,64,64]{2,3,1,0:T(8,128)} %get-tuple-element.31, f32[24,16,64]{2,1,0:T(8,128)S(1)} %get-tuple-element.30, bf16[24,64,1,16,32]{1,4,3,0,2:T(8,128)(2,1)} %copy.81), kind=kOutput, calls=%fused_computation.99 | convolution fusion | flops 104595456 | bytes 9535488 | tf_op jit(solution)/shard_map/nhqk,nkhd->nqhd/dot_general | solution.py:53
  451.1 8.0 %copy.70 = bf16[24,64,16,32]{3,2,1,0:T(8,128)(2,1)} copy(bf16[24,64,16,32]{1,3,2,0:T(8,128)(2,1)} %convert_bitcast_fusion) | data formatting | bytes 3145728 | tf_op jit(solution)/shard_map/convert_element_type | solution.py:55
  459.1 9.3 %reshape_reshape.7 = bf16[6,2,2,8,8,512]{5,4,3,2,1,0:T(8,128)(2,1)} reshape(bf16[24,64,16,32]{3,2,1,0:T(8,128)(2,1)} %copy.70) | data formatting | bytes 3145728 | tf_op jit(solution)/shard_map/reshape;reshape | solution.py:144
  471.4 57.6 %all_to_all.10 = bf16[48,2,16,512]{3,1,0,2:T(2,128)(2,1)S(1)} all-to-all(bf16[48,2,16,512]{3,1,0,2:T(2,128)(2,1)S(1)} %bitcast.95), channel_id=1, replica_groups=mesh['groups'=2,'lon'=16] {'lon'}, dimensions={2} | all-to-all | bytes 3145728 | tf_op jit(solution)/shard_map/all_to_all | solution.py:168
  (71 shorter events, 82.0 us)
Async XLA Ops:
  0.0 1.6 copy-start
  1.6 39.7 %copy-start.7 = (f32[9,2048]{1,0:T(8,128)S(1)}, f32[9,2048]{1,0:T(8,128)}, u32[]{:S(2)}) copy-start(f32[9,2048]{1,0:T(8,128)} %param.19) | copy-start | bytes 221188
  1.6 39.9 %copy-start.13 = (f32[225,16]{0,1:T(8,128)S(1)}, f32[225,16]{0,1:T(8,128)}, u32[]{:S(2)}) copy-start(f32[225,16]{0,1:T(8,128)} %param.27) | copy-start | bytes 43204
  32.4 2.7 copy-start.2
  32.4 20.8 %copy-start.8 = (f32[2048]{0:T(1024)S(1)}, f32[2048]{0:T(1024)}, u32[]{:S(2)}) copy-start(f32[2048]{0:T(1024)} %param.20) | copy-start | bytes 24580
  35.7 11.1 %collective-permute-start = (bf16[48,1,2048]{2,1,0:T(2,128)(2,1)S(1)}, bf16[48,1,2048]{2,1,0:T(2,128)(2,1)S(1)}, u32[]{:S(2)}, u32[]{:S(2)}) collective-permute-start(bf16[48,1,2048]{2,1,0:T(2,128)(2,1)S(1)} %get-tuple-element.13), channel_id=1, source_target_pairs={{0,1},{1,2},{2,3},{3,4},{4,5},{5,6},{6,7},{7,8},{8,9},{9,10},{10,1... | collective-permute-start | bytes 589832 | tf_op jit(solution)/shard_map/ppermute | solution.py:17
  36.2 10.6 %collective-permute-start.1 = (bf16[48,1,2048]{2,1,0:T(2,128)(2,1)S(1)}, bf16[48,1,2048]{2,1,0:T(2,128)(2,1)S(1)}, u32[]{:S(2)}, u32[]{:S(2)}) collective-permute-start(bf16[48,1,2048]{2,1,0:T(2,128)(2,1)S(1)} %get-tuple-element.14), channel_id=1, source_target_pairs={{1,0},{2,1},{3,2},{4,3},{5,4},{6,5},{7,6},{8,7},{9,8},{10,9},{11,1... | collective-permute-start | bytes 589832 | tf_op jit(solution)/shard_map/ppermute | solution.py:19
  53.3 83.9 %copy-start.5 = (bf16[2048,128]{1,0:T(8,128)(2,1)S(1)}, bf16[2048,128]{1,0:T(8,128)(2,1)}, u32[]{:S(2)}) copy-start(bf16[2048,128]{1,0:T(8,128)(2,1)} %param.21) | copy-start | bytes 1572868
  53.3 84.2 %copy-start.6 = (bf16[128,2048]{1,0:T(8,128)(2,1)S(1)}, bf16[128,2048]{1,0:T(8,128)(2,1)}, u32[]{:S(2)}) copy-start(bf16[128,2048]{1,0:T(8,128)(2,1)} %param.22) | copy-start | bytes 1572868
  137.1 5.3 copy-start.9
  142.4 5.9 %copy-start.10 = (bf16[512,1536]{1,0:T(8,128)(2,1)S(1)}, bf16[512,1536]{1,0:T(8,128)(2,1)}, u32[]{:S(2)}) copy-start(bf16[512,1536]{1,0:T(8,128)(2,1)} %param.25) | copy-start | bytes 4718596
  142.4 5.9 %copy-start.15 = (f32[512]{0:T(512)S(1)}, f32[512]{0:T(512)}, u32[]{:S(2)}) copy-start(f32[512]{0:T(512)} %param.24) | copy-start | bytes 6148
  147.4 6.8 %copy-start.4 = (bf16[1536,512]{1,0:T(8,128)(2,1)}, bf16[1536,512]{1,0:T(8,128)(2,1)S(1)}, u32[]{:S(2)}) copy-start(bf16[1536,512]{1,0:T(8,128)(2,1)S(1)} %get-tuple-element.25) | copy-start | bytes 4718596
  235.7 16.5 %copy-start.11 = (bf16[512,512]{1,0:T(8,128)(2,1)S(1)}, bf16[512,512]{1,0:T(8,128)(2,1)}, u32[]{:S(2)}) copy-start(bf16[512,512]{1,0:T(8,128)(2,1)} %param.26) | copy-start | bytes 1572868
  235.7 19.9 %copy-start.16 = (f32[512]{0:T(512)S(1)}, f32[512]{0:T(512)}, u32[]{:S(2)}) copy-start(f32[512]{0:T(512)} %param.28) | copy-start | bytes 6148
  254.7 16.3 %copy-start.3 = (bf16[1536,512]{1,0:T(8,128)(2,1)}, bf16[1536,512]{1,0:T(8,128)(2,1)S(1)}, u32[]{:S(2)}) copy-start(bf16[1536,512]{1,0:T(8,128)(2,1)S(1)} %get-tuple-element.29) | copy-start | bytes 4718596
  261.6 14.1 %copy-start.14 = (f32[225,16]{0,1:T(8,128)S(1)}, f32[225,16]{0,1:T(8,128)}, u32[]{:S(2)}) copy-start(f32[225,16]{0,1:T(8,128)} %param.31) | copy-start | bytes 43204
  271.0 91.5 %all-to-all-start = ((bf16[48,2,16,1536]{3,1,0,2:T(2,128)(2,1)}), bf16[48,2,16,1536]{3,1,0,2:T(2,128)(2,1)}, u32[]{:S(2)}, u32[]{:S(2)}) async-start(bf16[48,2,16,1536]{3,1,0,2:T(2,128)(2,1)} %copy.62), calls=%async_computation | async-start | bytes 9437184 | tf_op jit(solution)/shard_map/all_to_all | solution.py:166
  451.1 79.6 %copy-start.12 = (bf16[512,512]{1,0:T(8,128)(2,1)S(1)}, bf16[512,512]{1,0:T(8,128)(2,1)}, u32[]{:S(2)}) copy-start(bf16[512,512]{1,0:T(8,128)(2,1)} %param.30) | copy-start | bytes 1572868
  451.1 83.2 %copy-start.1 = (bf16[512,2048]{1,0:T(8,128)(2,1)S(1)}, bf16[512,2048]{1,0:T(8,128)(2,1)}, u32[]{:S(2)}) copy-start(bf16[512,2048]{1,0:T(8,128)(2,1)} %param.17) | copy-start | bytes 6291460
where the time goes:
time: 544 us; the launch traced here: 535 us
  local copies, waits for them, and re-layouts  182 us (33%)
  blocking collectives  92.5 us (17%)
  matrix products  85.6 us (16%)
  waiting for transfers between devices  85.1 us (16%)
  other arithmetic  78.1 us (14%)
  starting transfers between devices  10.3 us (2%)
    all_to_all x1, waiting for transfers between devices, grid_attention(): lax.all_to_all(mixed, 'lon', split_axis=2, concat_axis=2, tiled=True)  83.2 us
    all_to_all x1, blocking collectives, grid_attention(): lax.all_to_all(heads_out, 'lon', split_axis=2, concat_axis=2, tiled=True)  57.6 us
    unnamed x40, local copies, waits for them, and re-layouts  52.4 us
    reduce_sum x1, other arithmetic, mbconv_block(): partial_sum = jnp.sum(active, axis=(0, 1), dtype=jnp.float32)  48.9 us
    psum x1, blocking collectives, mbconv_block(): lax.psum(partial_sum, 'lon')  35 us
    dot_general x1, matrix products, expand_cells(): jnp.dot(cells.reshape(-1, channels), expand_weight, preferred_element_typ...  30.8 us
    slice x2, local copies, waits for them, and re-layouts, attend_windows(): mixed[:, :, 2]  28.7 us
    reshape x1, local copies, waits for them, and re-layouts, block_attention(): mixed = mixed.reshape(-1, 64, 3, HEADS, HEAD_DIM)  21.1 us
  transfers between devices with their start and end apart: 3, of which 2 were waited for; matrix products, arithmetic and copies ran while one was open for 1% of the time, Pallas kernels for 0%

commit v1 on v0

v1 whole, which is shorter than its diff:
```python
import functools

import jax
import jax.numpy as jnp
import numpy as np
from jax import lax
from jax.experimental import pallas as pl
from jax.experimental.pallas import tpu as pltpu
from jax.sharding import PartitionSpec as P

HEADS = 16
HEAD_DIM = 32
WIN = 8
CELLS = WIN * WIN
CHUNKS = (2, 2)
LANES = 256
LOG2E = 1.4426950408889634
SCORE_SCALE = HEAD_DIM ** (-0.5) * LOG2E
BF16 = jnp.bfloat16
F32 = jnp.float32


def gelu(value):
    return 0.5 * value * (1.0 + lax.erf(value * 0.7071067811865476))


def mbconv_kernel(x_ref, w_ref, b_ref, dw_ref, db_ref, down_ref, act_ref, part_ref, hid_ref):
    cols, rows, channels = x_ref.shape
    lanes = w_ref.shape[1]
    step = 2
    bias = b_ref[...]

    def expand(i, carry):
        cells = x_ref[pl.ds(i * step, step)].reshape(step * rows, channels)
        hidden = jnp.dot(cells, w_ref[...], preferred_element_type=F32) + bias
        hid_ref[pl.ds(i * step, step)] = gelu(hidden).reshape(step, rows, lanes)
        return carry

    lax.fori_loop(0, cols // step, expand, 0)
    row = lax.broadcasted_iota(jnp.int32, (rows, lanes), 0)
    first = row == 0
    last = row == rows - 1
    taps = dw_ref[...]
    shift = db_ref[...]

    def depth(c, total):
        sums = []
        for r in range(3):
            acc = hid_ref[c] * taps[3 * r : 3 * r + 1]
            acc = acc + hid_ref[c + 1] * taps[3 * r + 1 : 3 * r + 2]
            acc = acc + hid_ref[c + 2] * taps[3 * r + 2 : 3 * r + 3]
            sums.append(acc)
        above = jnp.where(first, 0.0, pltpu.roll(sums[0], 1, 0))
        below = jnp.where(last, 0.0, pltpu.roll(sums[2], rows - 1, 0))
        active = gelu(sums[1] + above + (below + shift))
        act_ref[c] = active.astype(BF16)
        return total + active.reshape(rows // 8, 8, lanes).sum(0)

    total = lax.fori_loop(0, cols - 2, depth, jnp.zeros((8, lanes), F32))
    pooled = jnp.sum(total, axis=0, keepdims=True)
    part = jnp.dot(
        jnp.broadcast_to(pooled, (8, lanes)),
        down_ref[...].astype(F32),
        precision=lax.Precision.HIGHEST,
        preferred_element_type=F32,
    )

    @pl.when(pl.program_id(0) == 0)
    def _():
        part_ref[...] = part

    @pl.when(pl.program_id(0) > 0)
    def _():
        part_ref[...] += part


def mbconv(rimmed, expand_weight, expand_bias, depth_weight, depth_bias, squeeze_down):
    cols, rows, channels = rimmed.shape
    expanded = expand_weight.shape[1]
    squeeze = squeeze_down.shape[1]
    return pl.pallas_call(
        mbconv_kernel,
        name="mbconv",
        grid=(expanded // LANES,),
        in_specs=[
            pl.BlockSpec((cols, rows, channels), lambda i: (0, 0, 0), pipeline_mode=pl.Buffered(1)),
            pl.BlockSpec((channels, LANES), lambda i: (0, i)),
            pl.BlockSpec((1, LANES), lambda i: (0, i)),
            pl.BlockSpec((9, LANES), lambda i: (0, i)),
            pl.BlockSpec((1, LANES), lambda i: (0, i)),
            pl.BlockSpec((LANES, squeeze), lambda i: (i, 0)),
        ],
        out_specs=[
            pl.BlockSpec((cols - 2, rows, LANES), lambda i: (0, 0, i)),
            pl.BlockSpec((8, squeeze), lambda i: (0, 0)),
        ],
        out_shape=[
            jax.ShapeDtypeStruct((cols - 2, rows, expanded), BF16),
            jax.ShapeDtypeStruct((8, squeeze), F32),
        ],
        scratch_shapes=[pltpu.VMEM((cols, rows, LANES), F32)],
        cost_estimate=pl.CostEstimate(
            flops=2 * cols * rows * channels * expanded * 4,
            bytes_accessed=20_000_000,
            transcendentals=0,
        ),
        compiler_params=pltpu.CompilerParams(vmem_limit_bytes=32 << 20),
    )(
        rimmed,
        expand_weight,
        expand_bias.reshape(1, -1),
        depth_weight,
        depth_bias.reshape(1, -1),
        squeeze_down,
    )


def attend(stream, gain_ref, wq_ref, wk_ref, wv_ref, wo_ref, bias_ref, mask_ref, scratch):
    q_ref, k_ref, vt_ref, o_ref = scratch
    cells, channels = stream.shape
    average = jnp.mean(stream, axis=-1, keepdims=True)
    centred = stream - average
    variance = jnp.mean(centred * centred, axis=-1, keepdims=True)
    normed = (centred * lax.rsqrt(variance + 1e-05) * gain_ref[...]).astype(BF16)
    q_ref[...] = jnp.dot(normed, wq_ref[...], preferred_element_type=F32).astype(BF16)
    k_ref[...] = jnp.dot(normed, wk_ref[...], preferred_element_type=F32).astype(BF16)
    vt_ref[...] = lax.dot_general(
        wv_ref[...], normed, (((1,), (1,)), ((), ())), preferred_element_type=F32
    ).astype(BF16)
    mask = mask_ref[...]
    group = 256 // HEAD_DIM
    even = (lax.broadcasted_iota(jnp.int32, (CELLS, 128), 1) // HEAD_DIM) % 2 == 0
    for w in range(cells // CELLS):
        span = slice(w * CELLS, (w + 1) * CELLS)
        for g in range(HEADS // group):
            part = slice(g * 256, (g + 1) * 256)
            query = jnp.concatenate([q_ref[span, part]] * group, axis=0) * mask
            lanes = slice(g * group * CELLS, (g + 1) * group * CELLS)
            scores = lax.dot_general(
                k_ref[span, part], query, (((1,), (1,)), ((), ())), preferred_element_type=F32
            )
            scores = scores * SCORE_SCALE + bias_ref[:, lanes]
            scores = jnp.exp2(scores - jnp.max(scores, axis=0, keepdims=True))
            weight = 1.0 / jnp.sum(scores, axis=0, keepdims=True)
            prob = (scores * weight).astype(BF16)
            for quad in range(group // 4):
                halves = []
                for pair in (2 * quad, 2 * quad + 1):
                    values = vt_ref[g * 256 + pair * 64 : g * 256 + pair * 64 + 64, span]
                    halves.append(
                        jnp.dot(
                            values,
                            prob[:, pair * 128 : pair * 128 + 128],
                            preferred_element_type=F32,
                        )
                    )
                turned = jnp.concatenate(halves, axis=0).T
                picked = jnp.where(even, turned[:CELLS], turned[CELLS:])
                o_ref[span, g * 256 + quad * 128 : g * 256 + quad * 128 + 128] = picked.astype(BF16)
    return stream + jnp.dot(o_ref[...], wo_ref[...], preferred_element_type=F32)


def block_kernel(
    act_ref, x_ref, part_ref, up_ref, proj_ref, gain_ref, wq_ref, wk_ref, wv_ref, wo_ref,
    bias_ref, mask_ref, out_ref, gate_ref, *scratch,
):
    cols, rows, expanded = act_ref.shape
    channels = x_ref.shape[2]

    @pl.when(pl.program_id(0) == 0)
    def _():
        squeezed = jnp.broadcast_to(part_ref[...], (8, part_ref.shape[1]))
        squeezed = squeezed * jax.nn.sigmoid(squeezed)
        gate = jnp.dot(
            squeezed,
            up_ref[...].astype(F32),
            precision=lax.Precision.HIGHEST,
            preferred_element_type=F32,
        )
        gate_ref[...] = jax.nn.sigmoid(gate)

    gated = act_ref[...].reshape(cols * rows, expanded).astype(F32) * gate_ref[0:1]
    first = jnp.dot(gated.astype(BF16), proj_ref[...], preferred_element_type=F32)
    first = first.reshape(cols, rows, channels) + x_ref[...].astype(F32)
    first = first.astype(BF16).astype(F32)
    windows = rows // WIN
    stream = jnp.concatenate(
        [first[:, a * WIN : (a + 1) * WIN].reshape(CELLS, channels) for a in range(windows)],
        axis=0,
    )
    second = attend(
        stream, gain_ref, wq_ref, wk_ref, wv_ref, wo_ref, bias_ref, mask_ref, scratch
    ).reshape(windows, cols, WIN, channels)
    second = jnp.concatenate([second[a] for a in range(windows)], axis=1)
    out_ref[...] = second.reshape(out_ref.shape).astype(BF16)


def grid_kernel(
    s_ref, perm_ref, back_ref, gain_ref, wq_ref, wk_ref, wv_ref, wo_ref,
    bias_ref, mask_ref, out_ref, *scratch,
):
    cells = perm_ref.shape[0]
    channels = s_ref.shape[-1]
    incoming = s_ref[...].reshape(cells, channels)
    stream = jnp.dot(perm_ref[...], incoming, preferred_element_type=F32)
    result = attend(
        stream, gain_ref, wq_ref, wk_ref, wv_ref, wo_ref, bias_ref, mask_ref, scratch
    ).astype(BF16)
    result = jnp.dot(back_ref[...], result, preferred_element_type=F32)
    out_ref[...] = result.astype(BF16).reshape(out_ref.shape)


def whole(shape):
    return pl.BlockSpec(shape, lambda *_: (0,) * len(shape), pipeline_mode=pl.Buffered(1))


def attention_scratch(cells, channels):
    return [
        pltpu.VMEM((cells, channels), BF16),
        pltpu.VMEM((cells, channels), BF16),
        pltpu.VMEM((channels, cells), BF16),
        pltpu.VMEM((cells, channels), BF16),
    ]


def block_stage(start, count, active, field, part, up, proj, params):
    cols, rows, channels = field.shape
    expanded = active.shape[2]
    cells = WIN * rows
    return pl.pallas_call(
        block_kernel,
        name="block_stage",
        grid=(count,),
        in_specs=[
            pl.BlockSpec((WIN, rows, expanded), lambda b: (b + start, 0, 0)),
            pl.BlockSpec((WIN, rows, channels), lambda b: (b + start, 0, 0)),
        ]
        + [whole(p.shape) for p in (part, up, proj, *params)],
        out_specs=pl.BlockSpec((WIN, 1, rows, channels), lambda b: (0, b, 0, 0)),
        out_shape=jax.ShapeDtypeStruct((WIN, count, rows, channels), BF16),
        scratch_shapes=[pltpu.VMEM((8, expanded), F32)] + attention_scratch(cells, channels),
        cost_estimate=pl.CostEstimate(
            flops=2 * count * cells * channels * (expanded + 4 * channels) * 4,
            bytes_accessed=8_000_000,
            transcendentals=0,
        ),
        compiler_params=pltpu.CompilerParams(vmem_limit_bytes=32 << 20),
    )(active, field, part, up, proj, *params)


def grid_stage(received, perm, back, params):
    _, count, rows, channels = received.shape
    cells = WIN * rows
    spec = pl.BlockSpec((WIN, 1, rows, channels), lambda b: (0, b, 0, 0))
    return pl.pallas_call(
        grid_kernel,
        name="grid_stage",
        grid=(count,),
        in_specs=[spec] + [whole(p.shape) for p in (perm, back, *params)],
        out_specs=spec,
        out_shape=jax.ShapeDtypeStruct(received.shape, BF16),
        scratch_shapes=attention_scratch(cells, channels),
        cost_estimate=pl.CostEstimate(
            flops=2 * count * cells * channels * 4 * channels * 4,
            bytes_accessed=6_000_000,
            transcendentals=0,
        ),
        compiler_params=pltpu.CompilerParams(vmem_limit_bytes=32 << 20),
    )(received, perm, back, *params)


def turned_bias(pos_table):
    position = jnp.arange(CELLS)
    row = position % WIN
    col = position // WIN
    index = (row[None, :] - row[:, None] + 7) * 15 + (col[None, :] - col[:, None] + 7)
    one_hot = (index[:, :, None] == jnp.arange(225)[None, None, :]).astype(F32)
    bias = jnp.einsum("jir,rh->jhi", one_hot, pos_table * LOG2E, precision=lax.Precision.HIGHEST)
    return bias.reshape(CELLS, HEADS * CELLS)


def attention_params(gain, in_weight, out_weight, pos_table, mask):
    channels = gain.shape[0]
    return (
        gain.reshape(1, -1),
        in_weight[:, :channels],
        in_weight[:, channels : 2 * channels],
        in_weight[:, 2 * channels :].T,
        out_weight,
        turned_bias(pos_table),
        mask,
    )


def head_mask():
    group = 256 // HEAD_DIM
    head = np.arange(group * CELLS) // CELLS
    lane = np.arange(256) // HEAD_DIM
    return jnp.asarray(head[:, None] == lane[None, :], BF16)


def grid_order(rows):
    per = rows // WIN
    source = np.zeros(WIN * rows, np.int64)
    for a in range(per):
        for j in range(WIN):
            for i in range(WIN):
                source[(a * WIN + j) * WIN + i] = j * rows + i * per + a
    one_hot = source[:, None] == np.arange(WIN * rows)[None, :]
    return jnp.asarray(one_hot, BF16), jnp.asarray(one_hot.T, BF16)


def per_device(
    input_field,
    expand_weight,
    expand_bias,
    depth_weight,
    depth_bias,
    squeeze_down,
    squeeze_up,
    project_weight,
    block_gain,
    block_in_weight,
    block_out_weight,
    block_table,
    grid_gain,
    grid_in_weight,
    grid_out_weight,
    grid_table,
):
    rows, cols, channels = input_field.shape
    count = lax.axis_size("lon")
    per = count // WIN
    groups = [[j * per + r for j in range(WIN)] for r in range(per)]
    field = jnp.swapaxes(input_field, 0, 1)
    before = lax.ppermute(field[-1:], "lon", [(i, (i + 1) % count) for i in range(count)])
    after = lax.ppermute(field[:1], "lon", [((i + 1) % count, i) for i in range(count)])
    rimmed = jnp.concatenate([before, field, after], axis=0)
    active, part = mbconv(
        rimmed, expand_weight, expand_bias, depth_weight, depth_bias, squeeze_down
    )
    parts = lax.all_to_all(
        jnp.broadcast_to(part[None, :1], (count, 1, part.shape[1])), "lon", 0, 0, tiled=True
    )
    part = jnp.sum(parts, axis=0) / (rows * cols * count)
    mask = head_mask()
    perm, back = grid_order(rows)
    block_params = attention_params(
        block_gain, block_in_weight, block_out_weight, block_table, mask
    )
    grid_params = attention_params(grid_gain, grid_in_weight, grid_out_weight, grid_table, mask)
    exchange = functools.partial(
        lax.all_to_all,
        axis_name="lon",
        split_axis=0,
        concat_axis=0,
        axis_index_groups=groups,
        tiled=True,
    )
    results = []
    start = 0
    total = cols // WIN
    for size in CHUNKS if sum(CHUNKS) == total else (total,):
        sent = block_stage(
            start, size, active, field, part, squeeze_up, project_weight, block_params
        )
        start += size
        result = grid_stage(exchange(sent), perm, back, grid_params)
        results.append(exchange(result))
    merged = jnp.concatenate(results, axis=1)
    return merged.transpose(2, 1, 0, 3).reshape(rows, cols, channels)


def solution(mesh):
    return jax.shard_map(
        per_device,
        mesh=mesh,
        in_specs=(P("groups", "lon", None),) + (P(),) * 15,
        out_specs=P("groups", "lon", None),
        check_vma=False,
    )
```

time: 544 us -> 197 us (0.36); the launches traced: 535 us -> 196 us
  local copies, waits for them, and re-layouts: 182 us -> 41.6 us
  Pallas kernels: 0 us -> 91 us
  matrix products: 85.6 us -> 5.24 us
  waiting for transfers between devices: 85.1 us -> 6.2 us
  other arithmetic: 78.1 us -> 1.59 us
  blocking collectives: 92.5 us -> 23.6 us
  starting transfers between devices: 10.3 us -> 26.3 us
    pallas_call x0 -> x5, Pallas kernels: none -> 91 us  [the longest x1 44.7 us: mbconv(): pl.pallas_call(mbconv_kernel, name='mbconv', grid=(expanded // LANES,), i...]
    dot_general x14 -> x2, matrix products: 85.6 us -> 5.24 us  [turned_bias(): jnp.einsum('jir,rh->jhi', one_hot, pos_table * LOG2E, precision=lax.Preci...]
    all_to_all x1 -> x4, waiting for transfers between devices: 83.2 us -> 5.48 us  [the longest x1 3.24 us: per_device(): results.append(exchange(result))]
    reduce_sum x3 -> x1, other arithmetic: 50.5 us -> 0.02 us  [per_device(): part = jnp.sum(parts, axis=0) / (rows * cols * count)]
    reshape x5 -> x2, local copies, waits for them, and re-layouts: 44.6 us -> 0.36 us  [turned_bias(): return bias.reshape(CELLS, HEADS * CELLS)]
    psum x1 -> x0, blocking collectives: 35 us -> none  [mbconv_block(): lax.psum(partial_sum, 'lon')]
    all_to_all x1, blocking collectives: 57.6 us -> 23.6 us  [per_device(): results.append(exchange(result))]
    another operation x2 -> x0, local copies, waits for them, and re-layouts: 30.4 us -> none  [the longest x1 21.1 us: grid_attend(): windows = grid_windows(mixed).reshape(-1, 64, 3, HEADS, HEAD_DIM)]
  transfers between devices with their start and end apart: 3 -> 6, of which waited for: 2 -> 3; matrix products, arithmetic and copies ran while one was open for 1% -> 6% of each run, Pallas kernels for 0% -> 17%
where the time goes in v1:
time: 197 us; the launch traced here: 196 us
  Pallas kernels  91 us (46%)
  local copies, waits for them, and re-layouts  41.6 us (21%)
  starting transfers between devices  26.3 us (13%)
  blocking collectives  23.6 us (12%)
  waiting for transfers between devices  6.2 us (3%)
  matrix products  5.24 us (3%)
    pallas_call x1, Pallas kernels, mbconv(): pl.pallas_call(mbconv_kernel, name='mbconv', grid=(expanded // LANES,), i...  44.7 us
    unnamed x77, local copies, waits for them, and re-layouts  35.3 us
    pallas_call x2, Pallas kernels, block_stage(): pl.pallas_call(block_kernel, name='block_stage', grid=(count,), in_specs=...  24.7 us
    all_to_all x1, blocking collectives, per_device(): results.append(exchange(result))  23.6 us
    pallas_call x2, Pallas kernels, grid_stage(): pl.pallas_call(grid_kernel, name='grid_stage', grid=(count,), in_specs=[s...  21.6 us
    all_to_all x2, starting transfers between devices, per_device(): result = grid_stage(exchange(sent), perm, back, grid_params)  9.68 us
    all_to_all x1, starting transfers between devices, per_device(): results.append(exchange(result))  5.98 us
    dot_general x2, matrix products, turned_bias(): jnp.einsum('jir,rh->jhi', one_hot, pos_table * LOG2E, precision=lax.Preci...  5.24 us
  transfers between devices with their start and end apart: 6, of which 3 were waited for; matrix products, arithmetic and copies ran while one was open for 6% of the time, Pallas kernels for 17%

profile of v1, /device:TPU:0, one launch (start us, length us, event | category | flops | bytes accessed | tf_op | source)
XLA Modules:
  0.0 195.8 jit_solution(4825825127697252286)
XLA Ops:
  0.0 2.4 %copy.41 = bf16[48,32,512]{2,0,1:T(8,128)(2,1)S(1)} copy(bf16[48,32,512]{2,1,0:T(8,128)(2,1)} %param.19) | data formatting | bytes 3145728 | tf_op args[0]
  2.9 5.1 %collective-permute-start.1 = (bf16[1,48,512]{2,1,0:T(8,128)(2,1)S(1)}, bf16[1,48,512]{2,1,0:T(8,128)(2,1)S(1)}, u32[]{:S(2)}, u32[]{:S(2)}) collective-permute-start(bf16[1,48,512]{2,1,0:T(8,128)(2,1)S(1)} %get-tuple-element.16), channel_id=1, source_target_pairs={{1,0},{2,1},{3,2},{4,3},{5,4},{6,5},{7,6},{8,7},{9,8},{10,9},{11,1... | collective-permute-start | bytes 147464 | tf_op jit(solution)/shard_map/ppermute | solution.py:337
  10.8 44.7 %mbconv.1 = (bf16[32,48,2048]{2,1,0:T(8,128)(2,1)S(1)}, f32[8,128]{1,0:T(8,128)S(1)}) custom-call(bf16[34,48,512]{2,1,0:T(8,128)(2,1)S(1)} %pad_maximum_fusion.x_ref, bf16[512,2048]{1,0:T(8,128)(2,1)S(1)} %copy-done.8, f32[1,2048]{1,0:T(1,128)S(1)} %bitcast.37, f32[9,2048]{1,0:T(8,128)S(1)} %copy-done.18, f32[1,2048]{1,0:T(1,128)S(1)} %bitcast.38, ...), custom_call_target="tpu_custom_call" | custom-call | flops 13690208256 | bytes 20000000 | tf_op jit(solution)/shard_map/mbconv/pallas_call | solution.py:81
  55.5 2.7 %copy-done.31 = bf16[32,48,2048]{2,1,0:T(8,128)(2,1)} copy-done((bf16[32,48,2048]{2,1,0:T(8,128)(2,1)}, bf16[32,48,2048]{2,1,0:T(8,128)(2,1)S(1)}, u32[]{:S(2)}) %copy-start.31) | copy-done | bytes 6291480
  58.8 5.1 %all-to-all-start = ((f32[16,1,128]{2,1,0:T(1,128)}), f32[16,1,128]{2,1,0:T(1,128)S(1)}, u32[]{:S(2)}, u32[]{:S(2)}) async-start(f32[16,1,128]{2,1,0:T(1,128)} %broadcast_in_dim.5), calls=%async_computation | async-start | bytes 16384 | tf_op jit(solution)/shard_map/all_to_all | solution.py:342
  63.9 2.6 %fusion.4 = f32[64,16,64]{2,1,0:T(8,128)S(1)} fusion(s32[64,64]{1,0:T(8,128)S(1)} %add_add_fusion, f32[225,16]{0,1:T(8,128)S(1)} %copy-done.35), kind=kOutput, calls=%fused_computation.9 | convolution fusion | flops 177872400 | bytes 292928 | tf_op jit(solution)/shard_map/jir,rh->jhi/dot_general | solution.py:278
  68.0 2.2 %all-to-all-done = f32[16,1,128]{2,1,0:T(1,128)S(1)} async-done(((f32[16,1,128]{2,1,0:T(1,128)}), f32[16,1,128]{2,1,0:T(1,128)S(1)}, u32[]{:S(2)}, u32[]{:S(2)}) %all-to-all-start) | async-done | bytes 8224 | tf_op jit(solution)/shard_map/all_to_all | solution.py:342
  70.3 1.6 copy-done.9
  74.9 2.8 %copy-done.32 = bf16[32,48,2048]{2,1,0:T(8,128)(2,1)S(1)} copy-done((bf16[32,48,2048]{2,1,0:T(8,128)(2,1)S(1)}, bf16[32,48,2048]{2,1,0:T(8,128)(2,1)}, u32[]{:S(2)}) %copy-start.32) | copy-done | bytes 6291480
  77.7 12.3 %block_stage.2 = bf16[8,2,48,512]{3,2,1,0:T(8,128)(2,1)} custom-call(bf16[32,48,2048]{2,1,0:T(8,128)(2,1)S(1)} %copy-done.32, bf16[32,48,512]{2,1,0:T(8,128)(2,1)S(1)} %bitcast.31, f32[1,128]{1,0:T(1,128)S(1)} %multiply_bitcast_fusion.part_ref, bf16[128,2048]{1,0:T(8,128)(2,1)S(1)} %copy-done.12, bf16[2048,512]{1,0:T(8,128)(2,1)S(1)} %copy-done.9, ...), custom_call_target="tpu_custom_call" | custom-call | flops 12884901888 | bytes 8000000 | tf_op jit(solution)/shard_map/block_stage/pallas_call | solution.py:230
  90.1 3.7 %all-to-all-start.1 = ((bf16[8,2,48,512]{3,2,1,0:T(8,128)(2,1)}), bf16[8,2,48,512]{3,2,1,0:T(8,128)(2,1)S(1)}, u32[]{:S(2)}, u32[]{:S(2)}) async-start(bf16[8,2,48,512]{3,2,1,0:T(8,128)(2,1)} %block_stage.2), calls=%async_computation.1 | async-start | bytes 1572864 | tf_op jit(solution)/shard_map/all_to_all | solution.py:368
  95.8 1.6 copy-done.10
  100.4 2.8 %copy-done.33 = bf16[32,48,2048]{2,1,0:T(8,128)(2,1)S(1)} copy-done((bf16[32,48,2048]{2,1,0:T(8,128)(2,1)S(1)}, bf16[32,48,2048]{2,1,0:T(8,128)(2,1)}, u32[]{:S(2)}) %copy-start.33) | copy-done | bytes 6291480
  103.2 12.4 %block_stage.3 = bf16[8,2,48,512]{3,2,1,0:T(8,128)(2,1)} custom-call(bf16[32,48,2048]{2,1,0:T(8,128)(2,1)S(1)} %copy-done.33, bf16[32,48,512]{2,1,0:T(8,128)(2,1)S(1)} %bitcast.32, f32[1,128]{1,0:T(1,128)S(1)} %multiply_bitcast_fusion.part_ref, bf16[128,2048]{1,0:T(8,128)(2,1)S(1)} %copy-done.13, bf16[2048,512]{1,0:T(8,128)(2,1)S(1)} %copy-done.10, ...), custom_call_target="tpu_custom_call" | custom-call | flops 12884901888 | bytes 8000000 | tf_op jit(solution)/shard_map/block_stage/pallas_call | solution.py:230
  115.6 6.0 %all-to-all-start.3 = ((bf16[8,2,48,512]{3,2,1,0:T(8,128)(2,1)}), bf16[8,2,48,512]{3,2,1,0:T(8,128)(2,1)S(1)}, u32[]{:S(2)}, u32[]{:S(2)}) async-start(bf16[8,2,48,512]{3,2,1,0:T(8,128)(2,1)} %block_stage.3), calls=%async_computation.3 | async-start | bytes 1572864 | tf_op jit(solution)/shard_map/all_to_all | solution.py:368
  121.5 2.6 %fusion.5 = f32[64,16,64]{2,1,0:T(8,128)S(1)} fusion(s32[64,64]{1,0:T(8,128)S(1)} %add_add_fusion, f32[225,16]{0,1:T(8,128)S(1)} %copy-done.36), kind=kOutput, calls=%fused_computation.10 | convolution fusion | flops 177872400 | bytes 292928 | tf_op jit(solution)/shard_map/jir,rh->jhi/dot_general | solution.py:278
  124.4 2.4 %fusion.14 = (bf16[512,512]{1,0:T(8,128)(2,1)}, bf16[512,512]{1,0:T(8,128)(2,1)S(1)}, bf16[512,512]{1,0:T(8,128)(2,1)S(1)}) fusion(bf16[512,1536]{1,0:T(8,128)(2,1)} %param.32), kind=kLoop, calls=%fused_computation.27 | loop fusion | bytes 3145728 | tf_op jit(solution)/shard_map/slice | solution.py:288
  126.7 1.4 copy.37
  132.1 11.2 %grid_stage.2 = bf16[8,2,48,512]{3,2,1,0:T(8,128)(2,1)} custom-call(bf16[8,2,48,512]{3,2,1,0:T(8,128)(2,1)S(1)} %all-to-all-done.1.s_ref, bf16[384,384]{1,0:T(8,128)(2,1)S(1)} %copy-done.23, bf16[384,384]{1,0:T(8,128)(2,1)S(1)} %copy-done.25, f32[1,512]{1,0:T(1,128)S(1)} %bitcast.41, bf16[512,512]{1,0:T(8,128)(2,1)S(1)} %get-tuple-element.10.wq_ref, ...), custom_call_target="tpu_custom_call" | custom-call | flops 6442450944 | bytes 6000000 | tf_op jit(solution)/shard_map/grid_stage/pallas_call | solution.py:255
  143.3 6.0 %all-to-all-start.2 = ((bf16[8,2,48,512]{3,2,1,0:T(8,128)(2,1)}), bf16[8,2,48,512]{3,2,1,0:T(8,128)(2,1)}, u32[]{:S(2)}, u32[]{:S(2)}) async-start(bf16[8,2,48,512]{3,2,1,0:T(8,128)(2,1)} %grid_stage.2), calls=%async_computation.2 | async-start | bytes 1572864 | tf_op jit(solution)/shard_map/all_to_all | solution.py:369
  155.2 10.4 %grid_stage.3 = bf16[8,2,48,512]{3,2,1,0:T(8,128)(2,1)S(1)} custom-call(bf16[8,2,48,512]{3,2,1,0:T(8,128)(2,1)S(1)} %all-to-all-done.3.s_ref, bf16[384,384]{1,0:T(8,128)(2,1)S(1)} %copy-done.24, bf16[384,384]{1,0:T(8,128)(2,1)S(1)} %copy-done.26, f32[1,512]{1,0:T(1,128)S(1)} %bitcast.42, bf16[512,512]{1,0:T(8,128)(2,1)S(1)} %get-tuple-element.10.wq_ref, ...), custom_call_target="tpu_custom_call" | custom-call | flops 6442450944 | bytes 6000000 | tf_op jit(solution)/shard_map/grid_stage/pallas_call | solution.py:255
  165.6 3.2 %all-to-all-done.2 = bf16[8,2,48,512]{3,2,1,0:T(8,128)(2,1)} async-done(((bf16[8,2,48,512]{3,2,1,0:T(8,128)(2,1)}), bf16[8,2,48,512]{3,2,1,0:T(8,128)(2,1)}, u32[]{:S(2)}, u32[]{:S(2)}) %all-to-all-start.2) | async-done | bytes 786464 | tf_op jit(solution)/shard_map/all_to_all | solution.py:369
  168.9 23.6 %all_to_all.25 = bf16[8,2,48,512]{3,2,1,0:T(8,128)(2,1)S(1)} all-to-all(bf16[8,2,48,512]{3,2,1,0:T(8,128)(2,1)S(1)} %grid_stage.3), channel_id=1, replica_groups={{0,2,4,6,8,10,12,14},{1,3,5,7,9,11,13,15},{16,18,20,22,24,26,28,30},{17..., dimensions={0} | all-to-all | bytes 1572864 | tf_op jit(solution)/shard_map/all_to_all | solution.py:369
  193.8 2.0 %copy.40 = bf16[48,4,8,512]{3,2,1,0:T(8,128)(2,1)} copy(bf16[48,4,8,512]{3,0,1,2:T(8,128)(2,1)S(1)} %maximum_bitcast_fusion) | data formatting | bytes 3145728 | tf_op jit(solution)/shard_map/transpose | solution.py:371
  (87 shorter events, 24.8 us)
Async XLA Ops:
  0.0 8.0 %copy-start.34 = (bf16[512,1536]{1,0:T(8,128)(2,1)S(1)}, bf16[512,1536]{1,0:T(8,128)(2,1)}, u32[]{:S(2)}) copy-start(bf16[512,1536]{1,0:T(8,128)(2,1)} %param.28) | copy-start | bytes 4718596
  2.4 7.4 %collective-permute-start = (bf16[1,48,512]{2,1,0:T(8,128)(2,1)S(1)}, bf16[1,48,512]{2,1,0:T(8,128)(2,1)S(1)}, u32[]{:S(2)}, u32[]{:S(2)}) collective-permute-start(bf16[1,48,512]{2,1,0:T(8,128)(2,1)S(1)} %get-tuple-element.15), channel_id=1, source_target_pairs={{0,1},{1,2},{2,3},{3,4},{4,5},{5,6},{6,7},{7,8},{8,9},{9,10},{10,1... | collective-permute-start | bytes 147464 | tf_op jit(solution)/shard_map/ppermute | solution.py:336
  2.9 6.9 %collective-permute-start.1 = (bf16[1,48,512]{2,1,0:T(8,128)(2,1)S(1)}, bf16[1,48,512]{2,1,0:T(8,128)(2,1)S(1)}, u32[]{:S(2)}, u32[]{:S(2)}) collective-permute-start(bf16[1,48,512]{2,1,0:T(8,128)(2,1)S(1)} %get-tuple-element.16), channel_id=1, source_target_pairs={{1,0},{2,1},{3,2},{4,3},{5,4},{6,5},{7,6},{8,7},{9,8},{10,9},{11,1... | collective-permute-start | bytes 147464 | tf_op jit(solution)/shard_map/ppermute | solution.py:337
  8.9 61.4 %copy-start = (bf16[512,512]{1,0:T(8,128)(2,1)}, bf16[512,512]{1,0:T(8,128)(2,1)S(1)}, u32[]{:S(2)}) copy-start(bf16[512,512]{1,0:T(8,128)(2,1)S(1)} %get-tuple-element.14.wk_ref) | copy-start | bytes 1572868
  9.0 1.7 copy-start.8
  9.0 1.8 copy-start.11
  9.0 1.8 copy-start.18
  9.0 1.8 copy-start.19
  9.0 1.8 copy-start.20
  10.8 53.0 %copy-start.35 = (f32[225,16]{0,1:T(8,128)S(1)}, f32[225,16]{0,1:T(8,128)}, u32[]{:S(2)}) copy-start(f32[225,16]{0,1:T(8,128)} %param.30) | copy-start | bytes 43204
  55.5 2.7 %copy-start.31 = (bf16[32,48,2048]{2,1,0:T(8,128)(2,1)}, bf16[32,48,2048]{2,1,0:T(8,128)(2,1)S(1)}, u32[]{:S(2)}) copy-start(bf16[32,48,2048]{2,1,0:T(8,128)(2,1)S(1)} %get-tuple-element.7.act_ref) | copy-start | bytes 18874372
  58.2 12.1 %copy-start.21 = (f32[512]{0:T(512)S(1)}, f32[512]{0:T(512)}, u32[]{:S(2)}) copy-start(f32[512]{0:T(512)} %param.27) | copy-start | bytes 6148
  58.8 11.5 %all-to-all-start = ((f32[16,1,128]{2,1,0:T(1,128)}), f32[16,1,128]{2,1,0:T(1,128)S(1)}, u32[]{:S(2)}, u32[]{:S(2)}) async-start(f32[16,1,128]{2,1,0:T(1,128)} %broadcast_in_dim.5), calls=%async_computation | async-start | bytes 16384 | tf_op jit(solution)/shard_map/all_to_all | solution.py:342
  66.7 23.4 %copy-start.4 = (f32[64,1024]{1,0:T(8,128)}, f32[64,1024]{1,0:T(8,128)S(1)}, u32[]{:S(2)}) copy-start(f32[64,1024]{1,0:T(8,128)S(1)} %reshape.140.bias_ref) | copy-start | bytes 786436
  70.3 1.6 copy-start.9
  74.9 2.8 %copy-start.32 = (bf16[32,48,2048]{2,1,0:T(8,128)(2,1)S(1)}, bf16[32,48,2048]{2,1,0:T(8,128)(2,1)}, u32[]{:S(2)}) copy-start(bf16[32,48,2048]{2,1,0:T(8,128)(2,1)} %copy-done.31) | copy-start | bytes 18874372
  90.1 25.5 %all-to-all-start.1 = ((bf16[8,2,48,512]{3,2,1,0:T(8,128)(2,1)}), bf16[8,2,48,512]{3,2,1,0:T(8,128)(2,1)S(1)}, u32[]{:S(2)}, u32[]{:S(2)}) async-start(bf16[8,2,48,512]{3,2,1,0:T(8,128)(2,1)} %block_stage.2), calls=%async_computation.1 | async-start | bytes 1572864 | tf_op jit(solution)/shard_map/all_to_all | solution.py:368
  100.4 2.8 %copy-start.33 = (bf16[32,48,2048]{2,1,0:T(8,128)(2,1)S(1)}, bf16[32,48,2048]{2,1,0:T(8,128)(2,1)}, u32[]{:S(2)}) copy-start(bf16[32,48,2048]{2,1,0:T(8,128)(2,1)} %copy-done.31) | copy-start | bytes 18874372
  103.2 18.3 %copy-start.36 = (f32[225,16]{0,1:T(8,128)S(1)}, f32[225,16]{0,1:T(8,128)}, u32[]{:S(2)}) copy-start(f32[225,16]{0,1:T(8,128)} %param.34) | copy-start | bytes 43204
  115.6 27.7 %all-to-all-start.3 = ((bf16[8,2,48,512]{3,2,1,0:T(8,128)(2,1)}), bf16[8,2,48,512]{3,2,1,0:T(8,128)(2,1)S(1)}, u32[]{:S(2)}, u32[]{:S(2)}) async-start(bf16[8,2,48,512]{3,2,1,0:T(8,128)(2,1)} %block_stage.3), calls=%async_computation.3 | async-start | bytes 1572864 | tf_op jit(solution)/shard_map/all_to_all | solution.py:368
  124.3 3.8 %copy-start.6 = (f32[64,1024]{1,0:T(8,128)}, f32[64,1024]{1,0:T(8,128)S(1)}, u32[]{:S(2)}) copy-start(f32[64,1024]{1,0:T(8,128)S(1)} %reshape.142.bias_ref) | copy-start | bytes 786436
  124.4 3.8 %copy-start.22 = (f32[512]{0:T(512)S(1)}, f32[512]{0:T(512)}, u32[]{:S(2)}) copy-start(f32[512]{0:T(512)} %param.31) | copy-start | bytes 6148
  126.7 16.6 %copy-start.2 = (bf16[512,512]{1,0:T(8,128)(2,1)}, bf16[512,512]{1,0:T(8,128)(2,1)S(1)}, u32[]{:S(2)}) copy-start(bf16[512,512]{1,0:T(8,128)(2,1)S(1)} %get-tuple-element.11.wk_ref) | copy-start | bytes 1572868
  143.3 25.6 %all-to-all-start.2 = ((bf16[8,2,48,512]{3,2,1,0:T(8,128)(2,1)}), bf16[8,2,48,512]{3,2,1,0:T(8,128)(2,1)}, u32[]{:S(2)}, u32[]{:S(2)}) async-start(bf16[8,2,48,512]{3,2,1,0:T(8,128)(2,1)} %grid_stage.2), calls=%async_computation.2 | async-start | bytes 1572864 | tf_op jit(solution)/shard_map/all_to_all | solution.py:369
  (19 other events, 19.5 us)

commit v2 on v1

--- a/solution.py
+++ b/solution.py
@@ -12,52 +12,65 @@
 HEAD_DIM = 32
 WIN = 8
 CELLS = WIN * WIN
-CHUNKS = (2, 2)
-LANES = 256
+CHUNKS = (1, 3)
+LANES = 512
+SUB = 256
+VMEM_BYTES = 60 << 20
+ROOT_HALF = 0.7071067811865476
 LOG2E = 1.4426950408889634
 SCORE_SCALE = HEAD_DIM ** (-0.5) * LOG2E
 BF16 = jnp.bfloat16
 F32 = jnp.float32
 
 
-def gelu(value):
-    return 0.5 * value * (1.0 + lax.erf(value * 0.7071067811865476))
-
-
-def mbconv_kernel(x_ref, w_ref, b_ref, dw_ref, db_ref, down_ref, act_ref, part_ref, hid_ref):
+def double_gelu(half):
+    return half + half * lax.erf(half)
+
+
+def mbconv_kernel(
+    x_ref, w_ref, b_ref, dw_ref, db_ref, down_ref, shift_ref, act_ref, part_ref,
+    total_ref, tap_ref, *hidden_refs,
+):
     cols, rows, channels = x_ref.shape
     lanes = w_ref.shape[1]
-    step = 2
-    bias = b_ref[...]
-
-    def expand(i, carry):
-        cells = x_ref[pl.ds(i * step, step)].reshape(step * rows, channels)
-        hidden = jnp.dot(cells, w_ref[...], preferred_element_type=F32) + bias
-        hid_ref[pl.ds(i * step, step)] = gelu(hidden).reshape(step, rows, lanes)
-        return carry
-
-    lax.fori_loop(0, cols // step, expand, 0)
-    row = lax.broadcasted_iota(jnp.int32, (rows, lanes), 0)
-    first = row == 0
-    last = row == rows - 1
-    taps = dw_ref[...]
-    shift = db_ref[...]
-
-    def depth(c, total):
+    sub = hidden_refs[0].shape[2]
+    out_cols = cols - 2
+    pieces = 2 if cols % 2 == 0 else 1
+    piece = cols // pieces
+    shift = shift_ref[...]
+    for k in range(9):
+        tap_ref[k] = jnp.broadcast_to(dw_ref[k : k + 1] * 0.5, (16, lanes)).astype(BF16)
+
+    def expand(s, i):
+        span = slice(s * sub, (s + 1) * sub)
+        cells = x_ref[i * piece : (i + 1) * piece].reshape(piece * rows, channels)
+        hidden = jnp.dot(cells, w_ref[:, span], preferred_element_type=F32)
+        hidden = double_gelu(hidden * ROOT_HALF + b_ref[:, span] * ROOT_HALF)
+        hidden_refs[s][i * piece : (i + 1) * piece] = hidden.astype(BF16).reshape(piece, rows, sub)
+
+    def depth(s, c, total):
+        span = slice(s * sub, (s + 1) * sub)
+        near = [hidden_refs[s][c + k].reshape(rows // 16, 16, sub) for k in range(3)]
         sums = []
         for r in range(3):
-            acc = hid_ref[c] * taps[3 * r : 3 * r + 1]
-            acc = acc + hid_ref[c + 1] * taps[3 * r + 1 : 3 * r + 2]
-            acc = acc + hid_ref[c + 2] * taps[3 * r + 2 : 3 * r + 3]
-            sums.append(acc)
-        above = jnp.where(first, 0.0, pltpu.roll(sums[0], 1, 0))
-        below = jnp.where(last, 0.0, pltpu.roll(sums[2], rows - 1, 0))
-        active = gelu(sums[1] + above + (below + shift))
-        act_ref[c] = active.astype(BF16)
-        return total + active.reshape(rows // 8, 8, lanes).sum(0)
-
-    total = lax.fori_loop(0, cols - 2, depth, jnp.zeros((8, lanes), F32))
-    pooled = jnp.sum(total, axis=0, keepdims=True)
+            terms = [near[k] * tap_ref[3 * r + k, :, span][None] for k in range(3)]
+            sums.append((terms[0] + terms[1] + terms[2]).reshape(rows, sub))
+        summed = jnp.dot(shift, jnp.concatenate(sums, axis=0), preferred_element_type=F32)
+        active = double_gelu(summed + db_ref[:, span] * ROOT_HALF)
+        act_ref[c, :, span] = active.astype(BF16)
+        return total + active.reshape(rows // 8, 8, sub).sum(0)
+
+    for i in range(pieces):
+        expand(0, i)
+    for s in range(len(hidden_refs)):
+        total = jnp.zeros((8, sub), F32)
+        for i in range(pieces):
+            if s + 1 < len(hidden_refs):
+                expand(s + 1, i)
+            for c in range(i * out_cols // pieces, (i + 1) * out_cols // pieces):
+                total = depth(s, c, total)
+        total_ref[:, s * sub : (s + 1) * sub] = total
+    pooled = jnp.sum(total_ref[...], axis=0, keepdims=True)
     part = jnp.dot(
         jnp.broadcast_to(pooled, (8, lanes)),
         down_ref[...].astype(F32),
@@ -72,6 +85,15 @@
     @pl.when(pl.program_id(0) > 0)
     def _():
         part_ref[...] += part
+
+
+def row_shifts(rows):
+    shift = np.zeros((rows, 3 * rows), np.float32)
+    for offset in range(3):
+        for row in range(rows):
+            if 0 <= row + offset - 1 < rows:
+                shift[row, offset * rows + row + offset - 1] = 1.0
+    return jnp.asarray(shift, BF16)
 
 
 def mbconv(rimmed, expand_weight, expand_bias, depth_weight, depth_bias, squeeze_down):
@@ -89,6 +111,7 @@
             pl.BlockSpec((9, LANES), lambda i: (0, i)),
             pl.BlockSpec((1, LANES), lambda i: (0, i)),
             pl.BlockSpec((LANES, squeeze), lambda i: (i, 0)),
+            pl.BlockSpec((rows, 3 * rows), lambda i: (0, 0)),
         ],
         out_specs=[
             pl.BlockSpec((cols - 2, rows, LANES), lambda i: (0, 0, i)),
@@ -98,13 +121,14 @@
             jax.ShapeDtypeStruct((cols - 2, rows, expanded), BF16),
             jax.ShapeDtypeStruct((8, squeeze), F32),
         ],
-        scratch_shapes=[pltpu.VMEM((cols, rows, LANES), F32)],
+        scratch_shapes=[pltpu.VMEM((8, LANES), F32), pltpu.VMEM((9, 16, LANES), BF16)]
+        + [pltpu.VMEM((cols, rows, SUB), BF16)] * (LANES // SUB),
         cost_estimate=pl.CostEstimate(
             flops=2 * cols * rows * channels * expanded * 4,
             bytes_accessed=20_000_000,
             transcendentals=0,
         ),
-        compiler_params=pltpu.CompilerParams(vmem_limit_bytes=32 << 20),
+        compiler_params=pltpu.CompilerParams(vmem_limit_bytes=VMEM_BYTES),
     )(
         rimmed,
         expand_weight,
@@ -112,57 +136,81 @@
         depth_weight,
         depth_bias.reshape(1, -1),
         squeeze_down,
-    )
-
-
-def attend(stream, gain_ref, wq_ref, wk_ref, wv_ref, wo_ref, bias_ref, mask_ref, scratch):
-    q_ref, k_ref, vt_ref, o_ref = scratch
+        row_shifts(rows),
+    )
+
+
+def prepare(in_ref, wv_ref, mask_ref):
+    channels = in_ref.shape[0]
+    wv_ref[...] = in_ref[:, 2 * channels :].T
+    head = lax.broadcasted_iota(jnp.int32, mask_ref.shape, 0) // CELLS
+    lane = lax.broadcasted_iota(jnp.int32, mask_ref.shape, 1) // HEAD_DIM
+    mask_ref[...] = (head == lane).astype(F32).astype(BF16)
+
+
+def attend(stream, gain_ref, in_ref, out_weight_ref, bias_ref, scratch):
+    wv_ref, mask_ref, q_ref, k_ref, vt_ref, o_ref = scratch
     cells, channels = stream.shape
     average = jnp.mean(stream, axis=-1, keepdims=True)
     centred = stream - average
     variance = jnp.mean(centred * centred, axis=-1, keepdims=True)
     normed = (centred * lax.rsqrt(variance + 1e-05) * gain_ref[...]).astype(BF16)
-    q_ref[...] = jnp.dot(normed, wq_ref[...], preferred_element_type=F32).astype(BF16)
-    k_ref[...] = jnp.dot(normed, wk_ref[...], preferred_element_type=F32).astype(BF16)
+    q_ref[...] = jnp.dot(normed, in_ref[:, :channels], preferred_element_type=F32).astype(BF16)
+    k_ref[...] = jnp.dot(
+        normed, in_ref[:, channels : 2 * channels], preferred_element_type=F32
+    ).astype(BF16)
     vt_ref[...] = lax.dot_general(
         wv_ref[...], normed, (((1,), (1,)), ((), ())), preferred_element_type=F32
     ).astype(BF16)
-    mask = mask_ref[...]
     group = 256 // HEAD_DIM
     even = (lax.broadcasted_iota(jnp.int32, (CELLS, 128), 1) // HEAD_DIM) % 2 == 0
-    for w in range(cells // CELLS):
-        span = slice(w * CELLS, (w + 1) * CELLS)
+    zero = jnp.zeros((CELLS, 128), BF16)
+    for duo in range(cells // 128):
+        both = slice(duo * 128, (duo + 1) * 128)
         for g in range(HEADS // group):
             part = slice(g * 256, (g + 1) * 256)
-            query = jnp.concatenate([q_ref[span, part]] * group, axis=0) * mask
             lanes = slice(g * group * CELLS, (g + 1) * group * CELLS)
-            scores = lax.dot_general(
-                k_ref[span, part], query, (((1,), (1,)), ((), ())), preferred_element_type=F32
-            )
-            scores = scores * SCORE_SCALE + bias_ref[:, lanes]
-            scores = jnp.exp2(scores - jnp.max(scores, axis=0, keepdims=True))
-            weight = 1.0 / jnp.sum(scores, axis=0, keepdims=True)
-            prob = (scores * weight).astype(BF16)
+            probs = []
+            for w in (2 * duo, 2 * duo + 1):
+                span = slice(w * CELLS, (w + 1) * CELLS)
+                query = jnp.concatenate([q_ref[span, part]] * group, axis=0) * mask_ref[...]
+                scores = lax.dot_general(
+                    k_ref[span, part], query, (((1,), (1,)), ((), ())), preferred_element_type=F32
+                )
+                scores = scores * SCORE_SCALE + bias_ref[:, lanes]
+                scores = jnp.exp2(scores - jnp.max(scores, axis=0, keepdims=True))
+                weight = 1.0 / jnp.sum(scores, axis=0, keepdims=True)
+                probs.append((scores * weight).astype(BF16))
             for quad in range(group // 4):
-                halves = []
+                outs = []
                 for pair in (2 * quad, 2 * quad + 1):
-                    values = vt_ref[g * 256 + pair * 64 : g * 256 + pair * 64 + 64, span]
-                    halves.append(
+                    c = slice(pair * 128, (pair + 1) * 128)
+                    right = jnp.concatenate(
+                        [
+                            jnp.concatenate([probs[0][:, c], zero], axis=1),
+                            jnp.concatenate([zero, probs[1][:, c]], axis=1),
+                        ],
+                        axis=0,
+                    )
+                    first = g * 256 + pair * 64
+                    outs.append(
                         jnp.dot(
-                            values,
-                            prob[:, pair * 128 : pair * 128 + 128],
-                            preferred_element_type=F32,
+                            vt_ref[first : first + 64, both], right, preferred_element_type=F32
                         )
                     )
-                turned = jnp.concatenate(halves, axis=0).T
-                picked = jnp.where(even, turned[:CELLS], turned[CELLS:])
-                o_ref[span, g * 256 + quad * 128 : g * 256 + quad * 128 + 128] = picked.astype(BF16)
-    return stream + jnp.dot(o_ref[...], wo_ref[...], preferred_element_type=F32)
+                first = g * 256 + quad * 128
+                for k in range(2):
+                    turned = jnp.concatenate([o[:, k * 128 : (k + 1) * 128] for o in outs], axis=0)
+                    turned = turned.T
+                    picked = jnp.where(even, turned[:CELLS], turned[CELLS:])
+                    row = (2 * duo + k) * CELLS
+                    o_ref[row : row + CELLS, first : first + 128] = picked.astype(BF16)
+    return stream + jnp.dot(o_ref[...], out_weight_ref[...], preferred_element_type=F32)
 
 
 def block_kernel(
-    act_ref, x_ref, part_ref, up_ref, proj_ref, gain_ref, wq_ref, wk_ref, wv_ref, wo_ref,
-    bias_ref, mask_ref, out_ref, gate_ref, *scratch,
+    act_ref, x_ref, part_ref, up_ref, proj_ref, gain_ref, in_ref, out_weight_ref, bias_ref,
+    out_ref, gate_ref, *scratch,
 ):
     cols, rows, expanded = act_ref.shape
     channels = x_ref.shape[2]
@@ -177,7 +225,8 @@
             precision=lax.Precision.HIGHEST,
             preferred_element_type=F32,
         )
-        gate_ref[...] = jax.nn.sigmoid(gate)
+        gate_ref[...] = jax.nn.sigmoid(gate) * ROOT_HALF
+        prepare(in_ref, scratch[0], scratch[1])
 
     gated = act_ref[...].reshape(cols * rows, expanded).astype(F32) * gate_ref[0:1]
     first = jnp.dot(gated.astype(BF16), proj_ref[...], preferred_element_type=F32)
@@ -189,22 +238,25 @@
         axis=0,
     )
     second = attend(
-        stream, gain_ref, wq_ref, wk_ref, wv_ref, wo_ref, bias_ref, mask_ref, scratch
+        stream, gain_ref, in_ref, out_weight_ref, bias_ref, scratch
     ).reshape(windows, cols, WIN, channels)
     second = jnp.concatenate([second[a] for a in range(windows)], axis=1)
     out_ref[...] = second.reshape(out_ref.shape).astype(BF16)
 
 
 def grid_kernel(
-    s_ref, perm_ref, back_ref, gain_ref, wq_ref, wk_ref, wv_ref, wo_ref,
-    bias_ref, mask_ref, out_ref, *scratch,
+    s_ref, perm_ref, back_ref, gain_ref, in_ref, out_weight_ref, bias_ref, out_ref, *scratch,
 ):
+    @pl.when(pl.program_id(0) == 0)
+    def _():
+        prepare(in_ref, scratch[0], scratch[1])
+
     cells = perm_ref.shape[0]
     channels = s_ref.shape[-1]
     incoming = s_ref[...].reshape(cells, channels)
     stream = jnp.dot(perm_ref[...], incoming, preferred_element_type=F32)
     result = attend(
-        stream, gain_ref, wq_ref, wk_ref, wv_ref, wo_ref, bias_ref, mask_ref, scratch
+        stream, gain_ref, in_ref, out_weight_ref, bias_ref, scratch
     ).astype(BF16)
     result = jnp.dot(back_ref[...], result, preferred_element_type=F32)
     out_ref[...] = result.astype(BF16).reshape(out_ref.shape)
@@ -216,6 +268,8 @@
 
 def attention_scratch(cells, channels):
     return [
+        pltpu.VMEM((channels, channels), BF16),
+        pltpu.VMEM((256 // HEAD_DIM * CELLS, 256), BF16),
         pltpu.VMEM((cells, channels), BF16),
         pltpu.VMEM((cells, channels), BF16),
         pltpu.VMEM((channels, cells), BF16),
@@ -244,7 +298,7 @@
             bytes_accessed=8_000_000,
             transcendentals=0,
         ),
-        compiler_params=pltpu.CompilerParams(vmem_limit_bytes=32 << 20),
+        compiler_params=pltpu.CompilerParams(vmem_limit_bytes=VMEM_BYTES),
     )(active, field, part, up, proj, *params)
 
 
@@ -265,7 +319,7 @@
             bytes_accessed=6_000_000,
             transcendentals=0,
         ),
-        compiler_params=pltpu.CompilerParams(vmem_limit_bytes=32 << 20),
+        compiler_params=pltpu.CompilerParams(vmem_limit_bytes=VMEM_BYTES),
     )(received, perm, back, *params)
 
 
@@ -279,24 +333,8 @@
     return bias.reshape(CELLS, HEADS * CELLS)
 
 
-def attention_params(gain, in_weight, out_weight, pos_table, mask):
-    channels = gain.shape[0]
-    return (
-        gain.reshape(1, -1),
-        in_weight[:, :channels],
-        in_weight[:, channels : 2 * channels],
-        in_weight[:, 2 * channels :].T,
-        out_weight,
-        turned_bias(pos_table),
-        mask,
-    )
-
-
-def head_mask():
-    group = 256 // HEAD_DIM
-    head = np.arange(group * CELLS) // CELLS
-    lane = np.arange(256) // HEAD_DIM
-    return jnp.asarray(head[:, None] == lane[None, :], BF16)
+def attention_params(gain, in_weight, out_weight, pos_table):
+    return gain.reshape(1, -1), in_weight, out_weight, turned_bias(pos_table)
 
 
 def grid_order(rows):
@@ -342,13 +380,10 @@
     parts = lax.all_to_all(
         jnp.broadcast_to(part[None, :1], (count, 1, part.shape[1])), "lon", 0, 0, tiled=True
     )
-    part = jnp.sum(parts, axis=0) / (rows * cols * count)
-    mask = head_mask()
+    part = jnp.sum(parts, axis=0) * (ROOT_HALF / (rows * cols * count))
     perm, back = grid_order(rows)
-    block_params = attention_params(
-        block_gain, block_in_weight, block_out_weight, block_table, mask
-    )
-    grid_params = attention_params(grid_gain, grid_in_weight, grid_out_weight, grid_table, mask)
+    block_params = attention_params(block_gain, block_in_weight, block_out_weight, block_table)
+    grid_params = attention_params(grid_gain, grid_in_weight, grid_out_weight, grid_table)
     exchange = functools.partial(
         lax.all_to_all,
         axis_name="lon",

time: 197 us -> 160 us (0.81)
  local copies, waits for them, and re-layouts: 41.6 us -> 7.4 us
  Pallas kernels: 91 us -> 62.7 us
  waiting for transfers between devices: 6.2 us -> 22.7 us
  blocking collectives: 23.6 us -> 34.4 us
    unnamed x77 -> x11, local copies, waits for them, and re-layouts: 35.3 us -> 2.3 us
    pallas_call x1, Pallas kernels: 44.7 us -> 14.5 us  [mbconv(): pl.pallas_call(mbconv_kernel, name='mbconv', grid=(expanded // LANES,), i...]
    all_to_all x2, waiting for transfers between devices: 0.01 us -> 18.1 us  [per_device(): result = grid_stage(exchange(sent), perm, back, grid_params)]
    all_to_all x1, blocking collectives: 23.6 us -> 34.4 us  [per_device(): results.append(exchange(result))]
    slice x2 -> x0, local copies, waits for them, and re-layouts: 3.29 us -> none  [attention_params(): in_weight[:, 2 * channels:]]
    all_to_all x1, waiting for transfers between devices: 3.24 us -> 0.01 us  [per_device(): results.append(exchange(result))]
    all_to_all x1, starting transfers between devices: 5.98 us -> 3.67 us  [per_device(): results.append(exchange(result))]
  transfers between devices with their start and end apart: 6 -> 6, of which waited for: 3 -> 3; matrix products, arithmetic and copies ran while one was open for 6% -> 4% of each run, Pallas kernels for 17% -> 25%
where the time goes in v2:
time: 160 us; the launch traced here: 159 us
  Pallas kernels  62.7 us (39%)
  blocking collectives  34.4 us (22%)
  starting transfers between devices  24.4 us (15%)
  waiting for transfers between devices  22.7 us (14%)
  local copies, waits for them, and re-layouts  7.4 us (5%)
  matrix products  5.24 us (3%)
  other arithmetic  2.14 us (1%)
    all_to_all x1, blocking collectives, per_device(): results.append(exchange(result))  34.4 us
    pallas_call x2, Pallas kernels, block_stage(): pl.pallas_call(block_kernel, name='block_stage', grid=(count,), in_specs=...  26.4 us
    pallas_call x2, Pallas kernels, grid_stage(): pl.pallas_call(grid_kernel, name='grid_stage', grid=(count,), in_specs=[s...  21.9 us
    all_to_all x2, waiting for transfers between devices, per_device(): result = grid_stage(exchange(sent), perm, back, grid_params)  18.1 us
    pallas_call x1, Pallas kernels, mbconv(): pl.pallas_call(mbconv_kernel, name='mbconv', grid=(expanded // LANES,), i...  14.5 us
    all_to_all x2, starting transfers between devices, per_device(): result = grid_stage(exchange(sent), perm, back, grid_params)  9.38 us
    all_to_all x1, starting transfers between devices, per_device(): lax.all_to_all(jnp.broadcast_to(part[None, :1], (count, 1, part.shape[1])...  5.8 us
    dot_general x2, matrix products, turned_bias(): jnp.einsum('jir,rh->jhi', one_hot, pos_table * LOG2E, precision=lax.Preci...  5.24 us
  transfers between devices with their start and end apart: 6, of which 3 were waited for; matrix products, arithmetic and copies ran while one was open for 4% of the time, Pallas kernels for 25%

profile of v2, /device:TPU:0, one launch (start us, length us, event | category | flops | bytes accessed | tf_op | source)
XLA Modules:
  0.0 159.1 jit_solution(11232469058609345701)
XLA Ops:
  0.0 2.3 %copy.31 = bf16[48,32,512]{2,0,1:T(8,128)(2,1)S(1)} copy(bf16[48,32,512]{2,1,0:T(8,128)(2,1)} %param.19) | data formatting | bytes 3145728 | tf_op args[0]
  2.3 0.5 collective-permute-start
  2.8 5.1 %collective-permute-start.1 = (bf16[1,48,512]{2,1,0:T(8,128)(2,1)S(1)}, bf16[1,48,512]{2,1,0:T(8,128)(2,1)S(1)}, u32[]{:S(2)}, u32[]{:S(2)}) collective-permute-start(bf16[1,48,512]{2,1,0:T(8,128)(2,1)S(1)} %get-tuple-element.10), channel_id=1, source_target_pairs={{1,0},{2,1},{3,2},{4,3},{5,4},{6,5},{7,6},{8,7},{9,8},{10,9},{11,1... | collective-permute-start | bytes 147464 | tf_op jit(solution)/shard_map/ppermute | solution.py:375
  8.0 1.7 %collective-permute-done = bf16[1,48,512]{2,1,0:T(8,128)(2,1)S(1)} collective-permute-done((bf16[1,48,512]{2,1,0:T(8,128)(2,1)S(1)}, bf16[1,48,512]{2,1,0:T(8,128)(2,1)S(1)}, u32[]{:S(2)}, u32[]{:S(2)}) %collective-permute-start) | collective-permute-done | bytes 49184 | tf_op jit(solution)/shard_map/ppermute | solution.py:374
  9.7 1.4 pad_maximum_fusion.x_ref
  11.1 14.5 %mbconv.1 = (bf16[32,48,2048]{2,1,0:T(8,128)(2,1)}, f32[8,128]{1,0:T(8,128)}) custom-call(bf16[34,48,512]{2,1,0:T(8,128)(2,1)} %pad_maximum_fusion.x_ref, bf16[512,2048]{1,0:T(8,128)(2,1)} %w_ref.1, f32[1,2048]{1,0:T(1,128)} %bitcast.32, f32[9,2048]{1,0:T(8,128)} %dw_ref.1, f32[1,2048]{1,0:T(1,128)} %bitcast.33, bf16[2048,128]{1,0:T(8,128)(2,1)} %down_ref.1, ...), custom_call_target="tpu_custom_call" | custom-call | flops 13690208256 | bytes 20000000 | tf_op jit(solution)/shard_map/mbconv/pallas_call | solution.py:103
  25.6 0.7 slice_bitcast_fusion
  26.2 0.6 broadcast_in_dim.5
  26.8 5.8 %all-to-all-start = ((f32[16,1,128]{2,1,0:T(1,128)}), f32[16,1,128]{2,1,0:T(1,128)S(1)}, u32[]{:S(2)}, u32[]{:S(2)}) async-start(f32[16,1,128]{2,1,0:T(1,128)} %broadcast_in_dim.5), calls=%async_computation | async-start | bytes 16384 | tf_op jit(solution)/shard_map/all_to_all | solution.py:380
  32.7 2.6 %fusion.4 = f32[64,16,64]{2,1,0:T(8,128)S(1)} fusion(s32[64,64]{1,0:T(8,128)S(1)} %add_add_fusion, f32[225,16]{0,1:T(8,128)S(1)} %copy-done.3), kind=kOutput, calls=%fused_computation.9 | convolution fusion | flops 177872400 | bytes 292928 | tf_op jit(solution)/shard_map/jir,rh->jhi/dot_general | solution.py:332
  35.3 0.9 reshape.140.bias_ref
  36.2 2.9 %all-to-all-done = f32[16,1,128]{2,1,0:T(1,128)S(1)} async-done(((f32[16,1,128]{2,1,0:T(1,128)}), f32[16,1,128]{2,1,0:T(1,128)S(1)}, u32[]{:S(2)}, u32[]{:S(2)}) %all-to-all-start) | async-done | bytes 8224 | tf_op jit(solution)/shard_map/all_to_all | solution.py:380
  39.6 8.6 %block_stage.2 = bf16[8,1,48,512]{3,2,1,0:T(8,128)(2,1)} custom-call(bf16[32,48,2048]{2,1,0:T(8,128)(2,1)} %get-tuple-element.7.act_ref, bf16[32,48,512]{2,1,0:T(8,128)(2,1)} %bitcast.29, f32[1,128]{1,0:T(1,128)} %multiply_bitcast_fusion.part_ref, bf16[128,2048]{1,0:T(8,128)(2,1)} %up_ref.3, bf16[2048,512]{1,0:T(8,128)(2,1)} %proj_ref.3, f32[1,512]{1,0:T(1,128)} %bitcast.34, ...), custom_call_target="tpu_custom_call" | custom-call | flops 6442450944 | bytes 8000000 | tf_op jit(solution)/shard_map/block_stage/pallas_call | solution.py:284
  48.1 3.6 %all-to-all-start.1 = ((bf16[8,1,48,512]{3,2,1,0:T(8,128)(2,1)}), bf16[8,1,48,512]{3,2,1,0:T(8,128)(2,1)S(1)}, u32[]{:S(2)}, u32[]{:S(2)}) async-start(bf16[8,1,48,512]{3,2,1,0:T(8,128)(2,1)} %block_stage.2), calls=%async_computation.1 | async-start | bytes 786432 | tf_op jit(solution)/shard_map/all_to_all | solution.py:403
  51.8 17.8 %block_stage.3 = bf16[8,3,48,512]{3,2,1,0:T(8,128)(2,1)} custom-call(bf16[32,48,2048]{2,1,0:T(8,128)(2,1)} %get-tuple-element.7.act_ref, bf16[32,48,512]{2,1,0:T(8,128)(2,1)} %bitcast.30, f32[1,128]{1,0:T(1,128)} %multiply_bitcast_fusion.part_ref, bf16[128,2048]{1,0:T(8,128)(2,1)} %up_ref.3, bf16[2048,512]{1,0:T(8,128)(2,1)} %proj_ref.3, f32[1,512]{1,0:T(1,128)} %bitcast.35, ...), custom_call_target="tpu_custom_call" | custom-call | flops 19327352832 | bytes 8000000 | tf_op jit(solution)/shard_map/block_stage/pallas_call | solution.py:284
  69.6 5.7 %all-to-all-start.3 = ((bf16[8,3,48,512]{3,2,1,0:T(8,128)(2,1)}), bf16[8,3,48,512]{3,2,1,0:T(8,128)(2,1)S(1)}, u32[]{:S(2)}, u32[]{:S(2)}) async-start(bf16[8,3,48,512]{3,2,1,0:T(8,128)(2,1)} %block_stage.3), calls=%async_computation.3 | async-start | bytes 2359296 | tf_op jit(solution)/shard_map/all_to_all | solution.py:403
  75.4 2.6 %fusion.5 = f32[64,16,64]{2,1,0:T(8,128)S(1)} fusion(s32[64,64]{1,0:T(8,128)S(1)} %add_add_fusion, f32[225,16]{0,1:T(8,128)S(1)} %copy-done.4), kind=kOutput, calls=%fused_computation.10 | convolution fusion | flops 177872400 | bytes 292928 | tf_op jit(solution)/shard_map/jir,rh->jhi/dot_general | solution.py:332
  78.0 0.9 reshape.142.bias_ref
  78.9 6.7 %grid_stage.2 = bf16[8,1,48,512]{3,2,1,0:T(8,128)(2,1)} custom-call(bf16[8,1,48,512]{3,2,1,0:T(8,128)(2,1)} %copy-done.2, bf16[384,384]{1,0:T(8,128)(2,1)} %constant.57.clone.perm_ref, bf16[384,384]{1,0:T(8,128)(2,1)} %constant.58.clone.back_ref, f32[1,512]{1,0:T(1,128)} %bitcast.36, bf16[512,1536]{1,0:T(8,128)(2,1)} %in_ref.7, ...), custom_call_target="tpu_custom_call" | custom-call | flops 3221225472 | bytes 6000000 | tf_op jit(solution)/shard_map/grid_stage/pallas_call | solution.py:309
  85.6 18.1 %all-to-all-done.3.s_ref = bf16[8,3,48,512]{3,2,1,0:T(8,128)(2,1)S(1)} async-done(((bf16[8,3,48,512]{3,2,1,0:T(8,128)(2,1)}), bf16[8,3,48,512]{3,2,1,0:T(8,128)(2,1)S(1)}, u32[]{:S(2)}, u32[]{:S(2)}) %all-to-all-start.3) | async-done | bytes 1179680 | tf_op jit(solution)/shard_map/all_to_all | solution.py:403
  103.7 3.7 %all-to-all-start.2 = ((bf16[8,1,48,512]{3,2,1,0:T(8,128)(2,1)}), bf16[8,1,48,512]{3,2,1,0:T(8,128)(2,1)S(1)}, u32[]{:S(2)}, u32[]{:S(2)}) async-start(bf16[8,1,48,512]{3,2,1,0:T(8,128)(2,1)} %grid_stage.2), calls=%async_computation.2 | async-start | bytes 786432 | tf_op jit(solution)/shard_map/all_to_all | solution.py:404
  107.4 15.2 %grid_stage.3 = bf16[8,3,48,512]{3,2,1,0:T(8,128)(2,1)} custom-call(bf16[8,3,48,512]{3,2,1,0:T(8,128)(2,1)} %copy-done.1, bf16[384,384]{1,0:T(8,128)(2,1)} %constant.57.clone.perm_ref, bf16[384,384]{1,0:T(8,128)(2,1)} %constant.58.clone.back_ref, f32[1,512]{1,0:T(1,128)} %bitcast.37, bf16[512,1536]{1,0:T(8,128)(2,1)} %in_ref.7, ...), custom_call_target="tpu_custom_call" | custom-call | flops 9663676416 | bytes 6000000 | tf_op jit(solution)/shard_map/grid_stage/pallas_call | solution.py:309
  122.5 34.4 %all_to_all.25 = bf16[8,3,48,512]{3,2,1,0:T(8,128)(2,1)S(1)} all-to-all(bf16[8,3,48,512]{3,2,1,0:T(8,128)(2,1)} %grid_stage.3), channel_id=1, replica_groups={{0,2,4,6,8,10,12,14},{1,3,5,7,9,11,13,15},{16,18,20,22,24,26,28,30},{17..., dimensions={0} | all-to-all | bytes 2359296 | tf_op jit(solution)/shard_map/all_to_all | solution.py:404
  157.1 2.0 %copy.30 = bf16[48,4,8,512]{3,2,1,0:T(8,128)(2,1)} copy(bf16[48,4,8,512]{3,0,1,2:T(8,128)(2,1)S(1)} %maximum_bitcast_fusion) | data formatting | bytes 3145728 | tf_op jit(solution)/shard_map/transpose | solution.py:406
  (19 shorter events, 0.8 us)
Async XLA Ops:
  2.3 8.8 %copy-start = (bf16[48,32,512]{2,0,1:T(8,128)(2,1)}, bf16[48,32,512]{2,0,1:T(8,128)(2,1)S(1)}, u32[]{:S(2)}) copy-start(bf16[48,32,512]{2,0,1:T(8,128)(2,1)S(1)} %copy.31) | copy-start | bytes 4718596
  2.3 7.4 %collective-permute-start = (bf16[1,48,512]{2,1,0:T(8,128)(2,1)S(1)}, bf16[1,48,512]{2,1,0:T(8,128)(2,1)S(1)}, u32[]{:S(2)}, u32[]{:S(2)}) collective-permute-start(bf16[1,48,512]{2,1,0:T(8,128)(2,1)S(1)} %get-tuple-element.9), channel_id=1, source_target_pairs={{0,1},{1,2},{2,3},{3,4},{4,5},{5,6},{6,7},{7,8},{8,9},{9,10},{10,1... | collective-permute-start | bytes 147464 | tf_op jit(solution)/shard_map/ppermute | solution.py:374
  2.8 6.9 %collective-permute-start.1 = (bf16[1,48,512]{2,1,0:T(8,128)(2,1)S(1)}, bf16[1,48,512]{2,1,0:T(8,128)(2,1)S(1)}, u32[]{:S(2)}, u32[]{:S(2)}) collective-permute-start(bf16[1,48,512]{2,1,0:T(8,128)(2,1)S(1)} %get-tuple-element.10), channel_id=1, source_target_pairs={{1,0},{2,1},{3,2},{4,3},{5,4},{6,5},{7,6},{8,7},{9,8},{10,9},{11,1... | collective-permute-start | bytes 147464 | tf_op jit(solution)/shard_map/ppermute | solution.py:375
  11.1 21.6 %copy-start.3 = (f32[225,16]{0,1:T(8,128)S(1)}, f32[225,16]{0,1:T(8,128)}, u32[]{:S(2)}) copy-start(f32[225,16]{0,1:T(8,128)} %param.30) | copy-start | bytes 43204
  26.8 12.2 %all-to-all-start = ((f32[16,1,128]{2,1,0:T(1,128)}), f32[16,1,128]{2,1,0:T(1,128)S(1)}, u32[]{:S(2)}, u32[]{:S(2)}) async-start(f32[16,1,128]{2,1,0:T(1,128)} %broadcast_in_dim.5), calls=%async_computation | async-start | bytes 16384 | tf_op jit(solution)/shard_map/all_to_all | solution.py:380
  48.1 21.4 %all-to-all-start.1 = ((bf16[8,1,48,512]{3,2,1,0:T(8,128)(2,1)}), bf16[8,1,48,512]{3,2,1,0:T(8,128)(2,1)S(1)}, u32[]{:S(2)}, u32[]{:S(2)}) async-start(bf16[8,1,48,512]{3,2,1,0:T(8,128)(2,1)} %block_stage.2), calls=%async_computation.1 | async-start | bytes 786432 | tf_op jit(solution)/shard_map/all_to_all | solution.py:403
  69.6 5.8 %copy-start.4 = (f32[225,16]{0,1:T(8,128)S(1)}, f32[225,16]{0,1:T(8,128)}, u32[]{:S(2)}) copy-start(f32[225,16]{0,1:T(8,128)} %param.34) | copy-start | bytes 43204
  69.6 8.4 %copy-start.2 = (bf16[8,1,48,512]{3,2,1,0:T(8,128)(2,1)}, bf16[8,1,48,512]{3,2,1,0:T(8,128)(2,1)S(1)}, u32[]{:S(2)}) copy-start(bf16[8,1,48,512]{3,2,1,0:T(8,128)(2,1)S(1)} %all-to-all-done.1.s_ref) | copy-start | bytes 1179652
  69.6 34.1 %all-to-all-start.3 = ((bf16[8,3,48,512]{3,2,1,0:T(8,128)(2,1)}), bf16[8,3,48,512]{3,2,1,0:T(8,128)(2,1)S(1)}, u32[]{:S(2)}, u32[]{:S(2)}) async-start(bf16[8,3,48,512]{3,2,1,0:T(8,128)(2,1)} %block_stage.3), calls=%async_computation.3 | async-start | bytes 2359296 | tf_op jit(solution)/shard_map/all_to_all | solution.py:403
  103.7 3.7 %copy-start.1 = (bf16[8,3,48,512]{3,2,1,0:T(8,128)(2,1)}, bf16[8,3,48,512]{3,2,1,0:T(8,128)(2,1)S(1)}, u32[]{:S(2)}) copy-start(bf16[8,3,48,512]{3,2,1,0:T(8,128)(2,1)S(1)} %all-to-all-done.3.s_ref) | copy-start | bytes 3538948
  103.7 18.9 %all-to-all-start.2 = ((bf16[8,1,48,512]{3,2,1,0:T(8,128)(2,1)}), bf16[8,1,48,512]{3,2,1,0:T(8,128)(2,1)S(1)}, u32[]{:S(2)}, u32[]{:S(2)}) async-start(bf16[8,1,48,512]{3,2,1,0:T(8,128)(2,1)} %grid_stage.2), calls=%async_computation.2 | async-start | bytes 786432 | tf_op jit(solution)/shard_map/all_to_all | solution.py:404

commit v3 on v2

--- a/solution.py
+++ b/solution.py
@@ -12,7 +12,7 @@
 HEAD_DIM = 32
 WIN = 8
 CELLS = WIN * WIN
-CHUNKS = (1, 3)
+CHUNKS = ((2, True), (2, True))
 LANES = 512
 SUB = 256
 VMEM_BYTES = 60 << 20
@@ -23,27 +23,35 @@
 F32 = jnp.float32
 
 
+def whole(shape):
+    return pl.BlockSpec(shape, lambda *_: (0,) * len(shape), pipeline_mode=pl.Buffered(1))
+
+
 def double_gelu(half):
     return half + half * lax.erf(half)
 
 
 def mbconv_kernel(
-    x_ref, w_ref, b_ref, dw_ref, db_ref, down_ref, shift_ref, act_ref, part_ref,
-    total_ref, tap_ref, *hidden_refs,
+    x_ref, before_ref, after_ref, w_ref, b_ref, dw_ref, db_ref, down_ref, shift_ref,
+    act_ref, part_ref, total_ref, tap_ref, *hidden_refs,
 ):
-    cols, rows, channels = x_ref.shape
+    out_cols, rows, channels = x_ref.shape
     lanes = w_ref.shape[1]
     sub = hidden_refs[0].shape[2]
-    out_cols = cols - 2
-    pieces = 2 if cols % 2 == 0 else 1
-    piece = cols // pieces
+    half = out_cols // 2
+    pieces = 2
+    piece = half + 1
     shift = shift_ref[...]
     for k in range(9):
         tap_ref[k] = jnp.broadcast_to(dw_ref[k : k + 1] * 0.5, (16, lanes)).astype(BF16)
 
     def expand(s, i):
         span = slice(s * sub, (s + 1) * sub)
-        cells = x_ref[i * piece : (i + 1) * piece].reshape(piece * rows, channels)
+        if i == 0:
+            cells = jnp.concatenate([before_ref[...], x_ref[:half]], axis=0)
+        else:
+            cells = jnp.concatenate([x_ref[half:], after_ref[...]], axis=0)
+        cells = cells.reshape(piece * rows, channels)
         hidden = jnp.dot(cells, w_ref[:, span], preferred_element_type=F32)
         hidden = double_gelu(hidden * ROOT_HALF + b_ref[:, span] * ROOT_HALF)
         hidden_refs[s][i * piece : (i + 1) * piece] = hidden.astype(BF16).reshape(piece, rows, sub)
@@ -76,11 +84,11 @@
         down_ref[...].astype(F32),
         precision=lax.Precision.HIGHEST,
         preferred_element_type=F32,
-    )
+    )[None]
 
     @pl.when(pl.program_id(0) == 0)
     def _():
-        part_ref[...] = part
+        part_ref[...] = jnp.broadcast_to(part, part_ref.shape)
 
     @pl.when(pl.program_id(0) > 0)
     def _():
@@ -96,8 +104,10 @@
     return jnp.asarray(shift, BF16)
 
 
-def mbconv(rimmed, expand_weight, expand_bias, depth_weight, depth_bias, squeeze_down):
-    cols, rows, channels = rimmed.shape
+def mbconv(
+    count, field, before, after, expand_weight, expand_bias, depth_weight, depth_bias, squeeze_down
+):
+    cols, rows, channels = field.shape
     expanded = expand_weight.shape[1]
     squeeze = squeeze_down.shape[1]
     return pl.pallas_call(
@@ -105,7 +115,9 @@
         name="mbconv",
         grid=(expanded // LANES,),
         in_specs=[
-            pl.BlockSpec((cols, rows, channels), lambda i: (0, 0, 0), pipeline_mode=pl.Buffered(1)),
+            whole(field.shape),
+            whole(before.shape),
+            whole(after.shape),
             pl.BlockSpec((channels, LANES), lambda i: (0, i)),
             pl.BlockSpec((1, LANES), lambda i: (0, i)),
             pl.BlockSpec((9, LANES), lambda i: (0, i)),
@@ -114,15 +126,15 @@
             pl.BlockSpec((rows, 3 * rows), lambda i: (0, 0)),
         ],
         out_specs=[
-            pl.BlockSpec((cols - 2, rows, LANES), lambda i: (0, 0, i)),
-            pl.BlockSpec((8, squeeze), lambda i: (0, 0)),
+            pl.BlockSpec((cols, rows, LANES), lambda i: (0, 0, i)),
+            pl.BlockSpec((count, 8, squeeze), lambda i: (0, 0, 0)),
         ],
         out_shape=[
-            jax.ShapeDtypeStruct((cols - 2, rows, expanded), BF16),
-            jax.ShapeDtypeStruct((8, squeeze), F32),
+            jax.ShapeDtypeStruct((cols, rows, expanded), BF16),
+            jax.ShapeDtypeStruct((count, 8, squeeze), F32),
         ],
         scratch_shapes=[pltpu.VMEM((8, LANES), F32), pltpu.VMEM((9, 16, LANES), BF16)]
-        + [pltpu.VMEM((cols, rows, SUB), BF16)] * (LANES // SUB),
+        + [pltpu.VMEM((cols + 2, rows, SUB), BF16)] * (LANES // SUB),
         cost_estimate=pl.CostEstimate(
             flops=2 * cols * rows * channels * expanded * 4,
             bytes_accessed=20_000_000,
@@ -130,7 +142,9 @@
         ),
         compiler_params=pltpu.CompilerParams(vmem_limit_bytes=VMEM_BYTES),
     )(
-        rimmed,
+        field,
+        before,
+        after,
         expand_weight,
         expand_bias.reshape(1, -1),
         depth_weight,
@@ -209,15 +223,16 @@
 
 
 def block_kernel(
-    act_ref, x_ref, part_ref, up_ref, proj_ref, gain_ref, in_ref, out_weight_ref, bias_ref,
-    out_ref, gate_ref, *scratch,
+    scale, split, me_ref, act_ref, x_ref, part_ref, up_ref, proj_ref, gain_ref, in_ref,
+    out_weight_ref, bias_ref, *refs,
 ):
+    outs, (gate_ref, sent_ref, *scratch) = (refs[:WIN], refs[WIN:]) if split else (refs[:1], refs[1:])
     cols, rows, expanded = act_ref.shape
     channels = x_ref.shape[2]
 
     @pl.when(pl.program_id(0) == 0)
     def _():
-        squeezed = jnp.broadcast_to(part_ref[...], (8, part_ref.shape[1]))
+        squeezed = jnp.sum(part_ref[...], axis=0) * scale
         squeezed = squeezed * jax.nn.sigmoid(squeezed)
         gate = jnp.dot(
             squeezed,
@@ -237,33 +252,50 @@
         [first[:, a * WIN : (a + 1) * WIN].reshape(CELLS, channels) for a in range(windows)],
         axis=0,
     )
-    second = attend(
-        stream, gain_ref, in_ref, out_weight_ref, bias_ref, scratch
-    ).reshape(windows, cols, WIN, channels)
-    second = jnp.concatenate([second[a] for a in range(windows)], axis=1)
-    out_ref[...] = second.reshape(out_ref.shape).astype(BF16)
-
-
-def grid_kernel(
-    s_ref, perm_ref, back_ref, gain_ref, in_ref, out_weight_ref, bias_ref, out_ref, *scratch,
-):
+    second = attend(stream, gain_ref, in_ref, out_weight_ref, bias_ref, scratch)
+    second = second.reshape(windows, cols, WIN, channels)
+    second = jnp.concatenate([second[a] for a in range(windows)], axis=1).astype(BF16)
+    deliver(second, me_ref, outs, sent_ref)
+
+
+def deliver(pieces, me_ref, outs, sent_ref):
+    if len(outs) == 1:
+        outs[0][:, 0] = pieces
+        return
+    sent_ref[...] = pieces
+    for s in range(WIN):
+        outs[s][0] = sent_ref[me_ref[0] ^ s]
+
+
+def gathered(ins):
+    if len(ins) == 1:
+        return ins[0][...].reshape(-1, ins[0].shape[-1])
+    return jnp.concatenate([ref[0] for ref in ins], axis=0)
+
+
+def grid_kernel(split, me_ref, *refs):
+    n = WIN if split else 1
+    ins, refs = refs[:n], refs[n:]
+    perm_ref, gain_ref, in_ref, out_weight_ref, bias_ref = refs[:5]
+    outs, (sent_ref, *scratch) = refs[5 : 5 + n], refs[5 + n :]
+
     @pl.when(pl.program_id(0) == 0)
     def _():
         prepare(in_ref, scratch[0], scratch[1])
 
-    cells = perm_ref.shape[0]
-    channels = s_ref.shape[-1]
-    incoming = s_ref[...].reshape(cells, channels)
-    stream = jnp.dot(perm_ref[...], incoming, preferred_element_type=F32)
-    result = attend(
-        stream, gain_ref, in_ref, out_weight_ref, bias_ref, scratch
-    ).astype(BF16)
-    result = jnp.dot(back_ref[...], result, preferred_element_type=F32)
-    out_ref[...] = result.astype(BF16).reshape(out_ref.shape)
-
-
-def whole(shape):
-    return pl.BlockSpec(shape, lambda *_: (0,) * len(shape), pipeline_mode=pl.Buffered(1))
+    stream = jnp.dot(perm_ref[0], gathered(ins), preferred_element_type=F32)
+    result = attend(stream, gain_ref, in_ref, out_weight_ref, bias_ref, scratch)
+    channels = result.shape[1]
+    result = result.reshape(-1, WIN, WIN, channels)
+    result = jnp.concatenate([result[a] for a in range(result.shape[0])], axis=1).astype(BF16)
+    deliver(result, me_ref, outs, sent_ref)
+
+
+def merge_kernel(split, me_ref, *refs):
+    n = WIN if split else 1
+    ins, perm_ref, out_ref = refs[:n], refs[n], refs[-1]
+    cells = jnp.dot(perm_ref[0], gathered(ins), preferred_element_type=F32)
+    out_ref[...] = cells.reshape(out_ref.shape).astype(BF16)
 
 
 def attention_scratch(cells, channels):
@@ -277,50 +309,100 @@
     ]
 
 
-def block_stage(start, count, active, field, part, up, proj, params):
+def partner_specs(split, rows, channels):
+    if split:
+        return [pl.BlockSpec((1, rows, channels), lambda b, me: (b, 0, 0))] * WIN
+    return [pl.BlockSpec((WIN, 1, rows, channels), lambda b, me: (0, b, 0, 0))]
+
+
+def partner_shapes(split, count, rows, channels):
+    if split:
+        return [jax.ShapeDtypeStruct((count, rows, channels), BF16)] * WIN
+    return [jax.ShapeDtypeStruct((WIN, count, rows, channels), BF16)]
+
+
+def block_stage(split, start, count, scale, me, active, field, parts, up, proj, params):
     cols, rows, channels = field.shape
     expanded = active.shape[2]
     cells = WIN * rows
     return pl.pallas_call(
-        block_kernel,
+        functools.partial(block_kernel, scale, split),
         name="block_stage",
-        grid=(count,),
-        in_specs=[
-            pl.BlockSpec((WIN, rows, expanded), lambda b: (b + start, 0, 0)),
-            pl.BlockSpec((WIN, rows, channels), lambda b: (b + start, 0, 0)),
-        ]
-        + [whole(p.shape) for p in (part, up, proj, *params)],
-        out_specs=pl.BlockSpec((WIN, 1, rows, channels), lambda b: (0, b, 0, 0)),
-        out_shape=jax.ShapeDtypeStruct((WIN, count, rows, channels), BF16),
-        scratch_shapes=[pltpu.VMEM((8, expanded), F32)] + attention_scratch(cells, channels),
+        grid_spec=pltpu.PrefetchScalarGridSpec(
+            num_scalar_prefetch=1,
+            grid=(count,),
+            in_specs=[
+                pl.BlockSpec((WIN, rows, expanded), lambda b, me: (b + start, 0, 0)),
+                pl.BlockSpec((WIN, rows, channels), lambda b, me: (b + start, 0, 0)),
+            ]
+            + [whole(p.shape) for p in (parts, up, proj, *params)],
+            out_specs=partner_specs(split, rows, channels),
+            scratch_shapes=[
+                pltpu.VMEM((8, expanded), F32),
+                pltpu.VMEM((WIN, rows, channels), BF16),
+            ]
+            + attention_scratch(cells, channels),
+        ),
+        out_shape=partner_shapes(split, count, rows, channels),
         cost_estimate=pl.CostEstimate(
             flops=2 * count * cells * channels * (expanded + 4 * channels) * 4,
             bytes_accessed=8_000_000,
             transcendentals=0,
         ),
         compiler_params=pltpu.CompilerParams(vmem_limit_bytes=VMEM_BYTES),
-    )(active, field, part, up, proj, *params)
-
-
-def grid_stage(received, perm, back, params):
-    _, count, rows, channels = received.shape
+    )(me, active, field, parts, up, proj, *params)
+
+
+def grid_stage(split, me, received, perm, params):
+    count, rows, channels = received[0].shape[-3:]
     cells = WIN * rows
-    spec = pl.BlockSpec((WIN, 1, rows, channels), lambda b: (0, b, 0, 0))
     return pl.pallas_call(
-        grid_kernel,
+        functools.partial(grid_kernel, split),
         name="grid_stage",
-        grid=(count,),
-        in_specs=[spec] + [whole(p.shape) for p in (perm, back, *params)],
-        out_specs=spec,
-        out_shape=jax.ShapeDtypeStruct(received.shape, BF16),
-        scratch_shapes=attention_scratch(cells, channels),
+        grid_spec=pltpu.PrefetchScalarGridSpec(
+            num_scalar_prefetch=1,
+            grid=(count,),
+            in_specs=partner_specs(split, rows, channels)
+            + [pl.BlockSpec((1, cells, cells), lambda b, me: (me[0], 0, 0))]
+            + [whole(p.shape) for p in params],
+            out_specs=partner_specs(split, rows, channels),
+            scratch_shapes=[pltpu.VMEM((WIN, rows, channels), BF16)]
+            + attention_scratch(cells, channels),
+        ),
+        out_shape=partner_shapes(split, count, rows, channels),
         cost_estimate=pl.CostEstimate(
             flops=2 * count * cells * channels * 4 * channels * 4,
             bytes_accessed=6_000_000,
             transcendentals=0,
         ),
         compiler_params=pltpu.CompilerParams(vmem_limit_bytes=VMEM_BYTES),
-    )(received, perm, back, *params)
+    )(me, *received, perm, *params)
+
+
+def merge_stage(split, start, total, me, received, perm, merged):
+    count, rows, channels = received[0].shape[-3:]
+    cells = WIN * rows
+    n = len(received)
+    return pl.pallas_call(
+        functools.partial(merge_kernel, split),
+        name="merge_stage",
+        grid_spec=pltpu.PrefetchScalarGridSpec(
+            num_scalar_prefetch=1,
+            grid=(count,),
+            in_specs=partner_specs(split, rows, channels)
+            + [pl.BlockSpec((1, cells, cells), lambda b, me: (me[0], 0, 0))]
+            + [pl.BlockSpec(memory_space=pl.ANY)] * (merged is not None),
+            out_specs=pl.BlockSpec((rows, WIN, channels), lambda b, me: (0, b + start, 0)),
+        ),
+        out_shape=jax.ShapeDtypeStruct((rows, total * WIN, channels), BF16),
+        input_output_aliases={} if merged is None else {n + 2: 0},
+        cost_estimate=pl.CostEstimate(
+            flops=2 * count * cells * cells * channels,
+            bytes_accessed=2_000_000,
+            transcendentals=0,
+        ),
+        compiler_params=pltpu.CompilerParams(vmem_limit_bytes=VMEM_BYTES),
+    )(me, *received, perm, *([] if merged is None else [merged]))
 
 
 def turned_bias(pos_table):
@@ -337,15 +419,16 @@
     return gain.reshape(1, -1), in_weight, out_weight, turned_bias(pos_table)
 
 
-def grid_order(rows):
+def cell_orders(rows):
     per = rows // WIN
-    source = np.zeros(WIN * rows, np.int64)
-    for a in range(per):
-        for j in range(WIN):
-            for i in range(WIN):
-                source[(a * WIN + j) * WIN + i] = j * rows + i * per + a
-    one_hot = source[:, None] == np.arange(WIN * rows)[None, :]
-    return jnp.asarray(one_hot, BF16), jnp.asarray(one_hot.T, BF16)
+    cells = WIN * rows
+    into = np.zeros((WIN, cells, cells), np.float32)
+    back = np.zeros((WIN, cells, cells), np.float32)
+    a, j, i = np.meshgrid(np.arange(per), np.arange(WIN), np.arange(WIN), indexing="ij")
+    for m in range(WIN):
+        into[m, (a * WIN + j) * WIN + i, (m ^ j) * rows + i * per + a] = 1.0
+        back[m, (i * per + a) * WIN + j, (m ^ j) * rows + a * WIN + i] = 1.0
+    return jnp.asarray(into, BF16), jnp.asarray(back, BF16)
 
 
 def per_device(
@@ -370,40 +453,68 @@
     count = lax.axis_size("lon")
     per = count // WIN
     groups = [[j * per + r for j in range(WIN)] for r in range(per)]
+    place = lax.axis_index("lon") // per
+    places = {True: place.reshape(1).astype(jnp.int32), False: jnp.zeros((1,), jnp.int32)}
+    before = lax.ppermute(
+        jnp.swapaxes(input_field[:, -1:], 0, 1),
+        "lon",
+        [(i, (i + 1) % count) for i in range(count)],
+    )
+    after = lax.ppermute(
+        jnp.swapaxes(input_field[:, :1], 0, 1),
+        "lon",
+        [((i + 1) % count, i) for i in range(count)],
+    )
     field = jnp.swapaxes(input_field, 0, 1)
-    before = lax.ppermute(field[-1:], "lon", [(i, (i + 1) % count) for i in range(count)])
-    after = lax.ppermute(field[:1], "lon", [((i + 1) % count, i) for i in range(count)])
-    rimmed = jnp.concatenate([before, field, after], axis=0)
     active, part = mbconv(
-        rimmed, expand_weight, expand_bias, depth_weight, depth_bias, squeeze_down
+        count, field, before, after, expand_weight, expand_bias, depth_weight, depth_bias,
+        squeeze_down,
     )
-    parts = lax.all_to_all(
-        jnp.broadcast_to(part[None, :1], (count, 1, part.shape[1])), "lon", 0, 0, tiled=True
-    )
-    part = jnp.sum(parts, axis=0) * (ROOT_HALF / (rows * cols * count))
-    perm, back = grid_order(rows)
+    parts = lax.all_to_all(part, "lon", 0, 0, tiled=True)
+    scale = ROOT_HALF / (rows * cols * count)
+    into, back = cell_orders(rows)
     block_params = attention_params(block_gain, block_in_weight, block_out_weight, block_table)
     grid_params = attention_params(grid_gain, grid_in_weight, grid_out_weight, grid_table)
-    exchange = functools.partial(
-        lax.all_to_all,
-        axis_name="lon",
-        split_axis=0,
-        concat_axis=0,
-        axis_index_groups=groups,
-        tiled=True,
-    )
+
+    def exchange(split, pieces):
+        if not split:
+            return [
+                lax.all_to_all(
+                    pieces[0], "lon", 0, 0, axis_index_groups=groups, tiled=True
+                )
+            ]
+        return [pieces[0]] + [
+            lax.ppermute(
+                pieces[s],
+                "lon",
+                [(j * per + r, (j ^ s) * per + r) for j in range(WIN) for r in range(per)],
+            )
+            for s in range(1, WIN)
+        ]
+
+    total = cols // WIN
+    chunks = CHUNKS if sum(c[0] for c in CHUNKS) == total else ((total, False),)
+    starts = [sum(c[0] for c in chunks[:k]) for k in range(len(chunks))]
+    sent = [
+        block_stage(
+            split, start, size, scale, places[split], active, field, parts, squeeze_up,
+            project_weight, block_params,
+        )
+        for start, (size, split) in zip(starts, chunks)
+    ]
+    received = [exchange(split, pieces) for pieces, (_, split) in zip(sent, chunks)]
     results = []
-    start = 0
-    total = cols // WIN
-    for size in CHUNKS if sum(CHUNKS) == total else (total,):
-        sent = block_stage(
-            start, size, active, field, part, squeeze_up, project_weight, block_params
+    for k, (_, split) in enumerate(chunks):
+        pieces = received[k]
+        if k + 1 < len(chunks):
+            pieces, _ = lax.optimization_barrier((pieces, sent[k + 1][0]))
+        results.append(grid_stage(split, places[split], pieces, into, grid_params))
+    merged = None
+    for start, result, (_, split) in zip(starts, results, chunks):
+        merged = merge_stage(
+            split, start, total, places[split], exchange(split, result), back, merged
         )
-        start += size
-        result = grid_stage(exchange(sent), perm, back, grid_params)
-        results.append(exchange(result))
-    merged = jnp.concatenate(results, axis=1)
-    return merged.transpose(2, 1, 0, 3).reshape(rows, cols, channels)
+    return merged
 
 
 def solution(mesh):

time: 160 us -> 146 us (0.912)
  blocking collectives: 34.4 us -> 0 us
  starting transfers between devices: 24.4 us -> 57.3 us
  waiting for transfers between devices: 22.7 us -> 8.12 us
  Pallas kernels: 62.7 us -> 68.1 us
  other arithmetic: 2.14 us -> 0.09 us
    ppermute x2 -> x30, starting transfers between devices: 5.56 us -> 51.5 us  [the longest x28 46 us: exchange(): lax.ppermute(pieces[s], 'lon', [(j * per + r, (j ^ s) * per + r) for j in...]
    all_to_all x1 -> x0, blocking collectives: 34.4 us -> none  [per_device(): results.append(exchange(result))]
    all_to_all x4 -> x1, waiting for transfers between devices: 21 us -> 3.39 us  [per_device(): parts = lax.all_to_all(part, 'lon', 0, 0, tiled=True)]
    all_to_all x4 -> x1, starting transfers between devices: 18.9 us -> 5.78 us  [per_device(): parts = lax.all_to_all(part, 'lon', 0, 0, tiled=True)]
    pallas_call x4 -> x6, Pallas kernels: 48.2 us -> 53.5 us  [the longest x2 26.6 us: block_stage(): pl.pallas_call(functools.partial(block_kernel, scale, split), name='block...]
    ppermute x2 -> x30, waiting for transfers between devices: 1.7 us -> 4.73 us  [the longest x28 3.04 us: exchange(): lax.ppermute(pieces[s], 'lon', [(j * per + r, (j ^ s) * per + r) for j in...]
    transpose x1, local copies, waits for them, and re-layouts: 2.01 us -> 0.01 us  [per_device(): jnp.swapaxes(input_field[:, :1], 0, 1)]
    unnamed x11 -> x77, local copies, waits for them, and re-layouts: 2.3 us -> 4.27 us
  transfers between devices with their start and end apart: 6 -> 31, of which waited for: 3 -> 5; matrix products, arithmetic and copies ran while one was open for 4% -> 5% of each run, Pallas kernels for 25% -> 26%
where the time goes in v3:
time: 146 us; the launch traced here: 145 us
  Pallas kernels  68.1 us (47%)
  starting transfers between devices  57.3 us (39%)
  waiting for transfers between devices  8.12 us (6%)
  local copies, waits for them, and re-layouts  6.04 us (4%)
  matrix products  5.24 us (4%)
    ppermute x28, starting transfers between devices, exchange(): lax.ppermute(pieces[s], 'lon', [(j * per + r, (j ^ s) * per + r) for j in...  46 us
    pallas_call x2, Pallas kernels, block_stage(): pl.pallas_call(functools.partial(block_kernel, scale, split), name='block...  26.6 us
    pallas_call x2, Pallas kernels, grid_stage(): pl.pallas_call(functools.partial(grid_kernel, split), name='grid_stage',...  21.3 us
    pallas_call x1, Pallas kernels, mbconv(): pl.pallas_call(mbconv_kernel, name='mbconv', grid=(expanded // LANES,), i...  14.6 us
    all_to_all x1, starting transfers between devices, per_device(): parts = lax.all_to_all(part, 'lon', 0, 0, tiled=True)  5.78 us
    pallas_call x2, Pallas kernels, merge_stage(): pl.pallas_call(functools.partial(merge_kernel, split), name='merge_stage'...  5.59 us
    dot_general x2, matrix products, turned_bias(): jnp.einsum('jir,rh->jhi', one_hot, pos_table * LOG2E, precision=lax.Preci...  5.24 us
    ppermute x1, starting transfers between devices, per_device(): lax.ppermute(jnp.swapaxes(input_field[:, :1], 0, 1), 'lon', [((i + 1) % c...  5.06 us
  transfers between devices with their start and end apart: 31, of which 5 were waited for; matrix products, arithmetic and copies ran while one was open for 5% of the time, Pallas kernels for 26%

profile of v3, /device:TPU:0, one launch (start us, length us, event | category | flops | bytes accessed | tf_op | source)
XLA Modules:
  0.0 145.3 jit_solution(17300468904833370551)
XLA Ops:
  2.8 5.1 %collective-permute-start.1 = (bf16[1,48,512]{2,1,0:T(8,128)(2,1)S(1)}, bf16[1,48,512]{2,1,0:T(8,128)(2,1)S(1)}, u32[]{:S(2)}, u32[]{:S(2)}) collective-permute-start(bf16[1,48,512]{2,1,0:T(8,128)(2,1)S(1)} %get-tuple-element.89), channel_id=1, source_target_pairs={{1,0},{2,1},{3,2},{4,3},{5,4},{6,5},{7,6},{8,7},{9,8},{10,9},{11,1... | collective-permute-start | bytes 147464 | tf_op jit(solution)/shard_map/ppermute | solution.py:463
  10.3 14.6 %mbconv.1 = (bf16[32,48,2048]{2,1,0:T(8,128)(2,1)}, f32[16,8,128]{2,1,0:T(8,128)}) custom-call(bf16[32,48,512]{2,1,0:T(8,128)(2,1)} %bitcast.21, bf16[1,48,512]{2,1,0:T(8,128)(2,1)} %copy-done.34, bf16[1,48,512]{2,1,0:T(8,128)(2,1)} %copy-done.35, bf16[512,2048]{1,0:T(8,128)(2,1)} %w_ref.1, f32[1,2048]{1,0:T(1,128)} %bitcast.24, f32[9,2048]{1,0:T(8,128)} %dw_ref.1, ...), custom_call_target="tpu_custom_call" | custom-call | flops 12884901888 | bytes 20000000 | tf_op jit(solution)/shard_map/mbconv/pallas_call | solution.py:113
  24.9 5.8 %all-to-all-start = ((f32[16,8,128]{2,1,0:T(8,128)}), f32[16,8,128]{2,1,0:T(8,128)S(1)}, u32[]{:S(2)}, u32[]{:S(2)}) async-start(f32[16,8,128]{2,1,0:T(8,128)} %get-tuple-element.48), calls=%async_computation | async-start | bytes 131072 | tf_op jit(solution)/shard_map/all_to_all | solution.py:473
  30.7 2.6 %fusion.4 = f32[64,16,64]{2,1,0:T(8,128)S(1)} fusion(s32[64,64]{1,0:T(8,128)S(1)} %add_add_fusion, f32[225,16]{0,1:T(8,128)S(1)} %copy-done.36), kind=kOutput, calls=%fused_computation.5 | convolution fusion | flops 177872400 | bytes 292928 | tf_op jit(solution)/shard_map/jir,rh->jhi/dot_general | solution.py:414
  34.2 3.4 %all-to-all-done.part_ref = f32[16,8,128]{2,1,0:T(8,128)S(1)} async-done(((f32[16,8,128]{2,1,0:T(8,128)}), f32[16,8,128]{2,1,0:T(8,128)S(1)}, u32[]{:S(2)}, u32[]{:S(2)}) %all-to-all-start) | async-done | bytes 65568 | tf_op jit(solution)/shard_map/all_to_all | solution.py:473
  38.2 13.3 %block_stage.3 = (bf16[2,48,512]{2,1,0:T(8,128)(2,1)}, bf16[2,48,512]{2,1,0:T(8,128)(2,1)}, bf16[2,48,512]{2,1,0:T(8,128)(2,1)}, bf16[2,48,512]{2,1,0:T(8,128)(2...) custom-call(s32[1]{0:T(128)} %bitcast.me_ref, ...), custom_call_target="tpu_custom_call" | custom-call | flops 12884901888 | bytes 8000000 | tf_op jit(solution)/shard_map/block_stage/pallas_call | solution.py:328
  52.3 2.7 %collective-permute-start.18 = (bf16[2,48,512]{2,1,0:T(8,128)(2,1)}, bf16[2,48,512]{2,1,0:T(8,128)(2,1)S(1)}, u32[]{:S(2)}, u32[]{:S(2)}) collective-permute-start(bf16[2,48,512]{2,1,0:T(8,128)(2,1)} %get-tuple-element.68), channel_id=1, source_target_pairs={{0,6},{1,7},{2,4},{3,5},{4,2},{5,3},{6,0},{7,1},{8,14},{9,15},{10,... | collective-permute-start | bytes 294920 | tf_op jit(solution)/shard_map/ppermute | solution.py:487
  55.2 2.3 %collective-permute-start.20 = (bf16[2,48,512]{2,1,0:T(8,128)(2,1)}, bf16[2,48,512]{2,1,0:T(8,128)(2,1)S(1)}, u32[]{:S(2)}, u32[]{:S(2)}) collective-permute-start(bf16[2,48,512]{2,1,0:T(8,128)(2,1)} %get-tuple-element.70), channel_id=1, source_target_pairs={{0,10},{1,11},{2,8},{3,9},{4,14},{5,15},{6,12},{7,13},{8,2},{9,3},... | collective-permute-start | bytes 294920 | tf_op jit(solution)/shard_map/ppermute | solution.py:487
  57.5 13.3 %block_stage.2 = (bf16[2,48,512]{2,1,0:T(8,128)(2,1)}, bf16[2,48,512]{2,1,0:T(8,128)(2,1)}, bf16[2,48,512]{2,1,0:T(8,128)(2,1)}, bf16[2,48,512]{2,1,0:T(8,128)(2...) custom-call(s32[1]{0:T(128)} %bitcast.me_ref, ...), custom_call_target="tpu_custom_call" | custom-call | flops 12884901888 | bytes 8000000 | tf_op jit(solution)/shard_map/block_stage/pallas_call | solution.py:328
  72.6 3.5 %collective-permute-start.22 = (bf16[2,48,512]{2,1,0:T(8,128)(2,1)S(1)}, bf16[2,48,512]{2,1,0:T(8,128)(2,1)S(1)}, u32[]{:S(2)}, u32[]{:S(2)}) collective-permute-start(bf16[2,48,512]{2,1,0:T(8,128)(2,1)S(1)} %copy-done.28), channel_id=1, source_target_pairs={{0,14},{1,15},{2,12},{3,13},{4,10},{5,11},{6,8},{7,9},{8,6},{9,7},... | collective-permute-start | bytes 294920 | tf_op jit(solution)/shard_map/ppermute | solution.py:487
  76.3 2.6 %fusion.5 = f32[64,16,64]{2,1,0:T(8,128)S(1)} fusion(s32[64,64]{1,0:T(8,128)S(1)} %add_add_fusion, f32[225,16]{0,1:T(8,128)S(1)} %copy-done.37), kind=kOutput, calls=%fused_computation.6 | convolution fusion | flops 177872400 | bytes 292928 | tf_op jit(solution)/shard_map/jir,rh->jhi/dot_general | solution.py:414
  79.9 3.3 %collective-permute-start.4 = (bf16[2,48,512]{2,1,0:T(8,128)(2,1)}, bf16[2,48,512]{2,1,0:T(8,128)(2,1)S(1)}, u32[]{:S(2)}, u32[]{:S(2)}) collective-permute-start(bf16[2,48,512]{2,1,0:T(8,128)(2,1)} %get-tuple-element.52), channel_id=1, source_target_pairs={{0,6},{1,7},{2,4},{3,5},{4,2},{5,3},{6,0},{7,1},{8,14},{9,15},{10,... | collective-permute-start | bytes 294920 | tf_op jit(solution)/shard_map/ppermute | solution.py:487
  83.2 2.5 %collective-permute-start.6 = (bf16[2,48,512]{2,1,0:T(8,128)(2,1)}, bf16[2,48,512]{2,1,0:T(8,128)(2,1)S(1)}, u32[]{:S(2)}, u32[]{:S(2)}) collective-permute-start(bf16[2,48,512]{2,1,0:T(8,128)(2,1)} %get-tuple-element.54), channel_id=1, source_target_pairs={{0,10},{1,11},{2,8},{3,9},{4,14},{5,15},{6,12},{7,13},{8,2},{9,3},... | collective-permute-start | bytes 294920 | tf_op jit(solution)/shard_map/ppermute | solution.py:487
  87.4 3.5 %collective-permute-start.8 = (bf16[2,48,512]{2,1,0:T(8,128)(2,1)}, bf16[2,48,512]{2,1,0:T(8,128)(2,1)S(1)}, u32[]{:S(2)}, u32[]{:S(2)}) collective-permute-start(bf16[2,48,512]{2,1,0:T(8,128)(2,1)} %get-tuple-element.56), channel_id=1, source_target_pairs={{0,14},{1,15},{2,12},{3,13},{4,10},{5,11},{6,8},{7,9},{8,6},{9,7},... | collective-permute-start | bytes 294920 | tf_op jit(solution)/shard_map/ppermute | solution.py:487
  90.9 10.6 %grid_stage.3 = (bf16[2,48,512]{2,1,0:T(8,128)(2,1)}, bf16[2,48,512]{2,1,0:T(8,128)(2,1)}, bf16[2,48,512]{2,1,0:T(8,128)(2,1)}, bf16[2,48,512]{2,1,0:T(8,128)(2,...) custom-call(s32[1]{0:T(128)} %bitcast.me_ref, ...), custom_call_target="tpu_custom_call" | custom-call | flops 6442450944 | bytes 6000000 | tf_op jit(solution)/shard_map/grid_stage/pallas_call | solution.py:359
  101.8 3.3 %collective-permute-start.25 = (bf16[2,48,512]{2,1,0:T(8,128)(2,1)}, bf16[2,48,512]{2,1,0:T(8,128)(2,1)S(1)}, u32[]{:S(2)}, u32[]{:S(2)}) collective-permute-start(bf16[2,48,512]{2,1,0:T(8,128)(2,1)} %get-tuple-element.84), channel_id=1, source_target_pairs={{0,6},{1,7},{2,4},{3,5},{4,2},{5,3},{6,0},{7,1},{8,14},{9,15},{10,... | collective-permute-start | bytes 294920 | tf_op jit(solution)/shard_map/ppermute | solution.py:487
  105.2 2.5 %collective-permute-start.27 = (bf16[2,48,512]{2,1,0:T(8,128)(2,1)}, bf16[2,48,512]{2,1,0:T(8,128)(2,1)S(1)}, u32[]{:S(2)}, u32[]{:S(2)}) collective-permute-start(bf16[2,48,512]{2,1,0:T(8,128)(2,1)} %get-tuple-element.86), channel_id=1, source_target_pairs={{0,10},{1,11},{2,8},{3,9},{4,14},{5,15},{6,12},{7,13},{8,2},{9,3},... | collective-permute-start | bytes 294920 | tf_op jit(solution)/shard_map/ppermute | solution.py:487
  107.8 10.7 %grid_stage.2 = (bf16[2,48,512]{2,1,0:T(8,128)(2,1)}, bf16[2,48,512]{2,1,0:T(8,128)(2,1)}, bf16[2,48,512]{2,1,0:T(8,128)(2,1)}, bf16[2,48,512]{2,1,0:T(8,128)(2,...) custom-call(s32[1]{0:T(128)} %bitcast.me_ref, ...), custom_call_target="tpu_custom_call" | custom-call | flops 6442450944 | bytes 6000000 | tf_op jit(solution)/shard_map/grid_stage/pallas_call | solution.py:359
  120.2 3.5 %collective-permute-start.29 = (bf16[2,48,512]{2,1,0:T(8,128)(2,1)S(1)}, bf16[2,48,512]{2,1,0:T(8,128)(2,1)S(1)}, u32[]{:S(2)}, u32[]{:S(2)}) collective-permute-start(bf16[2,48,512]{2,1,0:T(8,128)(2,1)S(1)} %copy-done.18), channel_id=1, source_target_pairs={{0,14},{1,15},{2,12},{3,13},{4,10},{5,11},{6,8},{7,9},{8,6},{9,7},... | collective-permute-start | bytes 294920 | tf_op jit(solution)/shard_map/ppermute | solution.py:487
  125.8 5.0 %collective-permute-start.13 = (bf16[2,48,512]{2,1,0:T(8,128)(2,1)}, bf16[2,48,512]{2,1,0:T(8,128)(2,1)S(1)}, u32[]{:S(2)}, u32[]{:S(2)}) collective-permute-start(bf16[2,48,512]{2,1,0:T(8,128)(2,1)} %get-tuple-element.62), channel_id=1, source_target_pairs={{0,10},{1,11},{2,8},{3,9},{4,14},{5,15},{6,12},{7,13},{8,2},{9,3},... | collective-permute-start | bytes 294920 | tf_op jit(solution)/shard_map/ppermute | solution.py:487
  130.8 2.8 %collective-permute-start.14 = (bf16[2,48,512]{2,1,0:T(8,128)(2,1)}, bf16[2,48,512]{2,1,0:T(8,128)(2,1)S(1)}, u32[]{:S(2)}, u32[]{:S(2)}) collective-permute-start(bf16[2,48,512]{2,1,0:T(8,128)(2,1)} %get-tuple-element.63), channel_id=1, source_target_pairs={{0,12},{1,13},{2,14},{3,15},{4,8},{5,9},{6,10},{7,11},{8,4},{9,5},... | collective-permute-start | bytes 294920 | tf_op jit(solution)/shard_map/ppermute | solution.py:487
  136.2 2.8 %merge_stage.2.refs_9_ = bf16[48,32,512]{2,1,0:T(8,128)(2,1)} custom-call(s32[1]{0:T(128)} %bitcast.me_ref, bf16[2,48,512]{2,1,0:T(8,128)(2,1)} %get-tuple-element.81.refs_0_, bf16[2,48,512]{2,1,0:T(8,128)(2,1)} %copy-done.1, bf16[2,48,512]{2,1,0:T(8,128)(2,1)} %copy-done.2, bf16[2,48,512]{2,1,0:T(8,128)(2,1)} %copy-done.3, bf16[2,48,512]{2,1,0:T(8,128)(2,1)} %copy-done.4, ...), custom_call_target="tpu_custom_call" | custom-call | flops 301989888 | bytes 2000000 | tf_op jit(solution)/shard_map/merge_stage/pallas_call | solution.py:386
  139.0 2.6 %collective-permute-done.13.refs_5_ = bf16[2,48,512]{2,1,0:T(8,128)(2,1)S(1)} collective-permute-done((bf16[2,48,512]{2,1,0:T(8,128)(2,1)}, bf16[2,48,512]{2,1,0:T(8,128)(2,1)S(1)}, u32[]{:S(2)}, u32[]{:S(2)}) %collective-permute-start.13) | collective-permute-done | bytes 98336 | tf_op jit(solution)/shard_map/ppermute | solution.py:487
  142.5 2.8 %merge_stage.3 = bf16[48,32,512]{2,1,0:T(8,128)(2,1)} custom-call(s32[1]{0:T(128)} %bitcast.me_ref, bf16[2,48,512]{2,1,0:T(8,128)(2,1)} %get-tuple-element.57.refs_0_, bf16[2,48,512]{2,1,0:T(8,128)(2,1)} %copy-done.14, bf16[2,48,512]{2,1,0:T(8,128)(2,1)} %copy-done.6, bf16[2,48,512]{2,1,0:T(8,128)(2,1)} %copy-done.7, ...), custom_call_target="tpu_custom_call", output_to_operand_aliasing={{}: (10, {})} | custom-call | flops 301989888 | bytes 2000000 | tf_op jit(solution)/shard_map/merge_stage/pallas_call | solution.py:386
  (129 shorter events, 19.7 us)
Async XLA Ops:
  24.9 12.7 %all-to-all-start = ((f32[16,8,128]{2,1,0:T(8,128)}), f32[16,8,128]{2,1,0:T(8,128)S(1)}, u32[]{:S(2)}, u32[]{:S(2)}) async-start(f32[16,8,128]{2,1,0:T(8,128)} %get-tuple-element.48), calls=%async_computation | async-start | bytes 131072 | tf_op jit(solution)/shard_map/all_to_all | solution.py:473
  51.5 19.4 %collective-permute-start.16 = (bf16[2,48,512]{2,1,0:T(8,128)(2,1)}, bf16[2,48,512]{2,1,0:T(8,128)(2,1)S(1)}, u32[]{:S(2)}, u32[]{:S(2)}) collective-permute-start(bf16[2,48,512]{2,1,0:T(8,128)(2,1)} %get-tuple-element.66), channel_id=1, source_target_pairs={{0,2},{1,3},{2,0},{3,1},{4,6},{5,7},{6,4},{7,5},{8,10},{9,11},{10,... | collective-permute-start | bytes 294920 | tf_op jit(solution)/shard_map/ppermute | solution.py:487
  51.7 21.0 %collective-permute-start.17 = (bf16[2,48,512]{2,1,0:T(8,128)(2,1)}, bf16[2,48,512]{2,1,0:T(8,128)(2,1)S(1)}, u32[]{:S(2)}, u32[]{:S(2)}) collective-permute-start(bf16[2,48,512]{2,1,0:T(8,128)(2,1)} %get-tuple-element.67), channel_id=1, source_target_pairs={{0,4},{1,5},{2,6},{3,7},{4,0},{5,1},{6,2},{7,3},{8,12},{9,13},{10,... | collective-permute-start | bytes 294920 | tf_op jit(solution)/shard_map/ppermute | solution.py:487
  52.3 23.9 %collective-permute-start.18 = (bf16[2,48,512]{2,1,0:T(8,128)(2,1)}, bf16[2,48,512]{2,1,0:T(8,128)(2,1)S(1)}, u32[]{:S(2)}, u32[]{:S(2)}) collective-permute-start(bf16[2,48,512]{2,1,0:T(8,128)(2,1)} %get-tuple-element.68), channel_id=1, source_target_pairs={{0,6},{1,7},{2,4},{3,5},{4,2},{5,3},{6,0},{7,1},{8,14},{9,15},{10,... | collective-permute-start | bytes 294920 | tf_op jit(solution)/shard_map/ppermute | solution.py:487
  55.0 21.3 %collective-permute-start.19 = (bf16[2,48,512]{2,1,0:T(8,128)(2,1)}, bf16[2,48,512]{2,1,0:T(8,128)(2,1)S(1)}, u32[]{:S(2)}, u32[]{:S(2)}) collective-permute-start(bf16[2,48,512]{2,1,0:T(8,128)(2,1)} %get-tuple-element.69), channel_id=1, source_target_pairs={{0,8},{1,9},{2,10},{3,11},{4,12},{5,13},{6,14},{7,15},{8,0},{9,1},... | collective-permute-start | bytes 294920 | tf_op jit(solution)/shard_map/ppermute | solution.py:487
  55.2 24.6 %collective-permute-start.20 = (bf16[2,48,512]{2,1,0:T(8,128)(2,1)}, bf16[2,48,512]{2,1,0:T(8,128)(2,1)S(1)}, u32[]{:S(2)}, u32[]{:S(2)}) collective-permute-start(bf16[2,48,512]{2,1,0:T(8,128)(2,1)} %get-tuple-element.70), channel_id=1, source_target_pairs={{0,10},{1,11},{2,8},{3,9},{4,14},{5,15},{6,12},{7,13},{8,2},{9,3},... | collective-permute-start | bytes 294920 | tf_op jit(solution)/shard_map/ppermute | solution.py:487
  70.9 12.3 %collective-permute-start.21 = (bf16[2,48,512]{2,1,0:T(8,128)(2,1)S(1)}, bf16[2,48,512]{2,1,0:T(8,128)(2,1)S(1)}, u32[]{:S(2)}, u32[]{:S(2)}) collective-permute-start(bf16[2,48,512]{2,1,0:T(8,128)(2,1)S(1)} %copy-done.31), channel_id=1, source_target_pairs={{0,12},{1,13},{2,14},{3,15},{4,8},{5,9},{6,10},{7,11},{8,4},{9,5},... | collective-permute-start | bytes 294920 | tf_op jit(solution)/shard_map/ppermute | solution.py:487
  72.6 10.6 %collective-permute-start.22 = (bf16[2,48,512]{2,1,0:T(8,128)(2,1)S(1)}, bf16[2,48,512]{2,1,0:T(8,128)(2,1)S(1)}, u32[]{:S(2)}, u32[]{:S(2)}) collective-permute-start(bf16[2,48,512]{2,1,0:T(8,128)(2,1)S(1)} %copy-done.28), channel_id=1, source_target_pairs={{0,14},{1,15},{2,12},{3,13},{4,10},{5,11},{6,8},{7,9},{8,6},{9,7},... | collective-permute-start | bytes 294920 | tf_op jit(solution)/shard_map/ppermute | solution.py:487
  76.3 11.1 %collective-permute-start.3 = (bf16[2,48,512]{2,1,0:T(8,128)(2,1)}, bf16[2,48,512]{2,1,0:T(8,128)(2,1)S(1)}, u32[]{:S(2)}, u32[]{:S(2)}) collective-permute-start(bf16[2,48,512]{2,1,0:T(8,128)(2,1)} %get-tuple-element.51), channel_id=1, source_target_pairs={{0,4},{1,5},{2,6},{3,7},{4,0},{5,1},{6,2},{7,3},{8,12},{9,13},{10,... | collective-permute-start | bytes 294920 | tf_op jit(solution)/shard_map/ppermute | solution.py:487
  79.9 21.7 %collective-permute-start.4 = (bf16[2,48,512]{2,1,0:T(8,128)(2,1)}, bf16[2,48,512]{2,1,0:T(8,128)(2,1)S(1)}, u32[]{:S(2)}, u32[]{:S(2)}) collective-permute-start(bf16[2,48,512]{2,1,0:T(8,128)(2,1)} %get-tuple-element.52), channel_id=1, source_target_pairs={{0,6},{1,7},{2,4},{3,5},{4,2},{5,3},{6,0},{7,1},{8,14},{9,15},{10,... | collective-permute-start | bytes 294920 | tf_op jit(solution)/shard_map/ppermute | solution.py:487
  83.2 18.6 %collective-permute-start.5 = (bf16[2,48,512]{2,1,0:T(8,128)(2,1)}, bf16[2,48,512]{2,1,0:T(8,128)(2,1)S(1)}, u32[]{:S(2)}, u32[]{:S(2)}) collective-permute-start(bf16[2,48,512]{2,1,0:T(8,128)(2,1)} %get-tuple-element.53), channel_id=1, source_target_pairs={{0,8},{1,9},{2,10},{3,11},{4,12},{5,13},{6,14},{7,15},{8,0},{9,1},... | collective-permute-start | bytes 294920 | tf_op jit(solution)/shard_map/ppermute | solution.py:487
  83.2 18.6 %collective-permute-start.6 = (bf16[2,48,512]{2,1,0:T(8,128)(2,1)}, bf16[2,48,512]{2,1,0:T(8,128)(2,1)S(1)}, u32[]{:S(2)}, u32[]{:S(2)}) collective-permute-start(bf16[2,48,512]{2,1,0:T(8,128)(2,1)} %get-tuple-element.54), channel_id=1, source_target_pairs={{0,10},{1,11},{2,8},{3,9},{4,14},{5,15},{6,12},{7,13},{8,2},{9,3},... | collective-permute-start | bytes 294920 | tf_op jit(solution)/shard_map/ppermute | solution.py:487
  85.7 19.5 %collective-permute-start.7 = (bf16[2,48,512]{2,1,0:T(8,128)(2,1)}, bf16[2,48,512]{2,1,0:T(8,128)(2,1)S(1)}, u32[]{:S(2)}, u32[]{:S(2)}) collective-permute-start(bf16[2,48,512]{2,1,0:T(8,128)(2,1)} %get-tuple-element.55), channel_id=1, source_target_pairs={{0,12},{1,13},{2,14},{3,15},{4,8},{5,9},{6,10},{7,11},{8,4},{9,5},... | collective-permute-start | bytes 294920 | tf_op jit(solution)/shard_map/ppermute | solution.py:487
  87.4 17.8 %collective-permute-start.8 = (bf16[2,48,512]{2,1,0:T(8,128)(2,1)}, bf16[2,48,512]{2,1,0:T(8,128)(2,1)S(1)}, u32[]{:S(2)}, u32[]{:S(2)}) collective-permute-start(bf16[2,48,512]{2,1,0:T(8,128)(2,1)} %get-tuple-element.56), channel_id=1, source_target_pairs={{0,14},{1,15},{2,12},{3,13},{4,10},{5,11},{6,8},{7,9},{8,6},{9,7},... | collective-permute-start | bytes 294920 | tf_op jit(solution)/shard_map/ppermute | solution.py:487
  101.6 16.8 %collective-permute-start.23 = (bf16[2,48,512]{2,1,0:T(8,128)(2,1)}, bf16[2,48,512]{2,1,0:T(8,128)(2,1)S(1)}, u32[]{:S(2)}, u32[]{:S(2)}) collective-permute-start(bf16[2,48,512]{2,1,0:T(8,128)(2,1)} %get-tuple-element.82), channel_id=1, source_target_pairs={{0,2},{1,3},{2,0},{3,1},{4,6},{5,7},{6,4},{7,5},{8,10},{9,11},{10,... | collective-permute-start | bytes 294920 | tf_op jit(solution)/shard_map/ppermute | solution.py:487
  101.8 18.4 %collective-permute-start.24 = (bf16[2,48,512]{2,1,0:T(8,128)(2,1)}, bf16[2,48,512]{2,1,0:T(8,128)(2,1)S(1)}, u32[]{:S(2)}, u32[]{:S(2)}) collective-permute-start(bf16[2,48,512]{2,1,0:T(8,128)(2,1)} %get-tuple-element.83), channel_id=1, source_target_pairs={{0,4},{1,5},{2,6},{3,7},{4,0},{5,1},{6,2},{7,3},{8,12},{9,13},{10,... | collective-permute-start | bytes 294920 | tf_op jit(solution)/shard_map/ppermute | solution.py:487
  101.8 21.9 %collective-permute-start.25 = (bf16[2,48,512]{2,1,0:T(8,128)(2,1)}, bf16[2,48,512]{2,1,0:T(8,128)(2,1)S(1)}, u32[]{:S(2)}, u32[]{:S(2)}) collective-permute-start(bf16[2,48,512]{2,1,0:T(8,128)(2,1)} %get-tuple-element.84), channel_id=1, source_target_pairs={{0,6},{1,7},{2,4},{3,5},{4,2},{5,3},{6,0},{7,1},{8,14},{9,15},{10,... | collective-permute-start | bytes 294920 | tf_op jit(solution)/shard_map/ppermute | solution.py:487
  105.2 18.6 %collective-permute-start.26 = (bf16[2,48,512]{2,1,0:T(8,128)(2,1)}, bf16[2,48,512]{2,1,0:T(8,128)(2,1)S(1)}, u32[]{:S(2)}, u32[]{:S(2)}) collective-permute-start(bf16[2,48,512]{2,1,0:T(8,128)(2,1)} %get-tuple-element.85), channel_id=1, source_target_pairs={{0,8},{1,9},{2,10},{3,11},{4,12},{5,13},{6,14},{7,15},{8,0},{9,1},... | collective-permute-start | bytes 294920 | tf_op jit(solution)/shard_map/ppermute | solution.py:487
  105.2 20.1 %collective-permute-start.27 = (bf16[2,48,512]{2,1,0:T(8,128)(2,1)}, bf16[2,48,512]{2,1,0:T(8,128)(2,1)S(1)}, u32[]{:S(2)}, u32[]{:S(2)}) collective-permute-start(bf16[2,48,512]{2,1,0:T(8,128)(2,1)} %get-tuple-element.86), channel_id=1, source_target_pairs={{0,10},{1,11},{2,8},{3,9},{4,14},{5,15},{6,12},{7,13},{8,2},{9,3},... | collective-permute-start | bytes 294920 | tf_op jit(solution)/shard_map/ppermute | solution.py:487
  120.2 10.6 %collective-permute-start.29 = (bf16[2,48,512]{2,1,0:T(8,128)(2,1)S(1)}, bf16[2,48,512]{2,1,0:T(8,128)(2,1)S(1)}, u32[]{:S(2)}, u32[]{:S(2)}) collective-permute-start(bf16[2,48,512]{2,1,0:T(8,128)(2,1)S(1)} %copy-done.18), channel_id=1, source_target_pairs={{0,14},{1,15},{2,12},{3,13},{4,10},{5,11},{6,8},{7,9},{8,6},{9,7},... | collective-permute-start | bytes 294920 | tf_op jit(solution)/shard_map/ppermute | solution.py:487
  123.8 11.4 %collective-permute-start.11 = (bf16[2,48,512]{2,1,0:T(8,128)(2,1)}, bf16[2,48,512]{2,1,0:T(8,128)(2,1)S(1)}, u32[]{:S(2)}, u32[]{:S(2)}) collective-permute-start(bf16[2,48,512]{2,1,0:T(8,128)(2,1)} %get-tuple-element.60), channel_id=1, source_target_pairs={{0,6},{1,7},{2,4},{3,5},{4,2},{5,3},{6,0},{7,1},{8,14},{9,15},{10,... | collective-permute-start | bytes 294920 | tf_op jit(solution)/shard_map/ppermute | solution.py:487
  125.4 13.6 %collective-permute-start.12 = (bf16[2,48,512]{2,1,0:T(8,128)(2,1)}, bf16[2,48,512]{2,1,0:T(8,128)(2,1)S(1)}, u32[]{:S(2)}, u32[]{:S(2)}) collective-permute-start(bf16[2,48,512]{2,1,0:T(8,128)(2,1)} %get-tuple-element.61), channel_id=1, source_target_pairs={{0,8},{1,9},{2,10},{3,11},{4,12},{5,13},{6,14},{7,15},{8,0},{9,1},... | collective-permute-start | bytes 294920 | tf_op jit(solution)/shard_map/ppermute | solution.py:487
  125.8 15.8 %collective-permute-start.13 = (bf16[2,48,512]{2,1,0:T(8,128)(2,1)}, bf16[2,48,512]{2,1,0:T(8,128)(2,1)S(1)}, u32[]{:S(2)}, u32[]{:S(2)}) collective-permute-start(bf16[2,48,512]{2,1,0:T(8,128)(2,1)} %get-tuple-element.62), channel_id=1, source_target_pairs={{0,10},{1,11},{2,8},{3,9},{4,14},{5,15},{6,12},{7,13},{8,2},{9,3},... | collective-permute-start | bytes 294920 | tf_op jit(solution)/shard_map/ppermute | solution.py:487
  130.8 10.7 %collective-permute-start.14 = (bf16[2,48,512]{2,1,0:T(8,128)(2,1)}, bf16[2,48,512]{2,1,0:T(8,128)(2,1)S(1)}, u32[]{:S(2)}, u32[]{:S(2)}) collective-permute-start(bf16[2,48,512]{2,1,0:T(8,128)(2,1)} %get-tuple-element.63), channel_id=1, source_target_pairs={{0,12},{1,13},{2,14},{3,15},{4,8},{5,9},{6,10},{7,11},{8,4},{9,5},... | collective-permute-start | bytes 294920 | tf_op jit(solution)/shard_map/ppermute | solution.py:487
  (45 other events, 414.0 us)

commit v4 on v3

--- a/solution.py
+++ b/solution.py
@@ -12,7 +12,7 @@
 HEAD_DIM = 32
 WIN = 8
 CELLS = WIN * WIN
-CHUNKS = ((2, True), (2, True))
+CHUNKS = ((2, False, True), (2, False, True))
 LANES = 512
 SUB = 256
 VMEM_BYTES = 60 << 20
@@ -273,17 +273,18 @@
     return jnp.concatenate([ref[0] for ref in ins], axis=0)
 
 
-def grid_kernel(split, me_ref, *refs):
-    n = WIN if split else 1
+def grid_kernel(split_in, split_out, me_ref, *refs):
+    n = WIN if split_in else 1
     ins, refs = refs[:n], refs[n:]
     perm_ref, gain_ref, in_ref, out_weight_ref, bias_ref = refs[:5]
+    n = WIN if split_out else 1
     outs, (sent_ref, *scratch) = refs[5 : 5 + n], refs[5 + n :]
 
     @pl.when(pl.program_id(0) == 0)
     def _():
         prepare(in_ref, scratch[0], scratch[1])
 
-    stream = jnp.dot(perm_ref[0], gathered(ins), preferred_element_type=F32)
+    stream = jnp.dot(perm_ref[...], gathered(ins), preferred_element_type=F32)
     result = attend(stream, gain_ref, in_ref, out_weight_ref, bias_ref, scratch)
     channels = result.shape[1]
     result = result.reshape(-1, WIN, WIN, channels)
@@ -294,7 +295,7 @@
 def merge_kernel(split, me_ref, *refs):
     n = WIN if split else 1
     ins, perm_ref, out_ref = refs[:n], refs[n], refs[-1]
-    cells = jnp.dot(perm_ref[0], gathered(ins), preferred_element_type=F32)
+    cells = jnp.dot(perm_ref[...], gathered(ins), preferred_element_type=F32)
     out_ref[...] = cells.reshape(out_ref.shape).astype(BF16)
 
 
@@ -345,34 +346,34 @@
         ),
         out_shape=partner_shapes(split, count, rows, channels),
         cost_estimate=pl.CostEstimate(
-            flops=2 * count * cells * channels * (expanded + 4 * channels) * 4,
-            bytes_accessed=8_000_000,
+            flops=1_000_000,
+            bytes_accessed=100_000,
             transcendentals=0,
         ),
         compiler_params=pltpu.CompilerParams(vmem_limit_bytes=VMEM_BYTES),
     )(me, active, field, parts, up, proj, *params)
 
 
-def grid_stage(split, me, received, perm, params):
+def grid_stage(split_in, split_out, me, received, perm, params):
     count, rows, channels = received[0].shape[-3:]
     cells = WIN * rows
     return pl.pallas_call(
-        functools.partial(grid_kernel, split),
+        functools.partial(grid_kernel, split_in, split_out),
         name="grid_stage",
         grid_spec=pltpu.PrefetchScalarGridSpec(
             num_scalar_prefetch=1,
             grid=(count,),
-            in_specs=partner_specs(split, rows, channels)
-            + [pl.BlockSpec((1, cells, cells), lambda b, me: (me[0], 0, 0))]
+            in_specs=partner_specs(split_in, rows, channels)
+            + [whole((cells, cells))]
             + [whole(p.shape) for p in params],
-            out_specs=partner_specs(split, rows, channels),
+            out_specs=partner_specs(split_out, rows, channels),
             scratch_shapes=[pltpu.VMEM((WIN, rows, channels), BF16)]
             + attention_scratch(cells, channels),
         ),
-        out_shape=partner_shapes(split, count, rows, channels),
+        out_shape=partner_shapes(split_out, count, rows, channels),
         cost_estimate=pl.CostEstimate(
-            flops=2 * count * cells * channels * 4 * channels * 4,
-            bytes_accessed=6_000_000,
+            flops=1_000_000,
+            bytes_accessed=100_000,
             transcendentals=0,
         ),
         compiler_params=pltpu.CompilerParams(vmem_limit_bytes=VMEM_BYTES),
@@ -390,15 +391,15 @@
             num_scalar_prefetch=1,
             grid=(count,),
             in_specs=partner_specs(split, rows, channels)
-            + [pl.BlockSpec((1, cells, cells), lambda b, me: (me[0], 0, 0))]
+            + [whole((cells, cells))]
             + [pl.BlockSpec(memory_space=pl.ANY)] * (merged is not None),
             out_specs=pl.BlockSpec((rows, WIN, channels), lambda b, me: (0, b + start, 0)),
         ),
         out_shape=jax.ShapeDtypeStruct((rows, total * WIN, channels), BF16),
         input_output_aliases={} if merged is None else {n + 2: 0},
         cost_estimate=pl.CostEstimate(
-            flops=2 * count * cells * cells * channels,
-            bytes_accessed=2_000_000,
+            flops=1_000_000,
+            bytes_accessed=100_000,
             transcendentals=0,
         ),
         compiler_params=pltpu.CompilerParams(vmem_limit_bytes=VMEM_BYTES),
@@ -419,16 +420,14 @@
     return gain.reshape(1, -1), in_weight, out_weight, turned_bias(pos_table)
 
 
-def cell_orders(rows):
+def cell_orders(rows, place):
     per = rows // WIN
-    cells = WIN * rows
-    into = np.zeros((WIN, cells, cells), np.float32)
-    back = np.zeros((WIN, cells, cells), np.float32)
-    a, j, i = np.meshgrid(np.arange(per), np.arange(WIN), np.arange(WIN), indexing="ij")
-    for m in range(WIN):
-        into[m, (a * WIN + j) * WIN + i, (m ^ j) * rows + i * per + a] = 1.0
-        back[m, (i * per + a) * WIN + j, (m ^ j) * rows + a * WIN + i] = 1.0
-    return jnp.asarray(into, BF16), jnp.asarray(back, BF16)
+    cells = jnp.arange(WIN * rows)
+    window, col, row = cells // CELLS, cells // WIN % WIN, cells % WIN
+    into = (col ^ place) * rows + row * per + window
+    row, col = cells // WIN, cells % WIN
+    back = (col ^ place) * rows + row % per * WIN + row // per
+    return tuple((source[:, None] == cells[None, :]).astype(BF16) for source in (into, back))
 
 
 def per_device(
@@ -453,6 +452,8 @@
     count = lax.axis_size("lon")
     per = count // WIN
     groups = [[j * per + r for j in range(WIN)] for r in range(per)]
+    total = cols // WIN
+    chunks = CHUNKS if sum(c[0] for c in CHUNKS) == total else ((total, False, False),)
     place = lax.axis_index("lon") // per
     places = {True: place.reshape(1).astype(jnp.int32), False: jnp.zeros((1,), jnp.int32)}
     before = lax.ppermute(
@@ -472,7 +473,9 @@
     )
     parts = lax.all_to_all(part, "lon", 0, 0, tiled=True)
     scale = ROOT_HALF / (rows * cols * count)
-    into, back = cell_orders(rows)
+    into, back = {}, {}
+    for split in sorted({split for _, *both in chunks for split in both}):
+        into[split], back[split] = cell_orders(rows, places[split][0])
     block_params = attention_params(block_gain, block_in_weight, block_out_weight, block_table)
     grid_params = attention_params(grid_gain, grid_in_weight, grid_out_weight, grid_table)
 
@@ -492,27 +495,27 @@
             for s in range(1, WIN)
         ]
 
-    total = cols // WIN
-    chunks = CHUNKS if sum(c[0] for c in CHUNKS) == total else ((total, False),)
     starts = [sum(c[0] for c in chunks[:k]) for k in range(len(chunks))]
     sent = [
         block_stage(
             split, start, size, scale, places[split], active, field, parts, squeeze_up,
             project_weight, block_params,
         )
-        for start, (size, split) in zip(starts, chunks)
+        for start, (size, split, _) in zip(starts, chunks)
     ]
-    received = [exchange(split, pieces) for pieces, (_, split) in zip(sent, chunks)]
+    received = [exchange(split, pieces) for pieces, (_, split, _) in zip(sent, chunks)]
     results = []
-    for k, (_, split) in enumerate(chunks):
+    for k, (_, split, returned) in enumerate(chunks):
         pieces = received[k]
         if k + 1 < len(chunks):
-            pieces, _ = lax.optimization_barrier((pieces, sent[k + 1][0]))
-        results.append(grid_stage(split, places[split], pieces, into, grid_params))
+            later = sent[k + 1][0]
+            pieces, _ = lax.optimization_barrier((pieces, later))
+        me = places[split or returned]
+        results.append(grid_stage(split, returned, me, pieces, into[split], grid_params))
     merged = None
-    for start, result, (_, split) in zip(starts, results, chunks):
+    for start, result, (_, _, split) in zip(starts, results, chunks):
         merged = merge_stage(
-            split, start, total, places[split], exchange(split, result), back, merged
+            split, start, total, places[split], exchange(split, result), back[split], merged
         )
     return merged
 

time: 146 us -> 142 us (0.973)
  starting transfers between devices: 57.3 us -> 40.6 us
  waiting for transfers between devices: 8.12 us -> 19.2 us
  other arithmetic: 0.09 us -> 1.77 us
    ppermute x28 -> x14, starting transfers between devices: 46 us -> 21.9 us  [exchange(): lax.ppermute(pieces[s], 'lon', [(j * per + r, (j ^ s) * per + r) for j in...]
    all_to_all x0 -> x2, starting transfers between devices: none -> 7.29 us  [exchange(): lax.all_to_all(pieces[0], 'lon', 0, 0, axis_index_groups=groups, tiled=True)]
    all_to_all x0 -> x2, waiting for transfers between devices: none -> 6.56 us  [exchange(): lax.all_to_all(pieces[0], 'lon', 0, 0, axis_index_groups=groups, tiled=True)]
    ppermute x28 -> x14, waiting for transfers between devices: 3.04 us -> 7.58 us  [exchange(): lax.ppermute(pieces[s], 'lon', [(j * per + r, (j ^ s) * per + r) for j in...]
    convert_element_type x0 -> x2, other arithmetic: none -> 1.66 us  [cell_orders(): (source[:, None] == cells[None, :]).astype(BF16)]
    unnamed x77 -> x49, local copies, waits for them, and re-layouts: 4.27 us -> 5.16 us
  transfers between devices with their start and end apart: 31 -> 19, of which waited for: 5 -> 7; matrix products, arithmetic and copies ran while one was open for 5% -> 6% of each run, Pallas kernels for 26% -> 26%
where the time goes in v4:
time: 142 us
  Pallas kernels  67.6 us (48%)
  starting transfers between devices  40.6 us (29%)
  waiting for transfers between devices  19.2 us (14%)
  local copies, waits for them, and re-layouts  6.95 us (5%)
  matrix products  5.24 us (4%)
  other arithmetic  1.77 us (1%)
    pallas_call x2, Pallas kernels, block_stage(): pl.pallas_call(functools.partial(block_kernel, scale, split), name='block...  26.6 us
    ppermute x14, starting transfers between devices, exchange(): lax.ppermute(pieces[s], 'lon', [(j * per + r, (j ^ s) * per + r) for j in...  21.9 us
    pallas_call x2, Pallas kernels, grid_stage(): pl.pallas_call(functools.partial(grid_kernel, split_in, split_out), name=...  20.9 us
    pallas_call x1, Pallas kernels, mbconv(): pl.pallas_call(mbconv_kernel, name='mbconv', grid=(expanded // LANES,), i...  14.6 us
    ppermute x14, waiting for transfers between devices, exchange(): lax.ppermute(pieces[s], 'lon', [(j * per + r, (j ^ s) * per + r) for j in...  7.58 us
    all_to_all x2, starting transfers between devices, exchange(): lax.all_to_all(pieces[0], 'lon', 0, 0, axis_index_groups=groups, tiled=True)  7.29 us
    all_to_all x2, waiting for transfers between devices, exchange(): lax.all_to_all(pieces[0], 'lon', 0, 0, axis_index_groups=groups, tiled=True)  6.56 us
    all_to_all x1, starting transfers between devices, per_device(): parts = lax.all_to_all(part, 'lon', 0, 0, tiled=True)  5.78 us
  transfers between devices with their start and end apart: 19, of which 7 were waited for; matrix products, arithmetic and copies ran while one was open for 6% of the time, Pallas kernels for 26%

profile of v4, /device:TPU:0, one launch (start us, length us, event | category | flops | bytes accessed | tf_op | source)
XLA Modules:
  0.0 141.6 jit_solution(17926420982071124089)
XLA Ops:
  0.0 2.3 %copy.24 = bf16[48,32,512]{2,0,1:T(8,128)(2,1)S(1)} copy(bf16[48,32,512]{2,1,0:T(8,128)(2,1)} %param.17) | data formatting | bytes 3145728 | tf_op args[0]
  2.8 5.1 %collective-permute-start.1 = (bf16[1,48,512]{2,1,0:T(8,128)(2,1)S(1)}, bf16[1,48,512]{2,1,0:T(8,128)(2,1)S(1)}, u32[]{:S(2)}, u32[]{:S(2)}) collective-permute-start(bf16[1,48,512]{2,1,0:T(8,128)(2,1)S(1)} %get-tuple-element.43), channel_id=1, source_target_pairs={{1,0},{2,1},{3,2},{4,3},{5,4},{6,5},{7,6},{8,7},{9,8},{10,9},{11,1... | collective-permute-start | bytes 147464 | tf_op jit(solution)/shard_map/ppermute | solution.py:464
  10.3 14.6 %mbconv.1 = (bf16[32,48,2048]{2,1,0:T(8,128)(2,1)}, f32[16,8,128]{2,1,0:T(8,128)}) custom-call(bf16[32,48,512]{2,1,0:T(8,128)(2,1)} %bitcast.21, bf16[1,48,512]{2,1,0:T(8,128)(2,1)} %copy-done.20, bf16[1,48,512]{2,1,0:T(8,128)(2,1)} %copy-done.21, bf16[512,2048]{1,0:T(8,128)(2,1)} %w_ref.1, f32[1,2048]{1,0:T(1,128)} %bitcast.28, f32[9,2048]{1,0:T(8,128)} %dw_ref.1, ...), custom_call_target="tpu_custom_call" | custom-call | flops 12884901888 | bytes 20000000 | tf_op jit(solution)/shard_map/mbconv/pallas_call | solution.py:113
  24.9 5.8 %all-to-all-start = ((f32[16,8,128]{2,1,0:T(8,128)}), f32[16,8,128]{2,1,0:T(8,128)S(1)}, u32[]{:S(2)}, u32[]{:S(2)}) async-start(f32[16,8,128]{2,1,0:T(8,128)} %get-tuple-element.25), calls=%async_computation | async-start | bytes 131072 | tf_op jit(solution)/shard_map/all_to_all | solution.py:474
  30.7 2.6 %fusion.4 = f32[64,16,64]{2,1,0:T(8,128)S(1)} fusion(s32[64,64]{1,0:T(8,128)S(1)} %add_add_fusion, f32[225,16]{0,1:T(8,128)S(1)} %copy-done.22), kind=kOutput, calls=%fused_computation.5 | convolution fusion | flops 177872400 | bytes 292928 | tf_op jit(solution)/shard_map/jir,rh->jhi/dot_general | solution.py:415
  34.2 3.4 %all-to-all-done.part_ref = f32[16,8,128]{2,1,0:T(8,128)S(1)} async-done(((f32[16,8,128]{2,1,0:T(8,128)}), f32[16,8,128]{2,1,0:T(8,128)S(1)}, u32[]{:S(2)}, u32[]{:S(2)}) %all-to-all-start) | async-done | bytes 65568 | tf_op jit(solution)/shard_map/all_to_all | solution.py:474
  38.2 13.2 %block_stage.3 = bf16[8,2,48,512]{3,2,1,0:T(8,128)(2,1)} custom-call(s32[1]{0:T(128)} %constant.116.clone.1.me_ref, bf16[32,48,2048]{2,1,0:T(8,128)(2,1)} %get-tuple-element.24.act_ref, bf16[32,48,512]{2,1,0:T(8,128)(2,1)} %bitcast.22, f32[16,8,128]{2,1,0:T(8,128)} %copy-done.3, bf16[128,2048]{1,0:T(8,128)(2,1)} %up_ref.3, bf16[2048,512]{1,0:T(8,128)(2,1)} %proj_ref.3, ...), custom_call_target="tpu_custom_call" | custom-call | flops 1000000 | bytes 100000 | tf_op jit(solution)/shard_map/block_stage/pallas_call | solution.py:329
  51.4 3.7 %all-to-all-start.2 = ((bf16[8,2,48,512]{3,2,1,0:T(8,128)(2,1)}), bf16[8,2,48,512]{3,2,1,0:T(8,128)(2,1)S(1)}, u32[]{:S(2)}, u32[]{:S(2)}) async-start(bf16[8,2,48,512]{3,2,1,0:T(8,128)(2,1)} %block_stage.3), calls=%async_computation.2 | async-start | bytes 1572864 | tf_op jit(solution)/shard_map/all_to_all | solution.py:485
  55.2 13.3 %block_stage.2 = bf16[8,2,48,512]{3,2,1,0:T(8,128)(2,1)} custom-call(s32[1]{0:T(128)} %constant.116.clone.1.me_ref, bf16[32,48,2048]{2,1,0:T(8,128)(2,1)} %get-tuple-element.24.act_ref, bf16[32,48,512]{2,1,0:T(8,128)(2,1)} %bitcast.23, f32[16,8,128]{2,1,0:T(8,128)} %copy-done.3, bf16[128,2048]{1,0:T(8,128)(2,1)} %up_ref.3, bf16[2048,512]{1,0:T(8,128)(2,1)} %proj_ref.3, ...), custom_call_target="tpu_custom_call" | custom-call | flops 1000000 | bytes 100000 | tf_op jit(solution)/shard_map/block_stage/pallas_call | solution.py:329
  68.5 6.6 %all-to-all-done.2.refs_0_ = bf16[8,2,48,512]{3,2,1,0:T(8,128)(2,1)S(1)} async-done(((bf16[8,2,48,512]{3,2,1,0:T(8,128)(2,1)}), bf16[8,2,48,512]{3,2,1,0:T(8,128)(2,1)S(1)}, u32[]{:S(2)}, u32[]{:S(2)}) %all-to-all-start.2) | async-done | bytes 786464 | tf_op jit(solution)/shard_map/all_to_all | solution.py:485
  75.1 3.6 %all-to-all-start.1 = ((bf16[8,2,48,512]{3,2,1,0:T(8,128)(2,1)}), bf16[8,2,48,512]{3,2,1,0:T(8,128)(2,1)S(1)}, u32[]{:S(2)}, u32[]{:S(2)}) async-start(bf16[8,2,48,512]{3,2,1,0:T(8,128)(2,1)} %block_stage.2), calls=%async_computation.1 | async-start | bytes 1572864 | tf_op jit(solution)/shard_map/all_to_all | solution.py:485
  78.6 2.6 %fusion.5 = f32[64,16,64]{2,1,0:T(8,128)S(1)} fusion(s32[64,64]{1,0:T(8,128)S(1)} %add_add_fusion, f32[225,16]{0,1:T(8,128)S(1)} %copy-done.23), kind=kOutput, calls=%fused_computation.6 | convolution fusion | flops 177872400 | bytes 292928 | tf_op jit(solution)/shard_map/jir,rh->jhi/dot_general | solution.py:415
  83.0 10.5 %grid_stage.3 = (bf16[2,48,512]{2,1,0:T(8,128)(2,1)}, bf16[2,48,512]{2,1,0:T(8,128)(2,1)}, bf16[2,48,512]{2,1,0:T(8,128)(2,1)}, bf16[2,48,512]{2,1,0:T(8,128)(2,...) custom-call(s32[1]{0:T(128)} %bitcast.me_ref, ...), custom_call_target="tpu_custom_call" | custom-call | flops 1000000 | bytes 100000 | tf_op jit(solution)/shard_map/grid_stage/pallas_call | solution.py:360
  93.5 2.1 %collective-permute-start.10 = (bf16[2,48,512]{2,1,0:T(8,128)(2,1)}, bf16[2,48,512]{2,1,0:T(8,128)(2,1)S(1)}, u32[]{:S(2)}, u32[]{:S(2)}) collective-permute-start(bf16[2,48,512]{2,1,0:T(8,128)(2,1)} %get-tuple-element.37), channel_id=1, source_target_pairs={{0,4},{1,5},{2,6},{3,7},{4,0},{5,1},{6,2},{7,3},{8,12},{9,13},{10,... | collective-permute-start | bytes 294920 | tf_op jit(solution)/shard_map/ppermute | solution.py:490
  97.0 2.4 %collective-permute-start.12 = (bf16[2,48,512]{2,1,0:T(8,128)(2,1)}, bf16[2,48,512]{2,1,0:T(8,128)(2,1)S(1)}, u32[]{:S(2)}, u32[]{:S(2)}) collective-permute-start(bf16[2,48,512]{2,1,0:T(8,128)(2,1)} %get-tuple-element.39), channel_id=1, source_target_pairs={{0,8},{1,9},{2,10},{3,11},{4,12},{5,13},{6,14},{7,15},{8,0},{9,1},... | collective-permute-start | bytes 294920 | tf_op jit(solution)/shard_map/ppermute | solution.py:490
  99.5 3.7 %collective-permute-start.14 = (bf16[2,48,512]{2,1,0:T(8,128)(2,1)}, bf16[2,48,512]{2,1,0:T(8,128)(2,1)S(1)}, u32[]{:S(2)}, u32[]{:S(2)}) collective-permute-start(bf16[2,48,512]{2,1,0:T(8,128)(2,1)} %get-tuple-element.41), channel_id=1, source_target_pairs={{0,12},{1,13},{2,14},{3,15},{4,8},{5,9},{6,10},{7,11},{8,4},{9,5},... | collective-permute-start | bytes 294920 | tf_op jit(solution)/shard_map/ppermute | solution.py:490
  104.1 10.5 %grid_stage.2 = (bf16[2,48,512]{2,1,0:T(8,128)(2,1)}, bf16[2,48,512]{2,1,0:T(8,128)(2,1)}, bf16[2,48,512]{2,1,0:T(8,128)(2,1)}, bf16[2,48,512]{2,1,0:T(8,128)(2,...) custom-call(s32[1]{0:T(128)} %bitcast.me_ref, ...), custom_call_target="tpu_custom_call" | custom-call | flops 1000000 | bytes 100000 | tf_op jit(solution)/shard_map/grid_stage/pallas_call | solution.py:360
  116.3 1.9 %collective-permute-start.2 = (bf16[2,48,512]{2,1,0:T(8,128)(2,1)}, bf16[2,48,512]{2,1,0:T(8,128)(2,1)S(1)}, u32[]{:S(2)}, u32[]{:S(2)}) collective-permute-start(bf16[2,48,512]{2,1,0:T(8,128)(2,1)} %get-tuple-element.27), channel_id=1, source_target_pairs={{0,2},{1,3},{2,0},{3,1},{4,6},{5,7},{6,4},{7,5},{8,10},{9,11},{10,... | collective-permute-start | bytes 294920 | tf_op jit(solution)/shard_map/ppermute | solution.py:490
  119.9 2.3 %collective-permute-done.15.refs_7_ = bf16[2,48,512]{2,1,0:T(8,128)(2,1)S(1)} collective-permute-done((bf16[2,48,512]{2,1,0:T(8,128)(2,1)S(1)}, bf16[2,48,512]{2,1,0:T(8,128)(2,1)S(1)}, u32[]{:S(2)}, u32[]{:S(2)}) %collective-permute-start.15) | collective-permute-done | bytes 98336 | tf_op jit(solution)/shard_map/ppermute | solution.py:490
  122.9 3.6 %collective-permute-start.6 = (bf16[2,48,512]{2,1,0:T(8,128)(2,1)}, bf16[2,48,512]{2,1,0:T(8,128)(2,1)S(1)}, u32[]{:S(2)}, u32[]{:S(2)}) collective-permute-start(bf16[2,48,512]{2,1,0:T(8,128)(2,1)} %get-tuple-element.31), channel_id=1, source_target_pairs={{0,10},{1,11},{2,8},{3,9},{4,14},{5,15},{6,12},{7,13},{8,2},{9,3},... | collective-permute-start | bytes 294920 | tf_op jit(solution)/shard_map/ppermute | solution.py:490
  127.4 2.4 %collective-permute-start.8 = (bf16[2,48,512]{2,1,0:T(8,128)(2,1)}, bf16[2,48,512]{2,1,0:T(8,128)(2,1)S(1)}, u32[]{:S(2)}, u32[]{:S(2)}) collective-permute-start(bf16[2,48,512]{2,1,0:T(8,128)(2,1)} %get-tuple-element.33), channel_id=1, source_target_pairs={{0,14},{1,15},{2,12},{3,13},{4,10},{5,11},{6,8},{7,9},{8,6},{9,7},... | collective-permute-start | bytes 294920 | tf_op jit(solution)/shard_map/ppermute | solution.py:490
  130.7 2.8 %merge_stage.2.refs_9_ = bf16[48,32,512]{2,1,0:T(8,128)(2,1)} custom-call(s32[1]{0:T(128)} %bitcast.me_ref, bf16[2,48,512]{2,1,0:T(8,128)(2,1)} %get-tuple-element.35.refs_0_, bf16[2,48,512]{2,1,0:T(8,128)(2,1)} %copy-done.10, bf16[2,48,512]{2,1,0:T(8,128)(2,1)} %copy-done.4, bf16[2,48,512]{2,1,0:T(8,128)(2,1)} %copy-done.5, bf16[2,48,512]{2,1,0:T(8,128)(2,1)} %copy-done.6, ...), custom_call_target="tpu_custom_call" | custom-call | flops 1000000 | bytes 100000 | tf_op jit(solution)/shard_map/merge_stage/pallas_call | solution.py:387
  135.4 2.7 %collective-permute-done.6.refs_5_ = bf16[2,48,512]{2,1,0:T(8,128)(2,1)S(1)} collective-permute-done((bf16[2,48,512]{2,1,0:T(8,128)(2,1)}, bf16[2,48,512]{2,1,0:T(8,128)(2,1)S(1)}, u32[]{:S(2)}, u32[]{:S(2)}) %collective-permute-start.6) | collective-permute-done | bytes 98336 | tf_op jit(solution)/shard_map/ppermute | solution.py:490
  138.8 2.8 %merge_stage.3 = bf16[48,32,512]{2,1,0:T(8,128)(2,1)} custom-call(s32[1]{0:T(128)} %bitcast.me_ref, bf16[2,48,512]{2,1,0:T(8,128)(2,1)} %get-tuple-element.26.refs_0_, bf16[2,48,512]{2,1,0:T(8,128)(2,1)} %copy-done.11, bf16[2,48,512]{2,1,0:T(8,128)(2,1)} %copy-done.12, bf16[2,48,512]{2,1,0:T(8,128)(2,1)} %copy-done.13, ...), custom_call_target="tpu_custom_call", output_to_operand_aliasing={{}: (10, {})} | custom-call | flops 1000000 | bytes 100000 | tf_op jit(solution)/shard_map/merge_stage/pallas_call | solution.py:387
  (81 shorter events, 17.0 us)
Async XLA Ops:
  2.3 7.4 %collective-permute-start = (bf16[1,48,512]{2,1,0:T(8,128)(2,1)S(1)}, bf16[1,48,512]{2,1,0:T(8,128)(2,1)S(1)}, u32[]{:S(2)}, u32[]{:S(2)}) collective-permute-start(bf16[1,48,512]{2,1,0:T(8,128)(2,1)S(1)} %get-tuple-element.44), channel_id=1, source_target_pairs={{0,1},{1,2},{2,3},{3,4},{4,5},{5,6},{6,7},{7,8},{8,9},{9,10},{10,1... | collective-permute-start | bytes 147464 | tf_op jit(solution)/shard_map/ppermute | solution.py:459
  2.8 6.9 %collective-permute-start.1 = (bf16[1,48,512]{2,1,0:T(8,128)(2,1)S(1)}, bf16[1,48,512]{2,1,0:T(8,128)(2,1)S(1)}, u32[]{:S(2)}, u32[]{:S(2)}) collective-permute-start(bf16[1,48,512]{2,1,0:T(8,128)(2,1)S(1)} %get-tuple-element.43), channel_id=1, source_target_pairs={{1,0},{2,1},{3,2},{4,3},{5,4},{6,5},{7,6},{8,7},{9,8},{10,9},{11,1... | collective-permute-start | bytes 147464 | tf_op jit(solution)/shard_map/ppermute | solution.py:464
  10.3 20.3 %copy-start.22 = (f32[225,16]{0,1:T(8,128)S(1)}, f32[225,16]{0,1:T(8,128)}, u32[]{:S(2)}) copy-start(f32[225,16]{0,1:T(8,128)} %param.28) | copy-start | bytes 43204
  24.9 12.7 %all-to-all-start = ((f32[16,8,128]{2,1,0:T(8,128)}), f32[16,8,128]{2,1,0:T(8,128)S(1)}, u32[]{:S(2)}, u32[]{:S(2)}) async-start(f32[16,8,128]{2,1,0:T(8,128)} %get-tuple-element.25), calls=%async_computation | async-start | bytes 131072 | tf_op jit(solution)/shard_map/all_to_all | solution.py:474
  51.4 23.6 %all-to-all-start.2 = ((bf16[8,2,48,512]{3,2,1,0:T(8,128)(2,1)}), bf16[8,2,48,512]{3,2,1,0:T(8,128)(2,1)S(1)}, u32[]{:S(2)}, u32[]{:S(2)}) async-start(bf16[8,2,48,512]{3,2,1,0:T(8,128)(2,1)} %block_stage.3), calls=%async_computation.2 | async-start | bytes 1572864 | tf_op jit(solution)/shard_map/all_to_all | solution.py:485
  55.2 23.5 %copy-start.23 = (f32[225,16]{0,1:T(8,128)S(1)}, f32[225,16]{0,1:T(8,128)}, u32[]{:S(2)}) copy-start(f32[225,16]{0,1:T(8,128)} %param.32) | copy-start | bytes 43204
  75.1 28.1 %all-to-all-start.1 = ((bf16[8,2,48,512]{3,2,1,0:T(8,128)(2,1)}), bf16[8,2,48,512]{3,2,1,0:T(8,128)(2,1)S(1)}, u32[]{:S(2)}, u32[]{:S(2)}) async-start(bf16[8,2,48,512]{3,2,1,0:T(8,128)(2,1)} %block_stage.2), calls=%async_computation.1 | async-start | bytes 1572864 | tf_op jit(solution)/shard_map/all_to_all | solution.py:485
  93.4 21.1 %copy-start.19 = (bf16[2,48,512]{2,1,0:T(8,128)(2,1)S(1)}, bf16[2,48,512]{2,1,0:T(8,128)(2,1)}, u32[]{:S(2)}) copy-start(bf16[2,48,512]{2,1,0:T(8,128)(2,1)} %get-tuple-element.42) | copy-start | bytes 294916
  93.5 22.7 %copy-start.18 = (bf16[2,48,512]{2,1,0:T(8,128)(2,1)S(1)}, bf16[2,48,512]{2,1,0:T(8,128)(2,1)}, u32[]{:S(2)}) copy-start(bf16[2,48,512]{2,1,0:T(8,128)(2,1)} %get-tuple-element.36) | copy-start | bytes 294916
  93.5 21.1 %collective-permute-start.10 = (bf16[2,48,512]{2,1,0:T(8,128)(2,1)}, bf16[2,48,512]{2,1,0:T(8,128)(2,1)S(1)}, u32[]{:S(2)}, u32[]{:S(2)}) collective-permute-start(bf16[2,48,512]{2,1,0:T(8,128)(2,1)} %get-tuple-element.37), channel_id=1, source_target_pairs={{0,4},{1,5},{2,6},{3,7},{4,0},{5,1},{6,2},{7,3},{8,12},{9,13},{10,... | collective-permute-start | bytes 294920 | tf_op jit(solution)/shard_map/ppermute | solution.py:490
  95.6 20.6 %collective-permute-start.11 = (bf16[2,48,512]{2,1,0:T(8,128)(2,1)}, bf16[2,48,512]{2,1,0:T(8,128)(2,1)S(1)}, u32[]{:S(2)}, u32[]{:S(2)}) collective-permute-start(bf16[2,48,512]{2,1,0:T(8,128)(2,1)} %get-tuple-element.38), channel_id=1, source_target_pairs={{0,6},{1,7},{2,4},{3,5},{4,2},{5,3},{6,0},{7,1},{8,14},{9,15},{10,... | collective-permute-start | bytes 294920 | tf_op jit(solution)/shard_map/ppermute | solution.py:490
  97.0 19.2 %collective-permute-start.12 = (bf16[2,48,512]{2,1,0:T(8,128)(2,1)}, bf16[2,48,512]{2,1,0:T(8,128)(2,1)S(1)}, u32[]{:S(2)}, u32[]{:S(2)}) collective-permute-start(bf16[2,48,512]{2,1,0:T(8,128)(2,1)} %get-tuple-element.39), channel_id=1, source_target_pairs={{0,8},{1,9},{2,10},{3,11},{4,12},{5,13},{6,14},{7,15},{8,0},{9,1},... | collective-permute-start | bytes 294920 | tf_op jit(solution)/shard_map/ppermute | solution.py:490
  99.4 18.8 %collective-permute-start.13 = (bf16[2,48,512]{2,1,0:T(8,128)(2,1)}, bf16[2,48,512]{2,1,0:T(8,128)(2,1)S(1)}, u32[]{:S(2)}, u32[]{:S(2)}) collective-permute-start(bf16[2,48,512]{2,1,0:T(8,128)(2,1)} %get-tuple-element.40), channel_id=1, source_target_pairs={{0,10},{1,11},{2,8},{3,9},{4,14},{5,15},{6,12},{7,13},{8,2},{9,3},... | collective-permute-start | bytes 294920 | tf_op jit(solution)/shard_map/ppermute | solution.py:490
  99.5 18.8 %collective-permute-start.14 = (bf16[2,48,512]{2,1,0:T(8,128)(2,1)}, bf16[2,48,512]{2,1,0:T(8,128)(2,1)S(1)}, u32[]{:S(2)}, u32[]{:S(2)}) collective-permute-start(bf16[2,48,512]{2,1,0:T(8,128)(2,1)} %get-tuple-element.41), channel_id=1, source_target_pairs={{0,12},{1,13},{2,14},{3,15},{4,8},{5,9},{6,10},{7,11},{8,4},{9,5},... | collective-permute-start | bytes 294920 | tf_op jit(solution)/shard_map/ppermute | solution.py:490
  114.6 16.1 %copy-start.4 = (bf16[2,48,512]{2,1,0:T(8,128)(2,1)}, bf16[2,48,512]{2,1,0:T(8,128)(2,1)S(1)}, u32[]{:S(2)}) copy-start(bf16[2,48,512]{2,1,0:T(8,128)(2,1)S(1)} %collective-permute-done.10.refs_2_) | copy-start | bytes 294916
  114.6 7.6 %collective-permute-start.15 = (bf16[2,48,512]{2,1,0:T(8,128)(2,1)S(1)}, bf16[2,48,512]{2,1,0:T(8,128)(2,1)S(1)}, u32[]{:S(2)}, u32[]{:S(2)}) collective-permute-start(bf16[2,48,512]{2,1,0:T(8,128)(2,1)S(1)} %copy-done.19), channel_id=1, source_target_pairs={{0,14},{1,15},{2,12},{3,13},{4,10},{5,11},{6,8},{7,9},{8,6},{9,7},... | collective-permute-start | bytes 294920 | tf_op jit(solution)/shard_map/ppermute | solution.py:490
  116.1 6.8 %collective-permute-start.9 = (bf16[2,48,512]{2,1,0:T(8,128)(2,1)S(1)}, bf16[2,48,512]{2,1,0:T(8,128)(2,1)S(1)}, u32[]{:S(2)}, u32[]{:S(2)}) collective-permute-start(bf16[2,48,512]{2,1,0:T(8,128)(2,1)S(1)} %copy-done.18), channel_id=1, source_target_pairs={{0,2},{1,3},{2,0},{3,1},{4,6},{5,7},{6,4},{7,5},{8,10},{9,11},{10,... | collective-permute-start | bytes 294920 | tf_op jit(solution)/shard_map/ppermute | solution.py:490
  116.3 10.3 %collective-permute-start.2 = (bf16[2,48,512]{2,1,0:T(8,128)(2,1)}, bf16[2,48,512]{2,1,0:T(8,128)(2,1)S(1)}, u32[]{:S(2)}, u32[]{:S(2)}) collective-permute-start(bf16[2,48,512]{2,1,0:T(8,128)(2,1)} %get-tuple-element.27), channel_id=1, source_target_pairs={{0,2},{1,3},{2,0},{3,1},{4,6},{5,7},{6,4},{7,5},{8,10},{9,11},{10,... | collective-permute-start | bytes 294920 | tf_op jit(solution)/shard_map/ppermute | solution.py:490
  118.2 9.2 %collective-permute-start.3 = (bf16[2,48,512]{2,1,0:T(8,128)(2,1)}, bf16[2,48,512]{2,1,0:T(8,128)(2,1)S(1)}, u32[]{:S(2)}, u32[]{:S(2)}) collective-permute-start(bf16[2,48,512]{2,1,0:T(8,128)(2,1)} %get-tuple-element.28), channel_id=1, source_target_pairs={{0,4},{1,5},{2,6},{3,7},{4,0},{5,1},{6,2},{7,3},{8,12},{9,13},{10,... | collective-permute-start | bytes 294920 | tf_op jit(solution)/shard_map/ppermute | solution.py:490
  118.3 15.2 %collective-permute-start.4 = (bf16[2,48,512]{2,1,0:T(8,128)(2,1)}, bf16[2,48,512]{2,1,0:T(8,128)(2,1)S(1)}, u32[]{:S(2)}, u32[]{:S(2)}) collective-permute-start(bf16[2,48,512]{2,1,0:T(8,128)(2,1)} %get-tuple-element.29), channel_id=1, source_target_pairs={{0,6},{1,7},{2,4},{3,5},{4,2},{5,3},{6,0},{7,1},{8,14},{9,15},{10,... | collective-permute-start | bytes 294920 | tf_op jit(solution)/shard_map/ppermute | solution.py:490
  122.2 13.2 %collective-permute-start.5 = (bf16[2,48,512]{2,1,0:T(8,128)(2,1)}, bf16[2,48,512]{2,1,0:T(8,128)(2,1)S(1)}, u32[]{:S(2)}, u32[]{:S(2)}) collective-permute-start(bf16[2,48,512]{2,1,0:T(8,128)(2,1)} %get-tuple-element.30), channel_id=1, source_target_pairs={{0,8},{1,9},{2,10},{3,11},{4,12},{5,13},{6,14},{7,15},{8,0},{9,1},... | collective-permute-start | bytes 294920 | tf_op jit(solution)/shard_map/ppermute | solution.py:490
  122.9 15.2 %collective-permute-start.6 = (bf16[2,48,512]{2,1,0:T(8,128)(2,1)}, bf16[2,48,512]{2,1,0:T(8,128)(2,1)S(1)}, u32[]{:S(2)}, u32[]{:S(2)}) collective-permute-start(bf16[2,48,512]{2,1,0:T(8,128)(2,1)} %get-tuple-element.31), channel_id=1, source_target_pairs={{0,10},{1,11},{2,8},{3,9},{4,14},{5,15},{6,12},{7,13},{8,2},{9,3},... | collective-permute-start | bytes 294920 | tf_op jit(solution)/shard_map/ppermute | solution.py:490
  126.5 11.6 %collective-permute-start.7 = (bf16[2,48,512]{2,1,0:T(8,128)(2,1)}, bf16[2,48,512]{2,1,0:T(8,128)(2,1)S(1)}, u32[]{:S(2)}, u32[]{:S(2)}) collective-permute-start(bf16[2,48,512]{2,1,0:T(8,128)(2,1)} %get-tuple-element.32), channel_id=1, source_target_pairs={{0,12},{1,13},{2,14},{3,15},{4,8},{5,9},{6,10},{7,11},{8,4},{9,5},... | collective-permute-start | bytes 294920 | tf_op jit(solution)/shard_map/ppermute | solution.py:490
  127.4 10.7 %collective-permute-start.8 = (bf16[2,48,512]{2,1,0:T(8,128)(2,1)}, bf16[2,48,512]{2,1,0:T(8,128)(2,1)S(1)}, u32[]{:S(2)}, u32[]{:S(2)}) collective-permute-start(bf16[2,48,512]{2,1,0:T(8,128)(2,1)} %get-tuple-element.33), channel_id=1, source_target_pairs={{0,14},{1,15},{2,12},{3,13},{4,10},{5,11},{6,8},{7,9},{8,6},{9,7},... | collective-permute-start | bytes 294920 | tf_op jit(solution)/shard_map/ppermute | solution.py:490
  (19 other events, 120.1 us)

commit v5 on v4

--- a/solution.py
+++ b/solution.py
@@ -456,13 +456,14 @@
     chunks = CHUNKS if sum(c[0] for c in CHUNKS) == total else ((total, False, False),)
     place = lax.axis_index("lon") // per
     places = {True: place.reshape(1).astype(jnp.int32), False: jnp.zeros((1,), jnp.int32)}
+    edges = lax.optimization_barrier(input_field)
     before = lax.ppermute(
-        jnp.swapaxes(input_field[:, -1:], 0, 1),
+        jnp.swapaxes(edges[:, -1:], 0, 1),
         "lon",
         [(i, (i + 1) % count) for i in range(count)],
     )
     after = lax.ppermute(
-        jnp.swapaxes(input_field[:, :1], 0, 1),
+        jnp.swapaxes(edges[:, :1], 0, 1),
         "lon",
         [((i + 1) % count, i) for i in range(count)],
     )
@@ -503,6 +504,10 @@
         )
         for start, (size, split, _) in zip(starts, chunks)
     ]
+    if len(chunks) > 1:
+        sent[1], grid_params, into, back = lax.optimization_barrier(
+            (sent[1], grid_params, into, back)
+        )
     received = [exchange(split, pieces) for pieces, (_, split, _) in zip(sent, chunks)]
     results = []
     for k, (_, split, returned) in enumerate(chunks):

time: 142 us -> 141 us (level)
  local copies, waits for them, and re-layouts: 6.95 us -> 9.38 us
  waiting for transfers between devices: 19.2 us -> 17.6 us
    all_to_all x2, waiting for transfers between devices: 6.56 us -> 9.38 us  [exchange(): lax.all_to_all(pieces[0], 'lon', 0, 0, axis_index_groups=groups, tiled=True)]
    ppermute x14, waiting for transfers between devices: 7.58 us -> 4.79 us  [exchange(): lax.ppermute(pieces[s], 'lon', [(j * per + r, (j ^ s) * per + r) for j in...]
    all_to_all x1, starting transfers between devices: 5.78 us -> 4.05 us  [per_device(): parts = lax.all_to_all(part, 'lon', 0, 0, tiled=True)]
    ppermute x2, waiting for transfers between devices: 1.7 us -> 0.01 us  [the longest x1 0.01 us: per_device(): lax.ppermute(jnp.swapaxes(edges[:, -1:], 0, 1), 'lon', [(i, (i + 1) % cou...]
  transfers between devices with their start and end apart: 19 -> 19, of which waited for: 7 -> 6; matrix products, arithmetic and copies ran while one was open for 6% -> 8% of each run, Pallas kernels for 26% -> 26%
where the time goes in v5:
time: 141 us
  Pallas kernels  67.6 us (48%)
  starting transfers between devices  39.3 us (28%)
  waiting for transfers between devices  17.6 us (12%)
  local copies, waits for them, and re-layouts  9.38 us (7%)
  matrix products  5.24 us (4%)
    pallas_call x2, Pallas kernels, block_stage(): pl.pallas_call(functools.partial(block_kernel, scale, split), name='block...  26.5 us
    ppermute x14, starting transfers between devices, exchange(): lax.ppermute(pieces[s], 'lon', [(j * per + r, (j ^ s) * per + r) for j in...  22.2 us
    pallas_call x2, Pallas kernels, grid_stage(): pl.pallas_call(functools.partial(grid_kernel, split_in, split_out), name=...  21 us
    pallas_call x1, Pallas kernels, mbconv(): pl.pallas_call(mbconv_kernel, name='mbconv', grid=(expanded // LANES,), i...  14.6 us
    all_to_all x2, waiting for transfers between devices, exchange(): lax.all_to_all(pieces[0], 'lon', 0, 0, axis_index_groups=groups, tiled=True)  9.38 us
    all_to_all x2, starting transfers between devices, exchange(): lax.all_to_all(pieces[0], 'lon', 0, 0, axis_index_groups=groups, tiled=True)  7.49 us
    unnamed x49, local copies, waits for them, and re-layouts  6.32 us
    pallas_call x2, Pallas kernels, merge_stage(): pl.pallas_call(functools.partial(merge_kernel, split), name='merge_stage'...  5.58 us
  transfers between devices with their start and end apart: 19, of which 6 were waited for; matrix products, arithmetic and copies ran while one was open for 8% of the time, Pallas kernels for 26%

profile of v5, /device:TPU:0, one launch (start us, length us, event | category | flops | bytes accessed | tf_op | source)
XLA Modules:
  0.0 140.6 jit_solution(6088902443705438937)
XLA Ops:
  1.8 5.1 %collective-permute-start.1 = (bf16[1,48,512]{2,1,0:T(8,128)(2,1)S(1)}, bf16[1,48,512]{2,1,0:T(8,128)(2,1)S(1)}, u32[]{:S(2)}, u32[]{:S(2)}) collective-permute-start(bf16[1,48,512]{2,1,0:T(8,128)(2,1)S(1)} %bitcast.28), channel_id=1, source_target_pairs={{1,0},{2,1},{3,2},{4,3},{5,4},{6,5},{7,6},{8,7},{9,8},{10,9},{11,1... | collective-permute-start | bytes 147464 | tf_op jit(solution)/shard_map/ppermute | solution.py:465
  7.0 3.4 %copy.27 = bf16[48,32,512]{2,0,1:T(8,128)(2,1)} copy(bf16[48,32,512]{2,1,0:T(8,128)(2,1)} %param.17) | data formatting | bytes 3145728 | tf_op args[0]
  11.0 14.6 %mbconv.1 = (bf16[32,48,2048]{2,1,0:T(8,128)(2,1)}, f32[16,8,128]{2,1,0:T(8,128)}) custom-call(bf16[32,48,512]{2,1,0:T(8,128)(2,1)} %bitcast.24, bf16[1,48,512]{2,1,0:T(8,128)(2,1)} %copy-done.19, bf16[1,48,512]{2,1,0:T(8,128)(2,1)} %copy-done.20, bf16[512,2048]{1,0:T(8,128)(2,1)} %w_ref.1, f32[1,2048]{1,0:T(1,128)} %bitcast.33, f32[9,2048]{1,0:T(8,128)} %dw_ref.1, ...), custom_call_target="tpu_custom_call" | custom-call | flops 12884901888 | bytes 20000000 | tf_op jit(solution)/shard_map/mbconv/pallas_call | solution.py:113
  25.6 4.0 %all-to-all-start = ((f32[16,8,128]{2,1,0:T(8,128)}), f32[16,8,128]{2,1,0:T(8,128)S(1)}, u32[]{:S(2)}, u32[]{:S(2)}) async-start(f32[16,8,128]{2,1,0:T(8,128)} %get-tuple-element.32), calls=%async_computation | async-start | bytes 131072 | tf_op jit(solution)/shard_map/all_to_all | solution.py:475
  29.7 2.6 %fusion.4 = f32[64,16,64]{2,1,0:T(8,128)S(1)} fusion(s32[64,64]{1,0:T(8,128)S(1)} %add_add_fusion, f32[225,16]{0,1:T(8,128)S(1)} %copy-done.21), kind=kOutput, calls=%fused_computation.6 | convolution fusion | flops 177872400 | bytes 292928 | tf_op jit(solution)/shard_map/jir,rh->jhi/dot_general | solution.py:415
  33.2 3.4 %all-to-all-done.part_ref = f32[16,8,128]{2,1,0:T(8,128)S(1)} async-done(((f32[16,8,128]{2,1,0:T(8,128)}), f32[16,8,128]{2,1,0:T(8,128)S(1)}, u32[]{:S(2)}, u32[]{:S(2)}) %all-to-all-start) | async-done | bytes 65568 | tf_op jit(solution)/shard_map/all_to_all | solution.py:475
  37.2 13.3 %block_stage.3 = bf16[8,2,48,512]{3,2,1,0:T(8,128)(2,1)} custom-call(s32[1]{0:T(128)} %constant.136.clone.1.me_ref, bf16[32,48,2048]{2,1,0:T(8,128)(2,1)} %get-tuple-element.31.act_ref, bf16[32,48,512]{2,1,0:T(8,128)(2,1)} %bitcast.25, f32[16,8,128]{2,1,0:T(8,128)} %copy-done.2, bf16[128,2048]{1,0:T(8,128)(2,1)} %up_ref.3, bf16[2048,512]{1,0:T(8,128)(2,1)} %proj_ref.3, ...), custom_call_target="tpu_custom_call" | custom-call | flops 1000000 | bytes 100000 | tf_op jit(solution)/shard_map/block_stage/pallas_call | solution.py:329
  50.4 3.7 %all-to-all-start.2 = ((bf16[8,2,48,512]{3,2,1,0:T(8,128)(2,1)}), bf16[8,2,48,512]{3,2,1,0:T(8,128)(2,1)S(1)}, u32[]{:S(2)}, u32[]{:S(2)}) async-start(bf16[8,2,48,512]{3,2,1,0:T(8,128)(2,1)} %block_stage.3), calls=%async_computation.2 | async-start | bytes 1572864 | tf_op jit(solution)/shard_map/all_to_all | solution.py:486
  54.2 2.6 %fusion.5 = f32[64,16,64]{2,1,0:T(8,128)S(1)} fusion(s32[64,64]{1,0:T(8,128)S(1)} %add_add_fusion, f32[225,16]{0,1:T(8,128)S(1)} %copy-done.22), kind=kOutput, calls=%fused_computation.7 | convolution fusion | flops 177872400 | bytes 292928 | tf_op jit(solution)/shard_map/jir,rh->jhi/dot_general | solution.py:415
  58.8 13.3 %block_stage.2 = bf16[8,2,48,512]{3,2,1,0:T(8,128)(2,1)} custom-call(s32[1]{0:T(128)} %constant.136.clone.1.me_ref, bf16[32,48,2048]{2,1,0:T(8,128)(2,1)} %get-tuple-element.31.act_ref, bf16[32,48,512]{2,1,0:T(8,128)(2,1)} %bitcast.26, f32[16,8,128]{2,1,0:T(8,128)} %copy-done.2, bf16[128,2048]{1,0:T(8,128)(2,1)} %up_ref.3, bf16[2048,512]{1,0:T(8,128)(2,1)} %proj_ref.3, ...), custom_call_target="tpu_custom_call" | custom-call | flops 1000000 | bytes 100000 | tf_op jit(solution)/shard_map/block_stage/pallas_call | solution.py:329
  72.1 2.0 %all-to-all-done.2.refs_0_ = bf16[8,2,48,512]{3,2,1,0:T(8,128)(2,1)S(1)} async-done(((bf16[8,2,48,512]{3,2,1,0:T(8,128)(2,1)}), bf16[8,2,48,512]{3,2,1,0:T(8,128)(2,1)S(1)}, u32[]{:S(2)}, u32[]{:S(2)}) %all-to-all-start.2) | async-done | bytes 786464 | tf_op jit(solution)/shard_map/all_to_all | solution.py:486
  74.1 3.8 %all-to-all-start.1 = ((bf16[8,2,48,512]{3,2,1,0:T(8,128)(2,1)}), bf16[8,2,48,512]{3,2,1,0:T(8,128)(2,1)S(1)}, u32[]{:S(2)}, u32[]{:S(2)}) async-start(bf16[8,2,48,512]{3,2,1,0:T(8,128)(2,1)} %block_stage.2), calls=%async_computation.1 | async-start | bytes 1572864 | tf_op jit(solution)/shard_map/all_to_all | solution.py:486
  77.9 10.5 %grid_stage.3 = (bf16[2,48,512]{2,1,0:T(8,128)(2,1)}, bf16[2,48,512]{2,1,0:T(8,128)(2,1)}, bf16[2,48,512]{2,1,0:T(8,128)(2,1)}, bf16[2,48,512]{2,1,0:T(8,128)(2,...) custom-call(s32[1]{0:T(128)} %bitcast.me_ref, ...), custom_call_target="tpu_custom_call" | custom-call | flops 1000000 | bytes 100000 | tf_op jit(solution)/shard_map/grid_stage/pallas_call | solution.py:360
  88.4 2.0 %collective-permute-start.9 = (bf16[2,48,512]{2,1,0:T(8,128)(2,1)}, bf16[2,48,512]{2,1,0:T(8,128)(2,1)S(1)}, u32[]{:S(2)}, u32[]{:S(2)}) collective-permute-start(bf16[2,48,512]{2,1,0:T(8,128)(2,1)} %get-tuple-element.50), channel_id=1, source_target_pairs={{0,2},{1,3},{2,0},{3,1},{4,6},{5,7},{6,4},{7,5},{8,10},{9,11},{10,... | collective-permute-start | bytes 294920 | tf_op jit(solution)/shard_map/ppermute | solution.py:491
  92.0 2.8 %collective-permute-start.12 = (bf16[2,48,512]{2,1,0:T(8,128)(2,1)}, bf16[2,48,512]{2,1,0:T(8,128)(2,1)S(1)}, u32[]{:S(2)}, u32[]{:S(2)}) collective-permute-start(bf16[2,48,512]{2,1,0:T(8,128)(2,1)} %get-tuple-element.53), channel_id=1, source_target_pairs={{0,8},{1,9},{2,10},{3,11},{4,12},{5,13},{6,14},{7,15},{8,0},{9,1},... | collective-permute-start | bytes 294920 | tf_op jit(solution)/shard_map/ppermute | solution.py:491
  96.3 7.4 %all-to-all-done.1.refs_0_ = bf16[8,2,48,512]{3,2,1,0:T(8,128)(2,1)S(1)} async-done(((bf16[8,2,48,512]{3,2,1,0:T(8,128)(2,1)}), bf16[8,2,48,512]{3,2,1,0:T(8,128)(2,1)S(1)}, u32[]{:S(2)}, u32[]{:S(2)}) %all-to-all-start.1) | async-done | bytes 786464 | tf_op jit(solution)/shard_map/all_to_all | solution.py:486
  104.6 10.4 %grid_stage.2 = (bf16[2,48,512]{2,1,0:T(8,128)(2,1)}, bf16[2,48,512]{2,1,0:T(8,128)(2,1)}, bf16[2,48,512]{2,1,0:T(8,128)(2,1)}, bf16[2,48,512]{2,1,0:T(8,128)(2,...) custom-call(s32[1]{0:T(128)} %bitcast.me_ref, ...), custom_call_target="tpu_custom_call" | custom-call | flops 1000000 | bytes 100000 | tf_op jit(solution)/shard_map/grid_stage/pallas_call | solution.py:360
  115.2 4.3 %collective-permute-start.15 = (bf16[2,48,512]{2,1,0:T(8,128)(2,1)S(1)}, bf16[2,48,512]{2,1,0:T(8,128)(2,1)S(1)}, u32[]{:S(2)}, u32[]{:S(2)}) collective-permute-start(bf16[2,48,512]{2,1,0:T(8,128)(2,1)S(1)} %copy-done.17), channel_id=1, source_target_pairs={{0,14},{1,15},{2,12},{3,13},{4,10},{5,11},{6,8},{7,9},{8,6},{9,7},... | collective-permute-start | bytes 294920 | tf_op jit(solution)/shard_map/ppermute | solution.py:491
  120.5 2.4 %collective-permute-start.4 = (bf16[2,48,512]{2,1,0:T(8,128)(2,1)}, bf16[2,48,512]{2,1,0:T(8,128)(2,1)S(1)}, u32[]{:S(2)}, u32[]{:S(2)}) collective-permute-start(bf16[2,48,512]{2,1,0:T(8,128)(2,1)} %get-tuple-element.42), channel_id=1, source_target_pairs={{0,6},{1,7},{2,4},{3,5},{4,2},{5,3},{6,0},{7,1},{8,14},{9,15},{10,... | collective-permute-start | bytes 294920 | tf_op jit(solution)/shard_map/ppermute | solution.py:491
  123.0 1.9 %collective-permute-done.15.refs_7_ = bf16[2,48,512]{2,1,0:T(8,128)(2,1)S(1)} collective-permute-done((bf16[2,48,512]{2,1,0:T(8,128)(2,1)S(1)}, bf16[2,48,512]{2,1,0:T(8,128)(2,1)S(1)}, u32[]{:S(2)}, u32[]{:S(2)}) %collective-permute-start.15) | collective-permute-done | bytes 98336 | tf_op jit(solution)/shard_map/ppermute | solution.py:491
  126.5 4.9 %collective-permute-start.8 = (bf16[2,48,512]{2,1,0:T(8,128)(2,1)}, bf16[2,48,512]{2,1,0:T(8,128)(2,1)S(1)}, u32[]{:S(2)}, u32[]{:S(2)}) collective-permute-start(bf16[2,48,512]{2,1,0:T(8,128)(2,1)} %get-tuple-element.46), channel_id=1, source_target_pairs={{0,14},{1,15},{2,12},{3,13},{4,10},{5,11},{6,8},{7,9},{8,6},{9,7},... | collective-permute-start | bytes 294920 | tf_op jit(solution)/shard_map/ppermute | solution.py:491
  131.4 2.8 %merge_stage.2.refs_9_ = bf16[48,32,512]{2,1,0:T(8,128)(2,1)} custom-call(s32[1]{0:T(128)} %bitcast.me_ref, bf16[2,48,512]{2,1,0:T(8,128)(2,1)} %get-tuple-element.49.refs_0_, bf16[2,48,512]{2,1,0:T(8,128)(2,1)} %copy-done.3, bf16[2,48,512]{2,1,0:T(8,128)(2,1)} %copy-done.4, bf16[2,48,512]{2,1,0:T(8,128)(2,1)} %copy-done.5, bf16[2,48,512]{2,1,0:T(8,128)(2,1)} %copy-done.6, ...), custom_call_target="tpu_custom_call" | custom-call | flops 1000000 | bytes 100000 | tf_op jit(solution)/shard_map/merge_stage/pallas_call | solution.py:387
  134.3 2.8 %collective-permute-done.6.refs_5_ = bf16[2,48,512]{2,1,0:T(8,128)(2,1)S(1)} collective-permute-done((bf16[2,48,512]{2,1,0:T(8,128)(2,1)}, bf16[2,48,512]{2,1,0:T(8,128)(2,1)S(1)}, u32[]{:S(2)}, u32[]{:S(2)}) %collective-permute-start.6) | collective-permute-done | bytes 98336 | tf_op jit(solution)/shard_map/ppermute | solution.py:491
  137.8 2.8 %merge_stage.3 = bf16[48,32,512]{2,1,0:T(8,128)(2,1)} custom-call(s32[1]{0:T(128)} %bitcast.me_ref, bf16[2,48,512]{2,1,0:T(8,128)(2,1)} %get-tuple-element.39.refs_0_, bf16[2,48,512]{2,1,0:T(8,128)(2,1)} %copy-done.10, bf16[2,48,512]{2,1,0:T(8,128)(2,1)} %copy-done.11, bf16[2,48,512]{2,1,0:T(8,128)(2,1)} %copy-done.12, ...), custom_call_target="tpu_custom_call", output_to_operand_aliasing={{}: (10, {})} | custom-call | flops 1000000 | bytes 100000 | tf_op jit(solution)/shard_map/merge_stage/pallas_call | solution.py:387
  (80 shorter events, 13.5 us)
Async XLA Ops:
  1.3 9.1 %collective-permute-start = (bf16[1,48,512]{2,1,0:T(8,128)(2,1)S(1)}, bf16[1,48,512]{2,1,0:T(8,128)(2,1)S(1)}, u32[]{:S(2)}, u32[]{:S(2)}) collective-permute-start(bf16[1,48,512]{2,1,0:T(8,128)(2,1)S(1)} %bitcast.27), channel_id=1, source_target_pairs={{0,1},{1,2},{2,3},{3,4},{4,5},{5,6},{6,7},{7,8},{8,9},{9,10},{10,1... | collective-permute-start | bytes 147464 | tf_op jit(solution)/shard_map/ppermute | solution.py:460
  1.8 8.6 %collective-permute-start.1 = (bf16[1,48,512]{2,1,0:T(8,128)(2,1)S(1)}, bf16[1,48,512]{2,1,0:T(8,128)(2,1)S(1)}, u32[]{:S(2)}, u32[]{:S(2)}) collective-permute-start(bf16[1,48,512]{2,1,0:T(8,128)(2,1)S(1)} %bitcast.28), channel_id=1, source_target_pairs={{1,0},{2,1},{3,2},{4,3},{5,4},{6,5},{7,6},{8,7},{9,8},{10,9},{11,1... | collective-permute-start | bytes 147464 | tf_op jit(solution)/shard_map/ppermute | solution.py:465
  11.0 18.6 %copy-start.21 = (f32[225,16]{0,1:T(8,128)S(1)}, f32[225,16]{0,1:T(8,128)}, u32[]{:S(2)}) copy-start(f32[225,16]{0,1:T(8,128)} %param.28) | copy-start | bytes 43204
  25.6 11.0 %all-to-all-start = ((f32[16,8,128]{2,1,0:T(8,128)}), f32[16,8,128]{2,1,0:T(8,128)S(1)}, u32[]{:S(2)}, u32[]{:S(2)}) async-start(f32[16,8,128]{2,1,0:T(8,128)} %get-tuple-element.32), calls=%async_computation | async-start | bytes 131072 | tf_op jit(solution)/shard_map/all_to_all | solution.py:475
  37.2 17.0 %copy-start.22 = (f32[225,16]{0,1:T(8,128)S(1)}, f32[225,16]{0,1:T(8,128)}, u32[]{:S(2)}) copy-start(f32[225,16]{0,1:T(8,128)} %param.32) | copy-start | bytes 43204
  50.4 23.6 %all-to-all-start.2 = ((bf16[8,2,48,512]{3,2,1,0:T(8,128)(2,1)}), bf16[8,2,48,512]{3,2,1,0:T(8,128)(2,1)S(1)}, u32[]{:S(2)}, u32[]{:S(2)}) async-start(bf16[8,2,48,512]{3,2,1,0:T(8,128)(2,1)} %block_stage.3), calls=%async_computation.2 | async-start | bytes 1572864 | tf_op jit(solution)/shard_map/all_to_all | solution.py:486
  74.1 29.6 %all-to-all-start.1 = ((bf16[8,2,48,512]{3,2,1,0:T(8,128)(2,1)}), bf16[8,2,48,512]{3,2,1,0:T(8,128)(2,1)S(1)}, u32[]{:S(2)}, u32[]{:S(2)}) async-start(bf16[8,2,48,512]{3,2,1,0:T(8,128)(2,1)} %block_stage.2), calls=%async_computation.1 | async-start | bytes 1572864 | tf_op jit(solution)/shard_map/all_to_all | solution.py:486
  88.4 26.6 %copy-start.18 = (bf16[2,48,512]{2,1,0:T(8,128)(2,1)S(1)}, bf16[2,48,512]{2,1,0:T(8,128)(2,1)}, u32[]{:S(2)}) copy-start(bf16[2,48,512]{2,1,0:T(8,128)(2,1)} %get-tuple-element.55) | copy-start | bytes 294916
  88.4 26.8 %copy-start.17 = (bf16[2,48,512]{2,1,0:T(8,128)(2,1)S(1)}, bf16[2,48,512]{2,1,0:T(8,128)(2,1)}, u32[]{:S(2)}) copy-start(bf16[2,48,512]{2,1,0:T(8,128)(2,1)} %get-tuple-element.56) | copy-start | bytes 294916
  88.4 26.6 %collective-permute-start.9 = (bf16[2,48,512]{2,1,0:T(8,128)(2,1)}, bf16[2,48,512]{2,1,0:T(8,128)(2,1)S(1)}, u32[]{:S(2)}, u32[]{:S(2)}) collective-permute-start(bf16[2,48,512]{2,1,0:T(8,128)(2,1)} %get-tuple-element.50), channel_id=1, source_target_pairs={{0,2},{1,3},{2,0},{3,1},{4,6},{5,7},{6,4},{7,5},{8,10},{9,11},{10,... | collective-permute-start | bytes 294920 | tf_op jit(solution)/shard_map/ppermute | solution.py:491
  90.4 24.7 %collective-permute-start.10 = (bf16[2,48,512]{2,1,0:T(8,128)(2,1)}, bf16[2,48,512]{2,1,0:T(8,128)(2,1)S(1)}, u32[]{:S(2)}, u32[]{:S(2)}) collective-permute-start(bf16[2,48,512]{2,1,0:T(8,128)(2,1)} %get-tuple-element.51), channel_id=1, source_target_pairs={{0,4},{1,5},{2,6},{3,7},{4,0},{5,1},{6,2},{7,3},{8,12},{9,13},{10,... | collective-permute-start | bytes 294920 | tf_op jit(solution)/shard_map/ppermute | solution.py:491
  91.9 27.5 %collective-permute-start.11 = (bf16[2,48,512]{2,1,0:T(8,128)(2,1)}, bf16[2,48,512]{2,1,0:T(8,128)(2,1)S(1)}, u32[]{:S(2)}, u32[]{:S(2)}) collective-permute-start(bf16[2,48,512]{2,1,0:T(8,128)(2,1)} %get-tuple-element.52), channel_id=1, source_target_pairs={{0,6},{1,7},{2,4},{3,5},{4,2},{5,3},{6,0},{7,1},{8,14},{9,15},{10,... | collective-permute-start | bytes 294920 | tf_op jit(solution)/shard_map/ppermute | solution.py:491
  92.0 28.5 %collective-permute-start.12 = (bf16[2,48,512]{2,1,0:T(8,128)(2,1)}, bf16[2,48,512]{2,1,0:T(8,128)(2,1)S(1)}, u32[]{:S(2)}, u32[]{:S(2)}) collective-permute-start(bf16[2,48,512]{2,1,0:T(8,128)(2,1)} %get-tuple-element.53), channel_id=1, source_target_pairs={{0,8},{1,9},{2,10},{3,11},{4,12},{5,13},{6,14},{7,15},{8,0},{9,1},... | collective-permute-start | bytes 294920 | tf_op jit(solution)/shard_map/ppermute | solution.py:491
  94.8 25.7 %collective-permute-start.13 = (bf16[2,48,512]{2,1,0:T(8,128)(2,1)}, bf16[2,48,512]{2,1,0:T(8,128)(2,1)S(1)}, u32[]{:S(2)}, u32[]{:S(2)}) collective-permute-start(bf16[2,48,512]{2,1,0:T(8,128)(2,1)} %get-tuple-element.54), channel_id=1, source_target_pairs={{0,10},{1,11},{2,8},{3,9},{4,14},{5,15},{6,12},{7,13},{8,2},{9,3},... | collective-permute-start | bytes 294920 | tf_op jit(solution)/shard_map/ppermute | solution.py:491
  115.0 16.4 %copy-start.3 = (bf16[2,48,512]{2,1,0:T(8,128)(2,1)}, bf16[2,48,512]{2,1,0:T(8,128)(2,1)S(1)}, u32[]{:S(2)}) copy-start(bf16[2,48,512]{2,1,0:T(8,128)(2,1)S(1)} %collective-permute-done.9.refs_1_) | copy-start | bytes 294916
  115.0 7.9 %collective-permute-start.14 = (bf16[2,48,512]{2,1,0:T(8,128)(2,1)S(1)}, bf16[2,48,512]{2,1,0:T(8,128)(2,1)S(1)}, u32[]{:S(2)}, u32[]{:S(2)}) collective-permute-start(bf16[2,48,512]{2,1,0:T(8,128)(2,1)S(1)} %copy-done.18), channel_id=1, source_target_pairs={{0,12},{1,13},{2,14},{3,15},{4,8},{5,9},{6,10},{7,11},{8,4},{9,5},... | collective-permute-start | bytes 294920 | tf_op jit(solution)/shard_map/ppermute | solution.py:491
  115.2 9.7 %collective-permute-start.15 = (bf16[2,48,512]{2,1,0:T(8,128)(2,1)S(1)}, bf16[2,48,512]{2,1,0:T(8,128)(2,1)S(1)}, u32[]{:S(2)}, u32[]{:S(2)}) collective-permute-start(bf16[2,48,512]{2,1,0:T(8,128)(2,1)S(1)} %copy-done.17), channel_id=1, source_target_pairs={{0,14},{1,15},{2,12},{3,13},{4,10},{5,11},{6,8},{7,9},{8,6},{9,7},... | collective-permute-start | bytes 294920 | tf_op jit(solution)/shard_map/ppermute | solution.py:491
  119.4 6.9 %collective-permute-start.2 = (bf16[2,48,512]{2,1,0:T(8,128)(2,1)}, bf16[2,48,512]{2,1,0:T(8,128)(2,1)S(1)}, u32[]{:S(2)}, u32[]{:S(2)}) collective-permute-start(bf16[2,48,512]{2,1,0:T(8,128)(2,1)} %get-tuple-element.40), channel_id=1, source_target_pairs={{0,2},{1,3},{2,0},{3,1},{4,6},{5,7},{6,4},{7,5},{8,10},{9,11},{10,... | collective-permute-start | bytes 294920 | tf_op jit(solution)/shard_map/ppermute | solution.py:491
  120.5 6.0 %collective-permute-start.3 = (bf16[2,48,512]{2,1,0:T(8,128)(2,1)}, bf16[2,48,512]{2,1,0:T(8,128)(2,1)S(1)}, u32[]{:S(2)}, u32[]{:S(2)}) collective-permute-start(bf16[2,48,512]{2,1,0:T(8,128)(2,1)} %get-tuple-element.41), channel_id=1, source_target_pairs={{0,4},{1,5},{2,6},{3,7},{4,0},{5,1},{6,2},{7,3},{8,12},{9,13},{10,... | collective-permute-start | bytes 294920 | tf_op jit(solution)/shard_map/ppermute | solution.py:491
  120.5 13.7 %collective-permute-start.4 = (bf16[2,48,512]{2,1,0:T(8,128)(2,1)}, bf16[2,48,512]{2,1,0:T(8,128)(2,1)S(1)}, u32[]{:S(2)}, u32[]{:S(2)}) collective-permute-start(bf16[2,48,512]{2,1,0:T(8,128)(2,1)} %get-tuple-element.42), channel_id=1, source_target_pairs={{0,6},{1,7},{2,4},{3,5},{4,2},{5,3},{6,0},{7,1},{8,14},{9,15},{10,... | collective-permute-start | bytes 294920 | tf_op jit(solution)/shard_map/ppermute | solution.py:491
  123.0 11.4 %collective-permute-start.5 = (bf16[2,48,512]{2,1,0:T(8,128)(2,1)}, bf16[2,48,512]{2,1,0:T(8,128)(2,1)S(1)}, u32[]{:S(2)}, u32[]{:S(2)}) collective-permute-start(bf16[2,48,512]{2,1,0:T(8,128)(2,1)} %get-tuple-element.43), channel_id=1, source_target_pairs={{0,8},{1,9},{2,10},{3,11},{4,12},{5,13},{6,14},{7,15},{8,0},{9,1},... | collective-permute-start | bytes 294920 | tf_op jit(solution)/shard_map/ppermute | solution.py:491
  124.9 12.3 %collective-permute-start.6 = (bf16[2,48,512]{2,1,0:T(8,128)(2,1)}, bf16[2,48,512]{2,1,0:T(8,128)(2,1)S(1)}, u32[]{:S(2)}, u32[]{:S(2)}) collective-permute-start(bf16[2,48,512]{2,1,0:T(8,128)(2,1)} %get-tuple-element.44), channel_id=1, source_target_pairs={{0,10},{1,11},{2,8},{3,9},{4,14},{5,15},{6,12},{7,13},{8,2},{9,3},... | collective-permute-start | bytes 294920 | tf_op jit(solution)/shard_map/ppermute | solution.py:491
  126.4 10.8 %collective-permute-start.7 = (bf16[2,48,512]{2,1,0:T(8,128)(2,1)}, bf16[2,48,512]{2,1,0:T(8,128)(2,1)S(1)}, u32[]{:S(2)}, u32[]{:S(2)}) collective-permute-start(bf16[2,48,512]{2,1,0:T(8,128)(2,1)} %get-tuple-element.45), channel_id=1, source_target_pairs={{0,12},{1,13},{2,14},{3,15},{4,8},{5,9},{6,10},{7,11},{8,4},{9,5},... | collective-permute-start | bytes 294920 | tf_op jit(solution)/shard_map/ppermute | solution.py:491
  126.5 10.6 %collective-permute-start.8 = (bf16[2,48,512]{2,1,0:T(8,128)(2,1)}, bf16[2,48,512]{2,1,0:T(8,128)(2,1)S(1)}, u32[]{:S(2)}, u32[]{:S(2)}) collective-permute-start(bf16[2,48,512]{2,1,0:T(8,128)(2,1)} %get-tuple-element.46), channel_id=1, source_target_pairs={{0,14},{1,15},{2,12},{3,13},{4,10},{5,11},{6,8},{7,9},{8,6},{9,7},... | collective-permute-start | bytes 294920 | tf_op jit(solution)/shard_map/ppermute | solution.py:491
  (18 other events, 100.8 us)

commit v6 on v5

--- a/solution.py
+++ b/solution.py
@@ -13,6 +13,7 @@
 WIN = 8
 CELLS = WIN * WIN
 CHUNKS = ((2, False, True), (2, False, True))
+TIED = 4
 LANES = 512
 SUB = 256
 VMEM_BYTES = 60 << 20
@@ -513,14 +514,16 @@
     for k, (_, split, returned) in enumerate(chunks):
         pieces = received[k]
         if k + 1 < len(chunks):
-            later = sent[k + 1][0]
-            pieces, _ = lax.optimization_barrier((pieces, later))
+            pieces, _ = lax.optimization_barrier((pieces, sent[k + 1][0]))
+        if k > 0 and chunks[k - 1][2]:
+            pieces, _ = lax.optimization_barrier((pieces, results[k - 1][1:TIED]))
         me = places[split or returned]
-        results.append(grid_stage(split, returned, me, pieces, into[split], grid_params))
+        result = grid_stage(split, returned, me, pieces, into[split], grid_params)
+        results.append(exchange(returned, result))
     merged = None
     for start, result, (_, _, split) in zip(starts, results, chunks):
         merged = merge_stage(
-            split, start, total, places[split], exchange(split, result), back[split], merged
+            split, start, total, places[split], result, back[split], merged
         )
     return merged
 

time: 141 us -> 140 us (level)
  waiting for transfers between devices: 17.6 us -> 15.4 us
    ppermute x14, waiting for transfers between devices: 4.79 us -> 2.2 us  [exchange(): lax.ppermute(pieces[s], 'lon', [(j * per + r, (j ^ s) * per + r) for j in...]
    unnamed x49 -> x45, local copies, waits for them, and re-layouts: 6.32 us -> 6.3 us
  transfers between devices with their start and end apart: 19 -> 19, of which waited for: 6 -> 4; matrix products, arithmetic and copies ran while one was open for 8% -> 8% of each run, Pallas kernels for 26% -> 27%
where the time goes in v6:
time: 140 us; the launch traced here: 139 us
  Pallas kernels  67.7 us (48%)
  starting transfers between devices  39.9 us (28%)
  waiting for transfers between devices  15.4 us (11%)
  local copies, waits for them, and re-layouts  9.35 us (7%)
  matrix products  5.24 us (4%)
    pallas_call x2, Pallas kernels, block_stage(): pl.pallas_call(functools.partial(block_kernel, scale, split), name='block...  26.6 us
    ppermute x14, starting transfers between devices, exchange(): lax.ppermute(pieces[s], 'lon', [(j * per + r, (j ^ s) * per + r) for j in...  22.8 us
    pallas_call x2, Pallas kernels, grid_stage(): pl.pallas_call(functools.partial(grid_kernel, split_in, split_out), name=...  21 us
    pallas_call x1, Pallas kernels, mbconv(): pl.pallas_call(mbconv_kernel, name='mbconv', grid=(expanded // LANES,), i...  14.6 us
    all_to_all x2, waiting for transfers between devices, exchange(): lax.all_to_all(pieces[0], 'lon', 0, 0, axis_index_groups=groups, tiled=True)  9.85 us
    all_to_all x2, starting transfers between devices, exchange(): lax.all_to_all(pieces[0], 'lon', 0, 0, axis_index_groups=groups, tiled=True)  7.5 us
    unnamed x45, local copies, waits for them, and re-layouts  6.3 us
    pallas_call x2, Pallas kernels, merge_stage(): pl.pallas_call(functools.partial(merge_kernel, split), name='merge_stage'...  5.58 us
  transfers between devices with their start and end apart: 19, of which 4 were waited for; matrix products, arithmetic and copies ran while one was open for 8% of the time, Pallas kernels for 27%

profile of v6, /device:TPU:0, one launch (start us, length us, event | category | flops | bytes accessed | tf_op | source)
XLA Modules:
  0.0 139.1 jit_solution(6717322688003470393)
XLA Ops:
  1.8 5.1 %collective-permute-start.1 = (bf16[1,48,512]{2,1,0:T(8,128)(2,1)S(1)}, bf16[1,48,512]{2,1,0:T(8,128)(2,1)S(1)}, u32[]{:S(2)}, u32[]{:S(2)}) collective-permute-start(bf16[1,48,512]{2,1,0:T(8,128)(2,1)S(1)} %bitcast.28), channel_id=1, source_target_pairs={{1,0},{2,1},{3,2},{4,3},{5,4},{6,5},{7,6},{8,7},{9,8},{10,9},{11,1... | collective-permute-start | bytes 147464 | tf_op jit(solution)/shard_map/ppermute | solution.py:466
  7.0 3.4 %copy.27 = bf16[48,32,512]{2,0,1:T(8,128)(2,1)} copy(bf16[48,32,512]{2,1,0:T(8,128)(2,1)} %param.17) | data formatting | bytes 3145728 | tf_op args[0]
  11.0 14.6 %mbconv.1 = (bf16[32,48,2048]{2,1,0:T(8,128)(2,1)}, f32[16,8,128]{2,1,0:T(8,128)}) custom-call(bf16[32,48,512]{2,1,0:T(8,128)(2,1)} %bitcast.24, bf16[1,48,512]{2,1,0:T(8,128)(2,1)} %copy-done.17, bf16[1,48,512]{2,1,0:T(8,128)(2,1)} %copy-done.18, bf16[512,2048]{1,0:T(8,128)(2,1)} %w_ref.1, f32[1,2048]{1,0:T(1,128)} %bitcast.33, f32[9,2048]{1,0:T(8,128)} %dw_ref.1, ...), custom_call_target="tpu_custom_call" | custom-call | flops 12884901888 | bytes 20000000 | tf_op jit(solution)/shard_map/mbconv/pallas_call | solution.py:114
  25.6 4.1 %all-to-all-start = ((f32[16,8,128]{2,1,0:T(8,128)}), f32[16,8,128]{2,1,0:T(8,128)S(1)}, u32[]{:S(2)}, u32[]{:S(2)}) async-start(f32[16,8,128]{2,1,0:T(8,128)} %get-tuple-element.33), calls=%async_computation | async-start | bytes 131072 | tf_op jit(solution)/shard_map/all_to_all | solution.py:476
  29.7 2.6 %fusion.4 = f32[64,16,64]{2,1,0:T(8,128)S(1)} fusion(s32[64,64]{1,0:T(8,128)S(1)} %add_add_fusion, f32[225,16]{0,1:T(8,128)S(1)} %copy-done.19), kind=kOutput, calls=%fused_computation.6 | convolution fusion | flops 177872400 | bytes 292928 | tf_op jit(solution)/shard_map/jir,rh->jhi/dot_general | solution.py:416
  33.2 3.4 %all-to-all-done.part_ref = f32[16,8,128]{2,1,0:T(8,128)S(1)} async-done(((f32[16,8,128]{2,1,0:T(8,128)}), f32[16,8,128]{2,1,0:T(8,128)S(1)}, u32[]{:S(2)}, u32[]{:S(2)}) %all-to-all-start) | async-done | bytes 65568 | tf_op jit(solution)/shard_map/all_to_all | solution.py:476
  37.2 13.3 %block_stage.3 = bf16[8,2,48,512]{3,2,1,0:T(8,128)(2,1)} custom-call(s32[1]{0:T(128)} %constant.136.clone.1.me_ref, bf16[32,48,2048]{2,1,0:T(8,128)(2,1)} %get-tuple-element.32.act_ref, bf16[32,48,512]{2,1,0:T(8,128)(2,1)} %bitcast.25, f32[16,8,128]{2,1,0:T(8,128)} %copy-done.2, bf16[128,2048]{1,0:T(8,128)(2,1)} %up_ref.3, bf16[2048,512]{1,0:T(8,128)(2,1)} %proj_ref.3, ...), custom_call_target="tpu_custom_call" | custom-call | flops 1000000 | bytes 100000 | tf_op jit(solution)/shard_map/block_stage/pallas_call | solution.py:330
  50.4 3.7 %all-to-all-start.2 = ((bf16[8,2,48,512]{3,2,1,0:T(8,128)(2,1)}), bf16[8,2,48,512]{3,2,1,0:T(8,128)(2,1)S(1)}, u32[]{:S(2)}, u32[]{:S(2)}) async-start(bf16[8,2,48,512]{3,2,1,0:T(8,128)(2,1)} %block_stage.3), calls=%async_computation.2 | async-start | bytes 1572864 | tf_op jit(solution)/shard_map/all_to_all | solution.py:487
  54.2 2.6 %fusion.5 = f32[64,16,64]{2,1,0:T(8,128)S(1)} fusion(s32[64,64]{1,0:T(8,128)S(1)} %add_add_fusion, f32[225,16]{0,1:T(8,128)S(1)} %copy-done.20), kind=kOutput, calls=%fused_computation.7 | convolution fusion | flops 177872400 | bytes 292928 | tf_op jit(solution)/shard_map/jir,rh->jhi/dot_general | solution.py:416
  58.8 13.3 %block_stage.2 = bf16[8,2,48,512]{3,2,1,0:T(8,128)(2,1)} custom-call(s32[1]{0:T(128)} %constant.136.clone.1.me_ref, bf16[32,48,2048]{2,1,0:T(8,128)(2,1)} %get-tuple-element.32.act_ref, bf16[32,48,512]{2,1,0:T(8,128)(2,1)} %bitcast.26, f32[16,8,128]{2,1,0:T(8,128)} %copy-done.2, bf16[128,2048]{1,0:T(8,128)(2,1)} %up_ref.3, bf16[2048,512]{1,0:T(8,128)(2,1)} %proj_ref.3, ...), custom_call_target="tpu_custom_call" | custom-call | flops 1000000 | bytes 100000 | tf_op jit(solution)/shard_map/block_stage/pallas_call | solution.py:330
  72.1 2.0 %all-to-all-done.2.refs_0_ = bf16[8,2,48,512]{3,2,1,0:T(8,128)(2,1)S(1)} async-done(((bf16[8,2,48,512]{3,2,1,0:T(8,128)(2,1)}), bf16[8,2,48,512]{3,2,1,0:T(8,128)(2,1)S(1)}, u32[]{:S(2)}, u32[]{:S(2)}) %all-to-all-start.2) | async-done | bytes 786464 | tf_op jit(solution)/shard_map/all_to_all | solution.py:487
  74.1 3.8 %all-to-all-start.1 = ((bf16[8,2,48,512]{3,2,1,0:T(8,128)(2,1)}), bf16[8,2,48,512]{3,2,1,0:T(8,128)(2,1)S(1)}, u32[]{:S(2)}, u32[]{:S(2)}) async-start(bf16[8,2,48,512]{3,2,1,0:T(8,128)(2,1)} %block_stage.2), calls=%async_computation.1 | async-start | bytes 1572864 | tf_op jit(solution)/shard_map/all_to_all | solution.py:487
  77.9 10.5 %grid_stage.2 = (bf16[2,48,512]{2,1,0:T(8,128)(2,1)}, bf16[2,48,512]{2,1,0:T(8,128)(2,1)}, bf16[2,48,512]{2,1,0:T(8,128)(2,1)}, bf16[2,48,512]{2,1,0:T(8,128)(2,...) custom-call(s32[1]{0:T(128)} %bitcast.me_ref, ...), custom_call_target="tpu_custom_call" | custom-call | flops 1000000 | bytes 100000 | tf_op jit(solution)/shard_map/grid_stage/pallas_call | solution.py:361
  88.3 2.1 %collective-permute-start.2 = (bf16[2,48,512]{2,1,0:T(8,128)(2,1)}, bf16[2,48,512]{2,1,0:T(8,128)(2,1)S(1)}, u32[]{:S(2)}, u32[]{:S(2)}) collective-permute-start(bf16[2,48,512]{2,1,0:T(8,128)(2,1)} %get-tuple-element.41), channel_id=1, source_target_pairs={{0,2},{1,3},{2,0},{3,1},{4,6},{5,7},{6,4},{7,5},{8,10},{9,11},{10,... | collective-permute-start | bytes 294920 | tf_op jit(solution)/shard_map/ppermute | solution.py:492
  91.9 2.8 %collective-permute-start.12 = (bf16[2,48,512]{2,1,0:T(8,128)(2,1)}, bf16[2,48,512]{2,1,0:T(8,128)(2,1)S(1)}, u32[]{:S(2)}, u32[]{:S(2)}) collective-permute-start(bf16[2,48,512]{2,1,0:T(8,128)(2,1)} %get-tuple-element.55), channel_id=1, source_target_pairs={{0,8},{1,9},{2,10},{3,11},{4,12},{5,13},{6,14},{7,15},{8,0},{9,1},... | collective-permute-start | bytes 294920 | tf_op jit(solution)/shard_map/ppermute | solution.py:492
  96.2 3.3 %collective-permute-start.14 = (bf16[2,48,512]{2,1,0:T(8,128)(2,1)}, bf16[2,48,512]{2,1,0:T(8,128)(2,1)S(1)}, u32[]{:S(2)}, u32[]{:S(2)}) collective-permute-start(bf16[2,48,512]{2,1,0:T(8,128)(2,1)} %get-tuple-element.57), channel_id=1, source_target_pairs={{0,12},{1,13},{2,14},{3,15},{4,8},{5,9},{6,10},{7,11},{8,4},{9,5},... | collective-permute-start | bytes 294920 | tf_op jit(solution)/shard_map/ppermute | solution.py:492
  100.0 7.9 %all-to-all-done.1.refs_0_ = bf16[8,2,48,512]{3,2,1,0:T(8,128)(2,1)S(1)} async-done(((bf16[8,2,48,512]{3,2,1,0:T(8,128)(2,1)}), bf16[8,2,48,512]{3,2,1,0:T(8,128)(2,1)S(1)}, u32[]{:S(2)}, u32[]{:S(2)}) %all-to-all-start.1) | async-done | bytes 786464 | tf_op jit(solution)/shard_map/all_to_all | solution.py:487
  108.8 10.5 %grid_stage.3 = (bf16[2,48,512]{2,1,0:T(8,128)(2,1)}, bf16[2,48,512]{2,1,0:T(8,128)(2,1)}, bf16[2,48,512]{2,1,0:T(8,128)(2,1)}, bf16[2,48,512]{2,1,0:T(8,128)(2,...) custom-call(s32[1]{0:T(128)} %bitcast.me_ref, ...), custom_call_target="tpu_custom_call" | custom-call | flops 1000000 | bytes 100000 | tf_op jit(solution)/shard_map/grid_stage/pallas_call | solution.py:361
  120.4 2.5 %collective-permute-start.7 = (bf16[2,48,512]{2,1,0:T(8,128)(2,1)}, bf16[2,48,512]{2,1,0:T(8,128)(2,1)S(1)}, u32[]{:S(2)}, u32[]{:S(2)}) collective-permute-start(bf16[2,48,512]{2,1,0:T(8,128)(2,1)} %get-tuple-element.48), channel_id=1, source_target_pairs={{0,6},{1,7},{2,4},{3,5},{4,2},{5,3},{6,0},{7,1},{8,14},{9,15},{10,... | collective-permute-start | bytes 294920 | tf_op jit(solution)/shard_map/ppermute | solution.py:492
  122.9 3.3 %collective-permute-start.9 = (bf16[2,48,512]{2,1,0:T(8,128)(2,1)}, bf16[2,48,512]{2,1,0:T(8,128)(2,1)S(1)}, u32[]{:S(2)}, u32[]{:S(2)}) collective-permute-start(bf16[2,48,512]{2,1,0:T(8,128)(2,1)} %get-tuple-element.50), channel_id=1, source_target_pairs={{0,10},{1,11},{2,8},{3,9},{4,14},{5,15},{6,12},{7,13},{8,2},{9,3},... | collective-permute-start | bytes 294920 | tf_op jit(solution)/shard_map/ppermute | solution.py:492
  126.2 4.3 %collective-permute-start.11 = (bf16[2,48,512]{2,1,0:T(8,128)(2,1)}, bf16[2,48,512]{2,1,0:T(8,128)(2,1)S(1)}, u32[]{:S(2)}, u32[]{:S(2)}) collective-permute-start(bf16[2,48,512]{2,1,0:T(8,128)(2,1)} %get-tuple-element.52), channel_id=1, source_target_pairs={{0,14},{1,15},{2,12},{3,13},{4,10},{5,11},{6,8},{7,9},{8,6},{9,7},... | collective-permute-start | bytes 294920 | tf_op jit(solution)/shard_map/ppermute | solution.py:492
  130.6 2.8 %merge_stage.2.refs_9_ = bf16[48,32,512]{2,1,0:T(8,128)(2,1)} custom-call(s32[1]{0:T(128)} %bitcast.me_ref, bf16[2,48,512]{2,1,0:T(8,128)(2,1)} %get-tuple-element.54.refs_0_, bf16[2,48,512]{2,1,0:T(8,128)(2,1)} %copy-done.3, bf16[2,48,512]{2,1,0:T(8,128)(2,1)} %copy-done.4, bf16[2,48,512]{2,1,0:T(8,128)(2,1)} %copy-done.5, bf16[2,48,512]{2,1,0:T(8,128)(2,1)} %copy-done.6, ...), custom_call_target="tpu_custom_call" | custom-call | flops 1000000 | bytes 100000 | tf_op jit(solution)/shard_map/merge_stage/pallas_call | solution.py:388
  133.4 2.2 %collective-permute-done.9.refs_5_ = bf16[2,48,512]{2,1,0:T(8,128)(2,1)S(1)} collective-permute-done((bf16[2,48,512]{2,1,0:T(8,128)(2,1)}, bf16[2,48,512]{2,1,0:T(8,128)(2,1)S(1)}, u32[]{:S(2)}, u32[]{:S(2)}) %collective-permute-start.9) | collective-permute-done | bytes 98336 | tf_op jit(solution)/shard_map/ppermute | solution.py:492
  136.3 2.8 %merge_stage.3 = bf16[48,32,512]{2,1,0:T(8,128)(2,1)} custom-call(s32[1]{0:T(128)} %bitcast.me_ref, bf16[2,48,512]{2,1,0:T(8,128)(2,1)} %get-tuple-element.45.refs_0_, bf16[2,48,512]{2,1,0:T(8,128)(2,1)} %copy-done.10, bf16[2,48,512]{2,1,0:T(8,128)(2,1)} %copy-done.11, bf16[2,48,512]{2,1,0:T(8,128)(2,1)} %copy-done.12, ...), custom_call_target="tpu_custom_call", output_to_operand_aliasing={{}: (10, {})} | custom-call | flops 1000000 | bytes 100000 | tf_op jit(solution)/shard_map/merge_stage/pallas_call | solution.py:388
  (76 shorter events, 12.2 us)
Async XLA Ops:
  1.3 9.1 %collective-permute-start = (bf16[1,48,512]{2,1,0:T(8,128)(2,1)S(1)}, bf16[1,48,512]{2,1,0:T(8,128)(2,1)S(1)}, u32[]{:S(2)}, u32[]{:S(2)}) collective-permute-start(bf16[1,48,512]{2,1,0:T(8,128)(2,1)S(1)} %bitcast.27), channel_id=1, source_target_pairs={{0,1},{1,2},{2,3},{3,4},{4,5},{5,6},{6,7},{7,8},{8,9},{9,10},{10,1... | collective-permute-start | bytes 147464 | tf_op jit(solution)/shard_map/ppermute | solution.py:461
  1.8 8.6 %collective-permute-start.1 = (bf16[1,48,512]{2,1,0:T(8,128)(2,1)S(1)}, bf16[1,48,512]{2,1,0:T(8,128)(2,1)S(1)}, u32[]{:S(2)}, u32[]{:S(2)}) collective-permute-start(bf16[1,48,512]{2,1,0:T(8,128)(2,1)S(1)} %bitcast.28), channel_id=1, source_target_pairs={{1,0},{2,1},{3,2},{4,3},{5,4},{6,5},{7,6},{8,7},{9,8},{10,9},{11,1... | collective-permute-start | bytes 147464 | tf_op jit(solution)/shard_map/ppermute | solution.py:466
  11.0 18.6 %copy-start.19 = (f32[225,16]{0,1:T(8,128)S(1)}, f32[225,16]{0,1:T(8,128)}, u32[]{:S(2)}) copy-start(f32[225,16]{0,1:T(8,128)} %param.28) | copy-start | bytes 43204
  25.6 11.0 %all-to-all-start = ((f32[16,8,128]{2,1,0:T(8,128)}), f32[16,8,128]{2,1,0:T(8,128)S(1)}, u32[]{:S(2)}, u32[]{:S(2)}) async-start(f32[16,8,128]{2,1,0:T(8,128)} %get-tuple-element.33), calls=%async_computation | async-start | bytes 131072 | tf_op jit(solution)/shard_map/all_to_all | solution.py:476
  37.2 17.0 %copy-start.20 = (f32[225,16]{0,1:T(8,128)S(1)}, f32[225,16]{0,1:T(8,128)}, u32[]{:S(2)}) copy-start(f32[225,16]{0,1:T(8,128)} %param.32) | copy-start | bytes 43204
  50.4 23.6 %all-to-all-start.2 = ((bf16[8,2,48,512]{3,2,1,0:T(8,128)(2,1)}), bf16[8,2,48,512]{3,2,1,0:T(8,128)(2,1)S(1)}, u32[]{:S(2)}, u32[]{:S(2)}) async-start(bf16[8,2,48,512]{3,2,1,0:T(8,128)(2,1)} %block_stage.3), calls=%async_computation.2 | async-start | bytes 1572864 | tf_op jit(solution)/shard_map/all_to_all | solution.py:487
  74.1 33.8 %all-to-all-start.1 = ((bf16[8,2,48,512]{3,2,1,0:T(8,128)(2,1)}), bf16[8,2,48,512]{3,2,1,0:T(8,128)(2,1)S(1)}, u32[]{:S(2)}, u32[]{:S(2)}) async-start(bf16[8,2,48,512]{3,2,1,0:T(8,128)(2,1)} %block_stage.2), calls=%async_computation.1 | async-start | bytes 1572864 | tf_op jit(solution)/shard_map/all_to_all | solution.py:487
  88.3 7.9 %collective-permute-start.2 = (bf16[2,48,512]{2,1,0:T(8,128)(2,1)}, bf16[2,48,512]{2,1,0:T(8,128)(2,1)S(1)}, u32[]{:S(2)}, u32[]{:S(2)}) collective-permute-start(bf16[2,48,512]{2,1,0:T(8,128)(2,1)} %get-tuple-element.41), channel_id=1, source_target_pairs={{0,2},{1,3},{2,0},{3,1},{4,6},{5,7},{6,4},{7,5},{8,10},{9,11},{10,... | collective-permute-start | bytes 294920 | tf_op jit(solution)/shard_map/ppermute | solution.py:492
  90.4 9.1 %collective-permute-start.3 = (bf16[2,48,512]{2,1,0:T(8,128)(2,1)}, bf16[2,48,512]{2,1,0:T(8,128)(2,1)S(1)}, u32[]{:S(2)}, u32[]{:S(2)}) collective-permute-start(bf16[2,48,512]{2,1,0:T(8,128)(2,1)} %get-tuple-element.42), channel_id=1, source_target_pairs={{0,4},{1,5},{2,6},{3,7},{4,0},{5,1},{6,2},{7,3},{8,12},{9,13},{10,... | collective-permute-start | bytes 294920 | tf_op jit(solution)/shard_map/ppermute | solution.py:492
  91.9 16.0 %collective-permute-start.4 = (bf16[2,48,512]{2,1,0:T(8,128)(2,1)}, bf16[2,48,512]{2,1,0:T(8,128)(2,1)S(1)}, u32[]{:S(2)}, u32[]{:S(2)}) collective-permute-start(bf16[2,48,512]{2,1,0:T(8,128)(2,1)} %get-tuple-element.43), channel_id=1, source_target_pairs={{0,6},{1,7},{2,4},{3,5},{4,2},{5,3},{6,0},{7,1},{8,14},{9,15},{10,... | collective-permute-start | bytes 294920 | tf_op jit(solution)/shard_map/ppermute | solution.py:492
  91.9 28.4 %collective-permute-start.12 = (bf16[2,48,512]{2,1,0:T(8,128)(2,1)}, bf16[2,48,512]{2,1,0:T(8,128)(2,1)S(1)}, u32[]{:S(2)}, u32[]{:S(2)}) collective-permute-start(bf16[2,48,512]{2,1,0:T(8,128)(2,1)} %get-tuple-element.55), channel_id=1, source_target_pairs={{0,8},{1,9},{2,10},{3,11},{4,12},{5,13},{6,14},{7,15},{8,0},{9,1},... | collective-permute-start | bytes 294920 | tf_op jit(solution)/shard_map/ppermute | solution.py:492
  94.8 25.6 %collective-permute-start.13 = (bf16[2,48,512]{2,1,0:T(8,128)(2,1)}, bf16[2,48,512]{2,1,0:T(8,128)(2,1)S(1)}, u32[]{:S(2)}, u32[]{:S(2)}) collective-permute-start(bf16[2,48,512]{2,1,0:T(8,128)(2,1)} %get-tuple-element.56), channel_id=1, source_target_pairs={{0,10},{1,11},{2,8},{3,9},{4,14},{5,15},{6,12},{7,13},{8,2},{9,3},... | collective-permute-start | bytes 294920 | tf_op jit(solution)/shard_map/ppermute | solution.py:492
  96.2 34.3 %copy-start.3 = (bf16[2,48,512]{2,1,0:T(8,128)(2,1)}, bf16[2,48,512]{2,1,0:T(8,128)(2,1)S(1)}, u32[]{:S(2)}) copy-start(bf16[2,48,512]{2,1,0:T(8,128)(2,1)S(1)} %collective-permute-done.2.refs_1_) | copy-start | bytes 294916
  96.2 26.6 %collective-permute-start.14 = (bf16[2,48,512]{2,1,0:T(8,128)(2,1)}, bf16[2,48,512]{2,1,0:T(8,128)(2,1)S(1)}, u32[]{:S(2)}, u32[]{:S(2)}) collective-permute-start(bf16[2,48,512]{2,1,0:T(8,128)(2,1)} %get-tuple-element.57), channel_id=1, source_target_pairs={{0,12},{1,13},{2,14},{3,15},{4,8},{5,9},{6,10},{7,11},{8,4},{9,5},... | collective-permute-start | bytes 294920 | tf_op jit(solution)/shard_map/ppermute | solution.py:492
  99.5 31.0 %copy-start.4 = (bf16[2,48,512]{2,1,0:T(8,128)(2,1)}, bf16[2,48,512]{2,1,0:T(8,128)(2,1)S(1)}, u32[]{:S(2)}) copy-start(bf16[2,48,512]{2,1,0:T(8,128)(2,1)S(1)} %collective-permute-done.3.refs_2_) | copy-start | bytes 294916
  99.5 23.4 %collective-permute-start.15 = (bf16[2,48,512]{2,1,0:T(8,128)(2,1)}, bf16[2,48,512]{2,1,0:T(8,128)(2,1)S(1)}, u32[]{:S(2)}, u32[]{:S(2)}) collective-permute-start(bf16[2,48,512]{2,1,0:T(8,128)(2,1)} %get-tuple-element.58), channel_id=1, source_target_pairs={{0,14},{1,15},{2,12},{3,13},{4,10},{5,11},{6,8},{7,9},{8,6},{9,7},... | collective-permute-start | bytes 294920 | tf_op jit(solution)/shard_map/ppermute | solution.py:492
  108.8 21.8 %copy-start.5 = (bf16[2,48,512]{2,1,0:T(8,128)(2,1)}, bf16[2,48,512]{2,1,0:T(8,128)(2,1)S(1)}, u32[]{:S(2)}) copy-start(bf16[2,48,512]{2,1,0:T(8,128)(2,1)S(1)} %collective-permute-done.4.refs_3_) | copy-start | bytes 294916
  119.3 6.9 %collective-permute-start.5 = (bf16[2,48,512]{2,1,0:T(8,128)(2,1)}, bf16[2,48,512]{2,1,0:T(8,128)(2,1)S(1)}, u32[]{:S(2)}, u32[]{:S(2)}) collective-permute-start(bf16[2,48,512]{2,1,0:T(8,128)(2,1)} %get-tuple-element.46), channel_id=1, source_target_pairs={{0,2},{1,3},{2,0},{3,1},{4,6},{5,7},{6,4},{7,5},{8,10},{9,11},{10,... | collective-permute-start | bytes 294920 | tf_op jit(solution)/shard_map/ppermute | solution.py:492
  120.3 5.9 %collective-permute-start.6 = (bf16[2,48,512]{2,1,0:T(8,128)(2,1)}, bf16[2,48,512]{2,1,0:T(8,128)(2,1)S(1)}, u32[]{:S(2)}, u32[]{:S(2)}) collective-permute-start(bf16[2,48,512]{2,1,0:T(8,128)(2,1)} %get-tuple-element.47), channel_id=1, source_target_pairs={{0,4},{1,5},{2,6},{3,7},{4,0},{5,1},{6,2},{7,3},{8,12},{9,13},{10,... | collective-permute-start | bytes 294920 | tf_op jit(solution)/shard_map/ppermute | solution.py:492
  120.4 13.0 %collective-permute-start.7 = (bf16[2,48,512]{2,1,0:T(8,128)(2,1)}, bf16[2,48,512]{2,1,0:T(8,128)(2,1)S(1)}, u32[]{:S(2)}, u32[]{:S(2)}) collective-permute-start(bf16[2,48,512]{2,1,0:T(8,128)(2,1)} %get-tuple-element.48), channel_id=1, source_target_pairs={{0,6},{1,7},{2,4},{3,5},{4,2},{5,3},{6,0},{7,1},{8,14},{9,15},{10,... | collective-permute-start | bytes 294920 | tf_op jit(solution)/shard_map/ppermute | solution.py:492
  122.8 10.5 %collective-permute-start.8 = (bf16[2,48,512]{2,1,0:T(8,128)(2,1)}, bf16[2,48,512]{2,1,0:T(8,128)(2,1)S(1)}, u32[]{:S(2)}, u32[]{:S(2)}) collective-permute-start(bf16[2,48,512]{2,1,0:T(8,128)(2,1)} %get-tuple-element.49), channel_id=1, source_target_pairs={{0,8},{1,9},{2,10},{3,11},{4,12},{5,13},{6,14},{7,15},{8,0},{9,1},... | collective-permute-start | bytes 294920 | tf_op jit(solution)/shard_map/ppermute | solution.py:492
  122.9 12.7 %collective-permute-start.9 = (bf16[2,48,512]{2,1,0:T(8,128)(2,1)}, bf16[2,48,512]{2,1,0:T(8,128)(2,1)S(1)}, u32[]{:S(2)}, u32[]{:S(2)}) collective-permute-start(bf16[2,48,512]{2,1,0:T(8,128)(2,1)} %get-tuple-element.50), channel_id=1, source_target_pairs={{0,10},{1,11},{2,8},{3,9},{4,14},{5,15},{6,12},{7,13},{8,2},{9,3},... | collective-permute-start | bytes 294920 | tf_op jit(solution)/shard_map/ppermute | solution.py:492
  126.2 9.4 %collective-permute-start.10 = (bf16[2,48,512]{2,1,0:T(8,128)(2,1)}, bf16[2,48,512]{2,1,0:T(8,128)(2,1)S(1)}, u32[]{:S(2)}, u32[]{:S(2)}) collective-permute-start(bf16[2,48,512]{2,1,0:T(8,128)(2,1)} %get-tuple-element.51), channel_id=1, source_target_pairs={{0,12},{1,13},{2,14},{3,15},{4,8},{5,9},{6,10},{7,11},{8,4},{9,5},... | collective-permute-start | bytes 294920 | tf_op jit(solution)/shard_map/ppermute | solution.py:492
  126.2 9.3 %collective-permute-start.11 = (bf16[2,48,512]{2,1,0:T(8,128)(2,1)}, bf16[2,48,512]{2,1,0:T(8,128)(2,1)S(1)}, u32[]{:S(2)}, u32[]{:S(2)}) collective-permute-start(bf16[2,48,512]{2,1,0:T(8,128)(2,1)} %get-tuple-element.52), channel_id=1, source_target_pairs={{0,14},{1,15},{2,12},{3,13},{4,10},{5,11},{6,8},{7,9},{8,6},{9,7},... | collective-permute-start | bytes 294920 | tf_op jit(solution)/shard_map/ppermute | solution.py:492
  (16 other events, 67.6 us)

commit v7 on v6

--- a/solution.py
+++ b/solution.py
@@ -32,6 +32,15 @@
     return half + half * lax.erf(half)
 
 
+def exact_dot(values, weight):
+    count = values.shape[0]
+    high = values.astype(BF16).astype(F32)
+    middle = (values - high).astype(BF16).astype(F32)
+    parts = jnp.concatenate([high, middle, values - high - middle], axis=0).astype(BF16)
+    sums = jnp.dot(parts, weight, preferred_element_type=F32)
+    return sums[:count] + sums[count : 2 * count] + sums[2 * count :]
+
+
 def mbconv_kernel(
     x_ref, before_ref, after_ref, w_ref, b_ref, dw_ref, db_ref, down_ref, shift_ref,
     act_ref, part_ref, total_ref, tap_ref, *hidden_refs,
@@ -80,12 +89,7 @@
                 total = depth(s, c, total)
         total_ref[:, s * sub : (s + 1) * sub] = total
     pooled = jnp.sum(total_ref[...], axis=0, keepdims=True)
-    part = jnp.dot(
-        jnp.broadcast_to(pooled, (8, lanes)),
-        down_ref[...].astype(F32),
-        precision=lax.Precision.HIGHEST,
-        preferred_element_type=F32,
-    )[None]
+    part = exact_dot(jnp.broadcast_to(pooled, (8, lanes)), down_ref[...])[None]
 
     @pl.when(pl.program_id(0) == 0)
     def _():
@@ -235,13 +239,7 @@
     def _():
         squeezed = jnp.sum(part_ref[...], axis=0) * scale
         squeezed = squeezed * jax.nn.sigmoid(squeezed)
-        gate = jnp.dot(
-            squeezed,
-            up_ref[...].astype(F32),
-            precision=lax.Precision.HIGHEST,
-            preferred_element_type=F32,
-        )
-        gate_ref[...] = jax.nn.sigmoid(gate) * ROOT_HALF
+        gate_ref[...] = jax.nn.sigmoid(exact_dot(squeezed, up_ref[...])) * ROOT_HALF
         prepare(in_ref, scratch[0], scratch[1])
 
     gated = act_ref[...].reshape(cols * rows, expanded).astype(F32) * gate_ref[0:1]

time: 140 us -> 139 us (level)
  transfers between devices with their start and end apart: 19 -> 19, of which waited for: 4 -> 5; matrix products, arithmetic and copies ran while one was open for 8% -> 8% of each run, Pallas kernels for 27% -> 27%
where the time goes in v7:
time: 139 us
  Pallas kernels  66.9 us (48%)
  starting transfers between devices  40.1 us (29%)
  waiting for transfers between devices  15.6 us (11%)
  local copies, waits for them, and re-layouts  9.35 us (7%)
  matrix products  5.24 us (4%)
    pallas_call x2, Pallas kernels, block_stage(): pl.pallas_call(functools.partial(block_kernel, scale, split), name='block...  25.9 us
    ppermute x14, starting transfers between devices, exchange(): lax.ppermute(pieces[s], 'lon', [(j * per + r, (j ^ s) * per + r) for j in...  22.9 us
    pallas_call x2, Pallas kernels, grid_stage(): pl.pallas_call(functools.partial(grid_kernel, split_in, split_out), name=...  21 us
    pallas_call x1, Pallas kernels, mbconv(): pl.pallas_call(mbconv_kernel, name='mbconv', grid=(expanded // LANES,), i...  14.4 us
    all_to_all x2, waiting for transfers between devices, exchange(): lax.all_to_all(pieces[0], 'lon', 0, 0, axis_index_groups=groups, tiled=True)  9.81 us
    all_to_all x2, starting transfers between devices, exchange(): lax.all_to_all(pieces[0], 'lon', 0, 0, axis_index_groups=groups, tiled=True)  7.49 us
    unnamed x45, local copies, waits for them, and re-layouts  6.3 us
    pallas_call x2, Pallas kernels, merge_stage(): pl.pallas_call(functools.partial(merge_kernel, split), name='merge_stage'...  5.58 us
  transfers between devices with their start and end apart: 19, of which 5 were waited for; matrix products, arithmetic and copies ran while one was open for 8% of the time, Pallas kernels for 27%

profile of v7, /device:TPU:0, one launch (start us, length us, event | category | flops | bytes accessed | tf_op | source)
XLA Modules:
  0.0 138.6 jit_solution(16261710129276955749)
XLA Ops:
  1.8 5.1 %collective-permute-start.1 = (bf16[1,48,512]{2,1,0:T(8,128)(2,1)S(1)}, bf16[1,48,512]{2,1,0:T(8,128)(2,1)S(1)}, u32[]{:S(2)}, u32[]{:S(2)}) collective-permute-start(bf16[1,48,512]{2,1,0:T(8,128)(2,1)S(1)} %bitcast.28), channel_id=1, source_target_pairs={{1,0},{2,1},{3,2},{4,3},{5,4},{6,5},{7,6},{8,7},{9,8},{10,9},{11,1... | collective-permute-start | bytes 147464 | tf_op jit(solution)/shard_map/ppermute | solution.py:464
  7.0 3.4 %copy.27 = bf16[48,32,512]{2,0,1:T(8,128)(2,1)} copy(bf16[48,32,512]{2,1,0:T(8,128)(2,1)} %param.17) | data formatting | bytes 3145728 | tf_op args[0]
  11.0 14.4 %mbconv.1 = (bf16[32,48,2048]{2,1,0:T(8,128)(2,1)}, f32[16,8,128]{2,1,0:T(8,128)}) custom-call(bf16[32,48,512]{2,1,0:T(8,128)(2,1)} %bitcast.24, bf16[1,48,512]{2,1,0:T(8,128)(2,1)} %copy-done.17, bf16[1,48,512]{2,1,0:T(8,128)(2,1)} %copy-done.18, bf16[512,2048]{1,0:T(8,128)(2,1)} %w_ref.1, f32[1,2048]{1,0:T(1,128)} %bitcast.33, f32[9,2048]{1,0:T(8,128)} %dw_ref.1, ...), custom_call_target="tpu_custom_call" | custom-call | flops 12884901888 | bytes 20000000 | tf_op jit(solution)/shard_map/mbconv/pallas_call | solution.py:118
  25.4 4.1 %all-to-all-start = ((f32[16,8,128]{2,1,0:T(8,128)}), f32[16,8,128]{2,1,0:T(8,128)S(1)}, u32[]{:S(2)}, u32[]{:S(2)}) async-start(f32[16,8,128]{2,1,0:T(8,128)} %get-tuple-element.33), calls=%async_computation | async-start | bytes 131072 | tf_op jit(solution)/shard_map/all_to_all | solution.py:474
  29.5 2.6 %fusion.4 = f32[64,16,64]{2,1,0:T(8,128)S(1)} fusion(s32[64,64]{1,0:T(8,128)S(1)} %add_add_fusion, f32[225,16]{0,1:T(8,128)S(1)} %copy-done.19), kind=kOutput, calls=%fused_computation.6 | convolution fusion | flops 177872400 | bytes 292928 | tf_op jit(solution)/shard_map/jir,rh->jhi/dot_general | solution.py:414
  33.0 3.4 %all-to-all-done.part_ref = f32[16,8,128]{2,1,0:T(8,128)S(1)} async-done(((f32[16,8,128]{2,1,0:T(8,128)}), f32[16,8,128]{2,1,0:T(8,128)S(1)}, u32[]{:S(2)}, u32[]{:S(2)}) %all-to-all-start) | async-done | bytes 65568 | tf_op jit(solution)/shard_map/all_to_all | solution.py:474
  37.0 13.0 %block_stage.3 = bf16[8,2,48,512]{3,2,1,0:T(8,128)(2,1)} custom-call(s32[1]{0:T(128)} %constant.136.clone.1.me_ref, bf16[32,48,2048]{2,1,0:T(8,128)(2,1)} %get-tuple-element.32.act_ref, bf16[32,48,512]{2,1,0:T(8,128)(2,1)} %bitcast.25, f32[16,8,128]{2,1,0:T(8,128)} %copy-done.2, bf16[128,2048]{1,0:T(8,128)(2,1)} %up_ref.3, bf16[2048,512]{1,0:T(8,128)(2,1)} %proj_ref.3, ...), custom_call_target="tpu_custom_call" | custom-call | flops 1000000 | bytes 100000 | tf_op jit(solution)/shard_map/block_stage/pallas_call | solution.py:328
  50.0 3.7 %all-to-all-start.2 = ((bf16[8,2,48,512]{3,2,1,0:T(8,128)(2,1)}), bf16[8,2,48,512]{3,2,1,0:T(8,128)(2,1)S(1)}, u32[]{:S(2)}, u32[]{:S(2)}) async-start(bf16[8,2,48,512]{3,2,1,0:T(8,128)(2,1)} %block_stage.3), calls=%async_computation.2 | async-start | bytes 1572864 | tf_op jit(solution)/shard_map/all_to_all | solution.py:485
  53.7 2.6 %fusion.5 = f32[64,16,64]{2,1,0:T(8,128)S(1)} fusion(s32[64,64]{1,0:T(8,128)S(1)} %add_add_fusion, f32[225,16]{0,1:T(8,128)S(1)} %copy-done.20), kind=kOutput, calls=%fused_computation.7 | convolution fusion | flops 177872400 | bytes 292928 | tf_op jit(solution)/shard_map/jir,rh->jhi/dot_general | solution.py:414
  58.3 13.0 %block_stage.2 = bf16[8,2,48,512]{3,2,1,0:T(8,128)(2,1)} custom-call(s32[1]{0:T(128)} %constant.136.clone.1.me_ref, bf16[32,48,2048]{2,1,0:T(8,128)(2,1)} %get-tuple-element.32.act_ref, bf16[32,48,512]{2,1,0:T(8,128)(2,1)} %bitcast.26, f32[16,8,128]{2,1,0:T(8,128)} %copy-done.2, bf16[128,2048]{1,0:T(8,128)(2,1)} %up_ref.3, bf16[2048,512]{1,0:T(8,128)(2,1)} %proj_ref.3, ...), custom_call_target="tpu_custom_call" | custom-call | flops 1000000 | bytes 100000 | tf_op jit(solution)/shard_map/block_stage/pallas_call | solution.py:328
  71.3 2.3 %all-to-all-done.2.refs_0_ = bf16[8,2,48,512]{3,2,1,0:T(8,128)(2,1)S(1)} async-done(((bf16[8,2,48,512]{3,2,1,0:T(8,128)(2,1)}), bf16[8,2,48,512]{3,2,1,0:T(8,128)(2,1)S(1)}, u32[]{:S(2)}, u32[]{:S(2)}) %all-to-all-start.2) | async-done | bytes 786464 | tf_op jit(solution)/shard_map/all_to_all | solution.py:485
  73.6 3.8 %all-to-all-start.1 = ((bf16[8,2,48,512]{3,2,1,0:T(8,128)(2,1)}), bf16[8,2,48,512]{3,2,1,0:T(8,128)(2,1)S(1)}, u32[]{:S(2)}, u32[]{:S(2)}) async-start(bf16[8,2,48,512]{3,2,1,0:T(8,128)(2,1)} %block_stage.2), calls=%async_computation.1 | async-start | bytes 1572864 | tf_op jit(solution)/shard_map/all_to_all | solution.py:485
  77.4 10.5 %grid_stage.2 = (bf16[2,48,512]{2,1,0:T(8,128)(2,1)}, bf16[2,48,512]{2,1,0:T(8,128)(2,1)}, bf16[2,48,512]{2,1,0:T(8,128)(2,1)}, bf16[2,48,512]{2,1,0:T(8,128)(2,...) custom-call(s32[1]{0:T(128)} %bitcast.me_ref, ...), custom_call_target="tpu_custom_call" | custom-call | flops 1000000 | bytes 100000 | tf_op jit(solution)/shard_map/grid_stage/pallas_call | solution.py:359
  87.9 1.8 %collective-permute-start.2 = (bf16[2,48,512]{2,1,0:T(8,128)(2,1)}, bf16[2,48,512]{2,1,0:T(8,128)(2,1)S(1)}, u32[]{:S(2)}, u32[]{:S(2)}) collective-permute-start(bf16[2,48,512]{2,1,0:T(8,128)(2,1)} %get-tuple-element.41), channel_id=1, source_target_pairs={{0,2},{1,3},{2,0},{3,1},{4,6},{5,7},{6,4},{7,5},{8,10},{9,11},{10,... | collective-permute-start | bytes 294920 | tf_op jit(solution)/shard_map/ppermute | solution.py:490
  91.4 2.7 %collective-permute-start.12 = (bf16[2,48,512]{2,1,0:T(8,128)(2,1)}, bf16[2,48,512]{2,1,0:T(8,128)(2,1)S(1)}, u32[]{:S(2)}, u32[]{:S(2)}) collective-permute-start(bf16[2,48,512]{2,1,0:T(8,128)(2,1)} %get-tuple-element.55), channel_id=1, source_target_pairs={{0,8},{1,9},{2,10},{3,11},{4,12},{5,13},{6,14},{7,15},{8,0},{9,1},... | collective-permute-start | bytes 294920 | tf_op jit(solution)/shard_map/ppermute | solution.py:490
  95.6 3.3 %collective-permute-start.14 = (bf16[2,48,512]{2,1,0:T(8,128)(2,1)}, bf16[2,48,512]{2,1,0:T(8,128)(2,1)S(1)}, u32[]{:S(2)}, u32[]{:S(2)}) collective-permute-start(bf16[2,48,512]{2,1,0:T(8,128)(2,1)} %get-tuple-element.57), channel_id=1, source_target_pairs={{0,12},{1,13},{2,14},{3,15},{4,8},{5,9},{6,10},{7,11},{8,4},{9,5},... | collective-permute-start | bytes 294920 | tf_op jit(solution)/shard_map/ppermute | solution.py:490
  99.7 7.5 %all-to-all-done.1.refs_0_ = bf16[8,2,48,512]{3,2,1,0:T(8,128)(2,1)S(1)} async-done(((bf16[8,2,48,512]{3,2,1,0:T(8,128)(2,1)}), bf16[8,2,48,512]{3,2,1,0:T(8,128)(2,1)S(1)}, u32[]{:S(2)}, u32[]{:S(2)}) %all-to-all-start.1) | async-done | bytes 786464 | tf_op jit(solution)/shard_map/all_to_all | solution.py:485
  108.1 10.5 %grid_stage.3 = (bf16[2,48,512]{2,1,0:T(8,128)(2,1)}, bf16[2,48,512]{2,1,0:T(8,128)(2,1)}, bf16[2,48,512]{2,1,0:T(8,128)(2,1)}, bf16[2,48,512]{2,1,0:T(8,128)(2,...) custom-call(s32[1]{0:T(128)} %bitcast.me_ref, ...), custom_call_target="tpu_custom_call" | custom-call | flops 1000000 | bytes 100000 | tf_op jit(solution)/shard_map/grid_stage/pallas_call | solution.py:359
  118.8 3.4 %collective-permute-start.7 = (bf16[2,48,512]{2,1,0:T(8,128)(2,1)}, bf16[2,48,512]{2,1,0:T(8,128)(2,1)S(1)}, u32[]{:S(2)}, u32[]{:S(2)}) collective-permute-start(bf16[2,48,512]{2,1,0:T(8,128)(2,1)} %get-tuple-element.48), channel_id=1, source_target_pairs={{0,6},{1,7},{2,4},{3,5},{4,2},{5,3},{6,0},{7,1},{8,14},{9,15},{10,... | collective-permute-start | bytes 294920 | tf_op jit(solution)/shard_map/ppermute | solution.py:490
  122.2 2.4 %collective-permute-start.9 = (bf16[2,48,512]{2,1,0:T(8,128)(2,1)}, bf16[2,48,512]{2,1,0:T(8,128)(2,1)S(1)}, u32[]{:S(2)}, u32[]{:S(2)}) collective-permute-start(bf16[2,48,512]{2,1,0:T(8,128)(2,1)} %get-tuple-element.50), channel_id=1, source_target_pairs={{0,10},{1,11},{2,8},{3,9},{4,14},{5,15},{6,12},{7,13},{8,2},{9,3},... | collective-permute-start | bytes 294920 | tf_op jit(solution)/shard_map/ppermute | solution.py:490
  124.7 5.1 %collective-permute-start.11 = (bf16[2,48,512]{2,1,0:T(8,128)(2,1)}, bf16[2,48,512]{2,1,0:T(8,128)(2,1)S(1)}, u32[]{:S(2)}, u32[]{:S(2)}) collective-permute-start(bf16[2,48,512]{2,1,0:T(8,128)(2,1)} %get-tuple-element.52), channel_id=1, source_target_pairs={{0,14},{1,15},{2,12},{3,13},{4,10},{5,11},{6,8},{7,9},{8,6},{9,7},... | collective-permute-start | bytes 294920 | tf_op jit(solution)/shard_map/ppermute | solution.py:490
  129.9 2.8 %merge_stage.2.refs_9_ = bf16[48,32,512]{2,1,0:T(8,128)(2,1)} custom-call(s32[1]{0:T(128)} %bitcast.me_ref, bf16[2,48,512]{2,1,0:T(8,128)(2,1)} %get-tuple-element.54.refs_0_, bf16[2,48,512]{2,1,0:T(8,128)(2,1)} %copy-done.3, bf16[2,48,512]{2,1,0:T(8,128)(2,1)} %copy-done.4, bf16[2,48,512]{2,1,0:T(8,128)(2,1)} %copy-done.5, bf16[2,48,512]{2,1,0:T(8,128)(2,1)} %copy-done.6, ...), custom_call_target="tpu_custom_call" | custom-call | flops 1000000 | bytes 100000 | tf_op jit(solution)/shard_map/merge_stage/pallas_call | solution.py:386
  133.3 1.8 %collective-permute-done.9.refs_5_ = bf16[2,48,512]{2,1,0:T(8,128)(2,1)S(1)} collective-permute-done((bf16[2,48,512]{2,1,0:T(8,128)(2,1)}, bf16[2,48,512]{2,1,0:T(8,128)(2,1)S(1)}, u32[]{:S(2)}, u32[]{:S(2)}) %collective-permute-start.9) | collective-permute-done | bytes 98336 | tf_op jit(solution)/shard_map/ppermute | solution.py:490
  135.9 2.8 %merge_stage.3 = bf16[48,32,512]{2,1,0:T(8,128)(2,1)} custom-call(s32[1]{0:T(128)} %bitcast.me_ref, bf16[2,48,512]{2,1,0:T(8,128)(2,1)} %get-tuple-element.45.refs_0_, bf16[2,48,512]{2,1,0:T(8,128)(2,1)} %copy-done.10, bf16[2,48,512]{2,1,0:T(8,128)(2,1)} %copy-done.11, bf16[2,48,512]{2,1,0:T(8,128)(2,1)} %copy-done.12, ...), custom_call_target="tpu_custom_call", output_to_operand_aliasing={{}: (10, {})} | custom-call | flops 1000000 | bytes 100000 | tf_op jit(solution)/shard_map/merge_stage/pallas_call | solution.py:386
  (76 shorter events, 12.5 us)
Async XLA Ops:
  1.3 9.1 %collective-permute-start = (bf16[1,48,512]{2,1,0:T(8,128)(2,1)S(1)}, bf16[1,48,512]{2,1,0:T(8,128)(2,1)S(1)}, u32[]{:S(2)}, u32[]{:S(2)}) collective-permute-start(bf16[1,48,512]{2,1,0:T(8,128)(2,1)S(1)} %bitcast.27), channel_id=1, source_target_pairs={{0,1},{1,2},{2,3},{3,4},{4,5},{5,6},{6,7},{7,8},{8,9},{9,10},{10,1... | collective-permute-start | bytes 147464 | tf_op jit(solution)/shard_map/ppermute | solution.py:459
  1.8 8.6 %collective-permute-start.1 = (bf16[1,48,512]{2,1,0:T(8,128)(2,1)S(1)}, bf16[1,48,512]{2,1,0:T(8,128)(2,1)S(1)}, u32[]{:S(2)}, u32[]{:S(2)}) collective-permute-start(bf16[1,48,512]{2,1,0:T(8,128)(2,1)S(1)} %bitcast.28), channel_id=1, source_target_pairs={{1,0},{2,1},{3,2},{4,3},{5,4},{6,5},{7,6},{8,7},{9,8},{10,9},{11,1... | collective-permute-start | bytes 147464 | tf_op jit(solution)/shard_map/ppermute | solution.py:464
  11.0 18.5 %copy-start.19 = (f32[225,16]{0,1:T(8,128)S(1)}, f32[225,16]{0,1:T(8,128)}, u32[]{:S(2)}) copy-start(f32[225,16]{0,1:T(8,128)} %param.28) | copy-start | bytes 43204
  25.4 11.0 %all-to-all-start = ((f32[16,8,128]{2,1,0:T(8,128)}), f32[16,8,128]{2,1,0:T(8,128)S(1)}, u32[]{:S(2)}, u32[]{:S(2)}) async-start(f32[16,8,128]{2,1,0:T(8,128)} %get-tuple-element.33), calls=%async_computation | async-start | bytes 131072 | tf_op jit(solution)/shard_map/all_to_all | solution.py:474
  37.0 16.7 %copy-start.20 = (f32[225,16]{0,1:T(8,128)S(1)}, f32[225,16]{0,1:T(8,128)}, u32[]{:S(2)}) copy-start(f32[225,16]{0,1:T(8,128)} %param.32) | copy-start | bytes 43204
  50.0 23.6 %all-to-all-start.2 = ((bf16[8,2,48,512]{3,2,1,0:T(8,128)(2,1)}), bf16[8,2,48,512]{3,2,1,0:T(8,128)(2,1)S(1)}, u32[]{:S(2)}, u32[]{:S(2)}) async-start(bf16[8,2,48,512]{3,2,1,0:T(8,128)(2,1)} %block_stage.3), calls=%async_computation.2 | async-start | bytes 1572864 | tf_op jit(solution)/shard_map/all_to_all | solution.py:485
  73.6 33.6 %all-to-all-start.1 = ((bf16[8,2,48,512]{3,2,1,0:T(8,128)(2,1)}), bf16[8,2,48,512]{3,2,1,0:T(8,128)(2,1)S(1)}, u32[]{:S(2)}, u32[]{:S(2)}) async-start(bf16[8,2,48,512]{3,2,1,0:T(8,128)(2,1)} %block_stage.2), calls=%async_computation.1 | async-start | bytes 1572864 | tf_op jit(solution)/shard_map/all_to_all | solution.py:485
  87.9 7.7 %collective-permute-start.2 = (bf16[2,48,512]{2,1,0:T(8,128)(2,1)}, bf16[2,48,512]{2,1,0:T(8,128)(2,1)S(1)}, u32[]{:S(2)}, u32[]{:S(2)}) collective-permute-start(bf16[2,48,512]{2,1,0:T(8,128)(2,1)} %get-tuple-element.41), channel_id=1, source_target_pairs={{0,2},{1,3},{2,0},{3,1},{4,6},{5,7},{6,4},{7,5},{8,10},{9,11},{10,... | collective-permute-start | bytes 294920 | tf_op jit(solution)/shard_map/ppermute | solution.py:490
  89.7 9.1 %collective-permute-start.3 = (bf16[2,48,512]{2,1,0:T(8,128)(2,1)}, bf16[2,48,512]{2,1,0:T(8,128)(2,1)S(1)}, u32[]{:S(2)}, u32[]{:S(2)}) collective-permute-start(bf16[2,48,512]{2,1,0:T(8,128)(2,1)} %get-tuple-element.42), channel_id=1, source_target_pairs={{0,4},{1,5},{2,6},{3,7},{4,0},{5,1},{6,2},{7,3},{8,12},{9,13},{10,... | collective-permute-start | bytes 294920 | tf_op jit(solution)/shard_map/ppermute | solution.py:490
  91.2 16.0 %collective-permute-start.4 = (bf16[2,48,512]{2,1,0:T(8,128)(2,1)}, bf16[2,48,512]{2,1,0:T(8,128)(2,1)S(1)}, u32[]{:S(2)}, u32[]{:S(2)}) collective-permute-start(bf16[2,48,512]{2,1,0:T(8,128)(2,1)} %get-tuple-element.43), channel_id=1, source_target_pairs={{0,6},{1,7},{2,4},{3,5},{4,2},{5,3},{6,0},{7,1},{8,14},{9,15},{10,... | collective-permute-start | bytes 294920 | tf_op jit(solution)/shard_map/ppermute | solution.py:490
  91.4 27.2 %collective-permute-start.12 = (bf16[2,48,512]{2,1,0:T(8,128)(2,1)}, bf16[2,48,512]{2,1,0:T(8,128)(2,1)S(1)}, u32[]{:S(2)}, u32[]{:S(2)}) collective-permute-start(bf16[2,48,512]{2,1,0:T(8,128)(2,1)} %get-tuple-element.55), channel_id=1, source_target_pairs={{0,8},{1,9},{2,10},{3,11},{4,12},{5,13},{6,14},{7,15},{8,0},{9,1},... | collective-permute-start | bytes 294920 | tf_op jit(solution)/shard_map/ppermute | solution.py:490
  94.1 24.6 %collective-permute-start.13 = (bf16[2,48,512]{2,1,0:T(8,128)(2,1)}, bf16[2,48,512]{2,1,0:T(8,128)(2,1)S(1)}, u32[]{:S(2)}, u32[]{:S(2)}) collective-permute-start(bf16[2,48,512]{2,1,0:T(8,128)(2,1)} %get-tuple-element.56), channel_id=1, source_target_pairs={{0,10},{1,11},{2,8},{3,9},{4,14},{5,15},{6,12},{7,13},{8,2},{9,3},... | collective-permute-start | bytes 294920 | tf_op jit(solution)/shard_map/ppermute | solution.py:490
  95.6 34.2 %copy-start.3 = (bf16[2,48,512]{2,1,0:T(8,128)(2,1)}, bf16[2,48,512]{2,1,0:T(8,128)(2,1)S(1)}, u32[]{:S(2)}) copy-start(bf16[2,48,512]{2,1,0:T(8,128)(2,1)S(1)} %collective-permute-done.2.refs_1_) | copy-start | bytes 294916
  95.6 26.6 %collective-permute-start.14 = (bf16[2,48,512]{2,1,0:T(8,128)(2,1)}, bf16[2,48,512]{2,1,0:T(8,128)(2,1)S(1)}, u32[]{:S(2)}, u32[]{:S(2)}) collective-permute-start(bf16[2,48,512]{2,1,0:T(8,128)(2,1)} %get-tuple-element.57), channel_id=1, source_target_pairs={{0,12},{1,13},{2,14},{3,15},{4,8},{5,9},{6,10},{7,11},{8,4},{9,5},... | collective-permute-start | bytes 294920 | tf_op jit(solution)/shard_map/ppermute | solution.py:490
  98.9 31.0 %copy-start.4 = (bf16[2,48,512]{2,1,0:T(8,128)(2,1)}, bf16[2,48,512]{2,1,0:T(8,128)(2,1)S(1)}, u32[]{:S(2)}) copy-start(bf16[2,48,512]{2,1,0:T(8,128)(2,1)S(1)} %collective-permute-done.3.refs_2_) | copy-start | bytes 294916
  98.9 23.3 %collective-permute-start.15 = (bf16[2,48,512]{2,1,0:T(8,128)(2,1)}, bf16[2,48,512]{2,1,0:T(8,128)(2,1)S(1)}, u32[]{:S(2)}, u32[]{:S(2)}) collective-permute-start(bf16[2,48,512]{2,1,0:T(8,128)(2,1)} %get-tuple-element.58), channel_id=1, source_target_pairs={{0,14},{1,15},{2,12},{3,13},{4,10},{5,11},{6,8},{7,9},{8,6},{9,7},... | collective-permute-start | bytes 294920 | tf_op jit(solution)/shard_map/ppermute | solution.py:490
  108.1 21.8 %copy-start.5 = (bf16[2,48,512]{2,1,0:T(8,128)(2,1)}, bf16[2,48,512]{2,1,0:T(8,128)(2,1)S(1)}, u32[]{:S(2)}) copy-start(bf16[2,48,512]{2,1,0:T(8,128)(2,1)S(1)} %collective-permute-done.4.refs_3_) | copy-start | bytes 294916
  118.6 6.0 %collective-permute-start.5 = (bf16[2,48,512]{2,1,0:T(8,128)(2,1)}, bf16[2,48,512]{2,1,0:T(8,128)(2,1)S(1)}, u32[]{:S(2)}, u32[]{:S(2)}) collective-permute-start(bf16[2,48,512]{2,1,0:T(8,128)(2,1)} %get-tuple-element.46), channel_id=1, source_target_pairs={{0,2},{1,3},{2,0},{3,1},{4,6},{5,7},{6,4},{7,5},{8,10},{9,11},{10,... | collective-permute-start | bytes 294920 | tf_op jit(solution)/shard_map/ppermute | solution.py:490
  118.7 6.0 %collective-permute-start.6 = (bf16[2,48,512]{2,1,0:T(8,128)(2,1)}, bf16[2,48,512]{2,1,0:T(8,128)(2,1)S(1)}, u32[]{:S(2)}, u32[]{:S(2)}) collective-permute-start(bf16[2,48,512]{2,1,0:T(8,128)(2,1)} %get-tuple-element.47), channel_id=1, source_target_pairs={{0,4},{1,5},{2,6},{3,7},{4,0},{5,1},{6,2},{7,3},{8,12},{9,13},{10,... | collective-permute-start | bytes 294920 | tf_op jit(solution)/shard_map/ppermute | solution.py:490
  118.8 13.9 %collective-permute-start.7 = (bf16[2,48,512]{2,1,0:T(8,128)(2,1)}, bf16[2,48,512]{2,1,0:T(8,128)(2,1)S(1)}, u32[]{:S(2)}, u32[]{:S(2)}) collective-permute-start(bf16[2,48,512]{2,1,0:T(8,128)(2,1)} %get-tuple-element.48), channel_id=1, source_target_pairs={{0,6},{1,7},{2,4},{3,5},{4,2},{5,3},{6,0},{7,1},{8,14},{9,15},{10,... | collective-permute-start | bytes 294920 | tf_op jit(solution)/shard_map/ppermute | solution.py:490
  122.2 11.1 %collective-permute-start.8 = (bf16[2,48,512]{2,1,0:T(8,128)(2,1)}, bf16[2,48,512]{2,1,0:T(8,128)(2,1)S(1)}, u32[]{:S(2)}, u32[]{:S(2)}) collective-permute-start(bf16[2,48,512]{2,1,0:T(8,128)(2,1)} %get-tuple-element.49), channel_id=1, source_target_pairs={{0,8},{1,9},{2,10},{3,11},{4,12},{5,13},{6,14},{7,15},{8,0},{9,1},... | collective-permute-start | bytes 294920 | tf_op jit(solution)/shard_map/ppermute | solution.py:490
  122.2 12.9 %collective-permute-start.9 = (bf16[2,48,512]{2,1,0:T(8,128)(2,1)}, bf16[2,48,512]{2,1,0:T(8,128)(2,1)S(1)}, u32[]{:S(2)}, u32[]{:S(2)}) collective-permute-start(bf16[2,48,512]{2,1,0:T(8,128)(2,1)} %get-tuple-element.50), channel_id=1, source_target_pairs={{0,10},{1,11},{2,8},{3,9},{4,14},{5,15},{6,12},{7,13},{8,2},{9,3},... | collective-permute-start | bytes 294920 | tf_op jit(solution)/shard_map/ppermute | solution.py:490
  124.6 10.5 %collective-permute-start.10 = (bf16[2,48,512]{2,1,0:T(8,128)(2,1)}, bf16[2,48,512]{2,1,0:T(8,128)(2,1)S(1)}, u32[]{:S(2)}, u32[]{:S(2)}) collective-permute-start(bf16[2,48,512]{2,1,0:T(8,128)(2,1)} %get-tuple-element.51), channel_id=1, source_target_pairs={{0,12},{1,13},{2,14},{3,15},{4,8},{5,9},{6,10},{7,11},{8,4},{9,5},... | collective-permute-start | bytes 294920 | tf_op jit(solution)/shard_map/ppermute | solution.py:490
  124.7 10.4 %collective-permute-start.11 = (bf16[2,48,512]{2,1,0:T(8,128)(2,1)}, bf16[2,48,512]{2,1,0:T(8,128)(2,1)S(1)}, u32[]{:S(2)}, u32[]{:S(2)}) collective-permute-start(bf16[2,48,512]{2,1,0:T(8,128)(2,1)} %get-tuple-element.52), channel_id=1, source_target_pairs={{0,14},{1,15},{2,12},{3,13},{4,10},{5,11},{6,8},{7,9},{8,6},{9,7},... | collective-permute-start | bytes 294920 | tf_op jit(solution)/shard_map/ppermute | solution.py:490
  (16 other events, 71.5 us)

commit v8 on v7

--- a/solution.py
+++ b/solution.py
@@ -14,7 +14,7 @@
 CELLS = WIN * WIN
 CHUNKS = ((2, False, True), (2, False, True))
 TIED = 4
-LANES = 512
+LANES = 1024
 SUB = 256
 VMEM_BYTES = 60 << 20
 ROOT_HALF = 0.7071067811865476

time: 139 us -> 139 us (level)
  no operation moved by 1% of the time
where the time goes in v8:
time: 139 us; the launch traced here: 138 us
  Pallas kernels  66.6 us (48%)
  starting transfers between devices  39.8 us (29%)
  waiting for transfers between devices  15.8 us (11%)
  local copies, waits for them, and re-layouts  9.35 us (7%)
  matrix products  5.24 us (4%)
    pallas_call x2, Pallas kernels, block_stage(): pl.pallas_call(functools.partial(block_kernel, scale, split), name='block...  25.9 us
    ppermute x14, starting transfers between devices, exchange(): lax.ppermute(pieces[s], 'lon', [(j * per + r, (j ^ s) * per + r) for j in...  22.9 us
    pallas_call x2, Pallas kernels, grid_stage(): pl.pallas_call(functools.partial(grid_kernel, split_in, split_out), name=...  21 us
    pallas_call x1, Pallas kernels, mbconv(): pl.pallas_call(mbconv_kernel, name='mbconv', grid=(expanded // LANES,), i...  14.1 us
    all_to_all x2, waiting for transfers between devices, exchange(): lax.all_to_all(pieces[0], 'lon', 0, 0, axis_index_groups=groups, tiled=True)  10 us
    all_to_all x2, starting transfers between devices, exchange(): lax.all_to_all(pieces[0], 'lon', 0, 0, axis_index_groups=groups, tiled=True)  7.31 us
    unnamed x45, local copies, waits for them, and re-layouts  6.3 us
    pallas_call x2, Pallas kernels, merge_stage(): pl.pallas_call(functools.partial(merge_kernel, split), name='merge_stage'...  5.58 us
  transfers between devices with their start and end apart: 19, of which 5 were waited for; matrix products, arithmetic and copies ran while one was open for 8% of the time, Pallas kernels for 27%

profile of v8, /device:TPU:0, one launch (start us, length us, event | category | flops | bytes accessed | tf_op | source)
XLA Modules:
  0.0 138.3 jit_solution(18322078269983514195)
XLA Ops:
  1.8 5.1 %collective-permute-start.1 = (bf16[1,48,512]{2,1,0:T(8,128)(2,1)S(1)}, bf16[1,48,512]{2,1,0:T(8,128)(2,1)S(1)}, u32[]{:S(2)}, u32[]{:S(2)}) collective-permute-start(bf16[1,48,512]{2,1,0:T(8,128)(2,1)S(1)} %bitcast.28), channel_id=1, source_target_pairs={{1,0},{2,1},{3,2},{4,3},{5,4},{6,5},{7,6},{8,7},{9,8},{10,9},{11,1... | collective-permute-start | bytes 147464 | tf_op jit(solution)/shard_map/ppermute | solution.py:464
  7.0 3.4 %copy.27 = bf16[48,32,512]{2,0,1:T(8,128)(2,1)} copy(bf16[48,32,512]{2,1,0:T(8,128)(2,1)} %param.17) | data formatting | bytes 3145728 | tf_op args[0]
  11.0 14.1 %mbconv.1 = (bf16[32,48,2048]{2,1,0:T(8,128)(2,1)}, f32[16,8,128]{2,1,0:T(8,128)}) custom-call(bf16[32,48,512]{2,1,0:T(8,128)(2,1)} %bitcast.24, bf16[1,48,512]{2,1,0:T(8,128)(2,1)} %copy-done.17, bf16[1,48,512]{2,1,0:T(8,128)(2,1)} %copy-done.18, bf16[512,2048]{1,0:T(8,128)(2,1)} %w_ref.1, f32[1,2048]{1,0:T(1,128)} %bitcast.33, f32[9,2048]{1,0:T(8,128)} %dw_ref.1, ...), custom_call_target="tpu_custom_call" | custom-call | flops 12884901888 | bytes 20000000 | tf_op jit(solution)/shard_map/mbconv/pallas_call | solution.py:118
  25.1 4.1 %all-to-all-start = ((f32[16,8,128]{2,1,0:T(8,128)}), f32[16,8,128]{2,1,0:T(8,128)S(1)}, u32[]{:S(2)}, u32[]{:S(2)}) async-start(f32[16,8,128]{2,1,0:T(8,128)} %get-tuple-element.33), calls=%async_computation | async-start | bytes 131072 | tf_op jit(solution)/shard_map/all_to_all | solution.py:474
  29.2 2.6 %fusion.4 = f32[64,16,64]{2,1,0:T(8,128)S(1)} fusion(s32[64,64]{1,0:T(8,128)S(1)} %add_add_fusion, f32[225,16]{0,1:T(8,128)S(1)} %copy-done.19), kind=kOutput, calls=%fused_computation.6 | convolution fusion | flops 177872400 | bytes 292928 | tf_op jit(solution)/shard_map/jir,rh->jhi/dot_general | solution.py:414
  32.7 3.4 %all-to-all-done.part_ref = f32[16,8,128]{2,1,0:T(8,128)S(1)} async-done(((f32[16,8,128]{2,1,0:T(8,128)}), f32[16,8,128]{2,1,0:T(8,128)S(1)}, u32[]{:S(2)}, u32[]{:S(2)}) %all-to-all-start) | async-done | bytes 65568 | tf_op jit(solution)/shard_map/all_to_all | solution.py:474
  36.7 13.0 %block_stage.3 = bf16[8,2,48,512]{3,2,1,0:T(8,128)(2,1)} custom-call(s32[1]{0:T(128)} %constant.136.clone.1.me_ref, bf16[32,48,2048]{2,1,0:T(8,128)(2,1)} %get-tuple-element.32.act_ref, bf16[32,48,512]{2,1,0:T(8,128)(2,1)} %bitcast.25, f32[16,8,128]{2,1,0:T(8,128)} %copy-done.2, bf16[128,2048]{1,0:T(8,128)(2,1)} %up_ref.3, bf16[2048,512]{1,0:T(8,128)(2,1)} %proj_ref.3, ...), custom_call_target="tpu_custom_call" | custom-call | flops 1000000 | bytes 100000 | tf_op jit(solution)/shard_map/block_stage/pallas_call | solution.py:328
  49.6 3.5 %all-to-all-start.2 = ((bf16[8,2,48,512]{3,2,1,0:T(8,128)(2,1)}), bf16[8,2,48,512]{3,2,1,0:T(8,128)(2,1)S(1)}, u32[]{:S(2)}, u32[]{:S(2)}) async-start(bf16[8,2,48,512]{3,2,1,0:T(8,128)(2,1)} %block_stage.3), calls=%async_computation.2 | async-start | bytes 1572864 | tf_op jit(solution)/shard_map/all_to_all | solution.py:485
  53.2 2.6 %fusion.5 = f32[64,16,64]{2,1,0:T(8,128)S(1)} fusion(s32[64,64]{1,0:T(8,128)S(1)} %add_add_fusion, f32[225,16]{0,1:T(8,128)S(1)} %copy-done.20), kind=kOutput, calls=%fused_computation.7 | convolution fusion | flops 177872400 | bytes 292928 | tf_op jit(solution)/shard_map/jir,rh->jhi/dot_general | solution.py:414
  57.8 13.0 %block_stage.2 = bf16[8,2,48,512]{3,2,1,0:T(8,128)(2,1)} custom-call(s32[1]{0:T(128)} %constant.136.clone.1.me_ref, bf16[32,48,2048]{2,1,0:T(8,128)(2,1)} %get-tuple-element.32.act_ref, bf16[32,48,512]{2,1,0:T(8,128)(2,1)} %bitcast.26, f32[16,8,128]{2,1,0:T(8,128)} %copy-done.2, bf16[128,2048]{1,0:T(8,128)(2,1)} %up_ref.3, bf16[2048,512]{1,0:T(8,128)(2,1)} %proj_ref.3, ...), custom_call_target="tpu_custom_call" | custom-call | flops 1000000 | bytes 100000 | tf_op jit(solution)/shard_map/block_stage/pallas_call | solution.py:328
  70.8 2.5 %all-to-all-done.2.refs_0_ = bf16[8,2,48,512]{3,2,1,0:T(8,128)(2,1)S(1)} async-done(((bf16[8,2,48,512]{3,2,1,0:T(8,128)(2,1)}), bf16[8,2,48,512]{3,2,1,0:T(8,128)(2,1)S(1)}, u32[]{:S(2)}, u32[]{:S(2)}) %all-to-all-start.2) | async-done | bytes 786464 | tf_op jit(solution)/shard_map/all_to_all | solution.py:485
  73.3 3.8 %all-to-all-start.1 = ((bf16[8,2,48,512]{3,2,1,0:T(8,128)(2,1)}), bf16[8,2,48,512]{3,2,1,0:T(8,128)(2,1)S(1)}, u32[]{:S(2)}, u32[]{:S(2)}) async-start(bf16[8,2,48,512]{3,2,1,0:T(8,128)(2,1)} %block_stage.2), calls=%async_computation.1 | async-start | bytes 1572864 | tf_op jit(solution)/shard_map/all_to_all | solution.py:485
  77.1 10.5 %grid_stage.2 = (bf16[2,48,512]{2,1,0:T(8,128)(2,1)}, bf16[2,48,512]{2,1,0:T(8,128)(2,1)}, bf16[2,48,512]{2,1,0:T(8,128)(2,1)}, bf16[2,48,512]{2,1,0:T(8,128)(2,...) custom-call(s32[1]{0:T(128)} %bitcast.me_ref, ...), custom_call_target="tpu_custom_call" | custom-call | flops 1000000 | bytes 100000 | tf_op jit(solution)/shard_map/grid_stage/pallas_call | solution.py:359
  87.6 1.8 %collective-permute-start.2 = (bf16[2,48,512]{2,1,0:T(8,128)(2,1)}, bf16[2,48,512]{2,1,0:T(8,128)(2,1)S(1)}, u32[]{:S(2)}, u32[]{:S(2)}) collective-permute-start(bf16[2,48,512]{2,1,0:T(8,128)(2,1)} %get-tuple-element.41), channel_id=1, source_target_pairs={{0,2},{1,3},{2,0},{3,1},{4,6},{5,7},{6,4},{7,5},{8,10},{9,11},{10,... | collective-permute-start | bytes 294920 | tf_op jit(solution)/shard_map/ppermute | solution.py:490
  91.1 2.6 %collective-permute-start.12 = (bf16[2,48,512]{2,1,0:T(8,128)(2,1)}, bf16[2,48,512]{2,1,0:T(8,128)(2,1)S(1)}, u32[]{:S(2)}, u32[]{:S(2)}) collective-permute-start(bf16[2,48,512]{2,1,0:T(8,128)(2,1)} %get-tuple-element.55), channel_id=1, source_target_pairs={{0,8},{1,9},{2,10},{3,11},{4,12},{5,13},{6,14},{7,15},{8,0},{9,1},... | collective-permute-start | bytes 294920 | tf_op jit(solution)/shard_map/ppermute | solution.py:490
  95.2 3.3 %collective-permute-start.14 = (bf16[2,48,512]{2,1,0:T(8,128)(2,1)}, bf16[2,48,512]{2,1,0:T(8,128)(2,1)S(1)}, u32[]{:S(2)}, u32[]{:S(2)}) collective-permute-start(bf16[2,48,512]{2,1,0:T(8,128)(2,1)} %get-tuple-element.57), channel_id=1, source_target_pairs={{0,12},{1,13},{2,14},{3,15},{4,8},{5,9},{6,10},{7,11},{8,4},{9,5},... | collective-permute-start | bytes 294920 | tf_op jit(solution)/shard_map/ppermute | solution.py:490
  99.4 7.5 %all-to-all-done.1.refs_0_ = bf16[8,2,48,512]{3,2,1,0:T(8,128)(2,1)S(1)} async-done(((bf16[8,2,48,512]{3,2,1,0:T(8,128)(2,1)}), bf16[8,2,48,512]{3,2,1,0:T(8,128)(2,1)S(1)}, u32[]{:S(2)}, u32[]{:S(2)}) %all-to-all-start.1) | async-done | bytes 786464 | tf_op jit(solution)/shard_map/all_to_all | solution.py:485
  107.7 10.5 %grid_stage.3 = (bf16[2,48,512]{2,1,0:T(8,128)(2,1)}, bf16[2,48,512]{2,1,0:T(8,128)(2,1)}, bf16[2,48,512]{2,1,0:T(8,128)(2,1)}, bf16[2,48,512]{2,1,0:T(8,128)(2,...) custom-call(s32[1]{0:T(128)} %bitcast.me_ref, ...), custom_call_target="tpu_custom_call" | custom-call | flops 1000000 | bytes 100000 | tf_op jit(solution)/shard_map/grid_stage/pallas_call | solution.py:359
  118.4 3.4 %collective-permute-start.7 = (bf16[2,48,512]{2,1,0:T(8,128)(2,1)}, bf16[2,48,512]{2,1,0:T(8,128)(2,1)S(1)}, u32[]{:S(2)}, u32[]{:S(2)}) collective-permute-start(bf16[2,48,512]{2,1,0:T(8,128)(2,1)} %get-tuple-element.48), channel_id=1, source_target_pairs={{0,6},{1,7},{2,4},{3,5},{4,2},{5,3},{6,0},{7,1},{8,14},{9,15},{10,... | collective-permute-start | bytes 294920 | tf_op jit(solution)/shard_map/ppermute | solution.py:490
  121.8 2.4 %collective-permute-start.9 = (bf16[2,48,512]{2,1,0:T(8,128)(2,1)}, bf16[2,48,512]{2,1,0:T(8,128)(2,1)S(1)}, u32[]{:S(2)}, u32[]{:S(2)}) collective-permute-start(bf16[2,48,512]{2,1,0:T(8,128)(2,1)} %get-tuple-element.50), channel_id=1, source_target_pairs={{0,10},{1,11},{2,8},{3,9},{4,14},{5,15},{6,12},{7,13},{8,2},{9,3},... | collective-permute-start | bytes 294920 | tf_op jit(solution)/shard_map/ppermute | solution.py:490
  124.4 5.1 %collective-permute-start.11 = (bf16[2,48,512]{2,1,0:T(8,128)(2,1)}, bf16[2,48,512]{2,1,0:T(8,128)(2,1)S(1)}, u32[]{:S(2)}, u32[]{:S(2)}) collective-permute-start(bf16[2,48,512]{2,1,0:T(8,128)(2,1)} %get-tuple-element.52), channel_id=1, source_target_pairs={{0,14},{1,15},{2,12},{3,13},{4,10},{5,11},{6,8},{7,9},{8,6},{9,7},... | collective-permute-start | bytes 294920 | tf_op jit(solution)/shard_map/ppermute | solution.py:490
  129.5 2.8 %merge_stage.2.refs_9_ = bf16[48,32,512]{2,1,0:T(8,128)(2,1)} custom-call(s32[1]{0:T(128)} %bitcast.me_ref, bf16[2,48,512]{2,1,0:T(8,128)(2,1)} %get-tuple-element.54.refs_0_, bf16[2,48,512]{2,1,0:T(8,128)(2,1)} %copy-done.3, bf16[2,48,512]{2,1,0:T(8,128)(2,1)} %copy-done.4, bf16[2,48,512]{2,1,0:T(8,128)(2,1)} %copy-done.5, bf16[2,48,512]{2,1,0:T(8,128)(2,1)} %copy-done.6, ...), custom_call_target="tpu_custom_call" | custom-call | flops 1000000 | bytes 100000 | tf_op jit(solution)/shard_map/merge_stage/pallas_call | solution.py:386
  133.0 1.8 %collective-permute-done.9.refs_5_ = bf16[2,48,512]{2,1,0:T(8,128)(2,1)S(1)} collective-permute-done((bf16[2,48,512]{2,1,0:T(8,128)(2,1)}, bf16[2,48,512]{2,1,0:T(8,128)(2,1)S(1)}, u32[]{:S(2)}, u32[]{:S(2)}) %collective-permute-start.9) | collective-permute-done | bytes 98336 | tf_op jit(solution)/shard_map/ppermute | solution.py:490
  135.5 2.8 %merge_stage.3 = bf16[48,32,512]{2,1,0:T(8,128)(2,1)} custom-call(s32[1]{0:T(128)} %bitcast.me_ref, bf16[2,48,512]{2,1,0:T(8,128)(2,1)} %get-tuple-element.45.refs_0_, bf16[2,48,512]{2,1,0:T(8,128)(2,1)} %copy-done.10, bf16[2,48,512]{2,1,0:T(8,128)(2,1)} %copy-done.11, bf16[2,48,512]{2,1,0:T(8,128)(2,1)} %copy-done.12, ...), custom_call_target="tpu_custom_call", output_to_operand_aliasing={{}: (10, {})} | custom-call | flops 1000000 | bytes 100000 | tf_op jit(solution)/shard_map/merge_stage/pallas_call | solution.py:386
  (76 shorter events, 12.6 us)
Async XLA Ops:
  1.3 9.1 %collective-permute-start = (bf16[1,48,512]{2,1,0:T(8,128)(2,1)S(1)}, bf16[1,48,512]{2,1,0:T(8,128)(2,1)S(1)}, u32[]{:S(2)}, u32[]{:S(2)}) collective-permute-start(bf16[1,48,512]{2,1,0:T(8,128)(2,1)S(1)} %bitcast.27), channel_id=1, source_target_pairs={{0,1},{1,2},{2,3},{3,4},{4,5},{5,6},{6,7},{7,8},{8,9},{9,10},{10,1... | collective-permute-start | bytes 147464 | tf_op jit(solution)/shard_map/ppermute | solution.py:459
  1.8 8.6 %collective-permute-start.1 = (bf16[1,48,512]{2,1,0:T(8,128)(2,1)S(1)}, bf16[1,48,512]{2,1,0:T(8,128)(2,1)S(1)}, u32[]{:S(2)}, u32[]{:S(2)}) collective-permute-start(bf16[1,48,512]{2,1,0:T(8,128)(2,1)S(1)} %bitcast.28), channel_id=1, source_target_pairs={{1,0},{2,1},{3,2},{4,3},{5,4},{6,5},{7,6},{8,7},{9,8},{10,9},{11,1... | collective-permute-start | bytes 147464 | tf_op jit(solution)/shard_map/ppermute | solution.py:464
  11.0 18.1 %copy-start.19 = (f32[225,16]{0,1:T(8,128)S(1)}, f32[225,16]{0,1:T(8,128)}, u32[]{:S(2)}) copy-start(f32[225,16]{0,1:T(8,128)} %param.28) | copy-start | bytes 43204
  25.1 11.0 %all-to-all-start = ((f32[16,8,128]{2,1,0:T(8,128)}), f32[16,8,128]{2,1,0:T(8,128)S(1)}, u32[]{:S(2)}, u32[]{:S(2)}) async-start(f32[16,8,128]{2,1,0:T(8,128)} %get-tuple-element.33), calls=%async_computation | async-start | bytes 131072 | tf_op jit(solution)/shard_map/all_to_all | solution.py:474
  36.7 16.5 %copy-start.20 = (f32[225,16]{0,1:T(8,128)S(1)}, f32[225,16]{0,1:T(8,128)}, u32[]{:S(2)}) copy-start(f32[225,16]{0,1:T(8,128)} %param.32) | copy-start | bytes 43204
  49.6 23.7 %all-to-all-start.2 = ((bf16[8,2,48,512]{3,2,1,0:T(8,128)(2,1)}), bf16[8,2,48,512]{3,2,1,0:T(8,128)(2,1)S(1)}, u32[]{:S(2)}, u32[]{:S(2)}) async-start(bf16[8,2,48,512]{3,2,1,0:T(8,128)(2,1)} %block_stage.3), calls=%async_computation.2 | async-start | bytes 1572864 | tf_op jit(solution)/shard_map/all_to_all | solution.py:485
  73.3 33.5 %all-to-all-start.1 = ((bf16[8,2,48,512]{3,2,1,0:T(8,128)(2,1)}), bf16[8,2,48,512]{3,2,1,0:T(8,128)(2,1)S(1)}, u32[]{:S(2)}, u32[]{:S(2)}) async-start(bf16[8,2,48,512]{3,2,1,0:T(8,128)(2,1)} %block_stage.2), calls=%async_computation.1 | async-start | bytes 1572864 | tf_op jit(solution)/shard_map/all_to_all | solution.py:485
  87.6 7.6 %collective-permute-start.2 = (bf16[2,48,512]{2,1,0:T(8,128)(2,1)}, bf16[2,48,512]{2,1,0:T(8,128)(2,1)S(1)}, u32[]{:S(2)}, u32[]{:S(2)}) collective-permute-start(bf16[2,48,512]{2,1,0:T(8,128)(2,1)} %get-tuple-element.41), channel_id=1, source_target_pairs={{0,2},{1,3},{2,0},{3,1},{4,6},{5,7},{6,4},{7,5},{8,10},{9,11},{10,... | collective-permute-start | bytes 294920 | tf_op jit(solution)/shard_map/ppermute | solution.py:490
  89.4 9.1 %collective-permute-start.3 = (bf16[2,48,512]{2,1,0:T(8,128)(2,1)}, bf16[2,48,512]{2,1,0:T(8,128)(2,1)S(1)}, u32[]{:S(2)}, u32[]{:S(2)}) collective-permute-start(bf16[2,48,512]{2,1,0:T(8,128)(2,1)} %get-tuple-element.42), channel_id=1, source_target_pairs={{0,4},{1,5},{2,6},{3,7},{4,0},{5,1},{6,2},{7,3},{8,12},{9,13},{10,... | collective-permute-start | bytes 294920 | tf_op jit(solution)/shard_map/ppermute | solution.py:490
  90.8 16.0 %collective-permute-start.4 = (bf16[2,48,512]{2,1,0:T(8,128)(2,1)}, bf16[2,48,512]{2,1,0:T(8,128)(2,1)S(1)}, u32[]{:S(2)}, u32[]{:S(2)}) collective-permute-start(bf16[2,48,512]{2,1,0:T(8,128)(2,1)} %get-tuple-element.43), channel_id=1, source_target_pairs={{0,6},{1,7},{2,4},{3,5},{4,2},{5,3},{6,0},{7,1},{8,14},{9,15},{10,... | collective-permute-start | bytes 294920 | tf_op jit(solution)/shard_map/ppermute | solution.py:490
  91.1 27.2 %collective-permute-start.12 = (bf16[2,48,512]{2,1,0:T(8,128)(2,1)}, bf16[2,48,512]{2,1,0:T(8,128)(2,1)S(1)}, u32[]{:S(2)}, u32[]{:S(2)}) collective-permute-start(bf16[2,48,512]{2,1,0:T(8,128)(2,1)} %get-tuple-element.55), channel_id=1, source_target_pairs={{0,8},{1,9},{2,10},{3,11},{4,12},{5,13},{6,14},{7,15},{8,0},{9,1},... | collective-permute-start | bytes 294920 | tf_op jit(solution)/shard_map/ppermute | solution.py:490
  93.8 24.6 %collective-permute-start.13 = (bf16[2,48,512]{2,1,0:T(8,128)(2,1)}, bf16[2,48,512]{2,1,0:T(8,128)(2,1)S(1)}, u32[]{:S(2)}, u32[]{:S(2)}) collective-permute-start(bf16[2,48,512]{2,1,0:T(8,128)(2,1)} %get-tuple-element.56), channel_id=1, source_target_pairs={{0,10},{1,11},{2,8},{3,9},{4,14},{5,15},{6,12},{7,13},{8,2},{9,3},... | collective-permute-start | bytes 294920 | tf_op jit(solution)/shard_map/ppermute | solution.py:490
  95.2 34.2 %copy-start.3 = (bf16[2,48,512]{2,1,0:T(8,128)(2,1)}, bf16[2,48,512]{2,1,0:T(8,128)(2,1)S(1)}, u32[]{:S(2)}) copy-start(bf16[2,48,512]{2,1,0:T(8,128)(2,1)S(1)} %collective-permute-done.2.refs_1_) | copy-start | bytes 294916
  95.2 26.6 %collective-permute-start.14 = (bf16[2,48,512]{2,1,0:T(8,128)(2,1)}, bf16[2,48,512]{2,1,0:T(8,128)(2,1)S(1)}, u32[]{:S(2)}, u32[]{:S(2)}) collective-permute-start(bf16[2,48,512]{2,1,0:T(8,128)(2,1)} %get-tuple-element.57), channel_id=1, source_target_pairs={{0,12},{1,13},{2,14},{3,15},{4,8},{5,9},{6,10},{7,11},{8,4},{9,5},... | collective-permute-start | bytes 294920 | tf_op jit(solution)/shard_map/ppermute | solution.py:490
  98.5 31.0 %copy-start.4 = (bf16[2,48,512]{2,1,0:T(8,128)(2,1)}, bf16[2,48,512]{2,1,0:T(8,128)(2,1)S(1)}, u32[]{:S(2)}) copy-start(bf16[2,48,512]{2,1,0:T(8,128)(2,1)S(1)} %collective-permute-done.3.refs_2_) | copy-start | bytes 294916
  98.5 23.3 %collective-permute-start.15 = (bf16[2,48,512]{2,1,0:T(8,128)(2,1)}, bf16[2,48,512]{2,1,0:T(8,128)(2,1)S(1)}, u32[]{:S(2)}, u32[]{:S(2)}) collective-permute-start(bf16[2,48,512]{2,1,0:T(8,128)(2,1)} %get-tuple-element.58), channel_id=1, source_target_pairs={{0,14},{1,15},{2,12},{3,13},{4,10},{5,11},{6,8},{7,9},{8,6},{9,7},... | collective-permute-start | bytes 294920 | tf_op jit(solution)/shard_map/ppermute | solution.py:490
  107.7 21.8 %copy-start.5 = (bf16[2,48,512]{2,1,0:T(8,128)(2,1)}, bf16[2,48,512]{2,1,0:T(8,128)(2,1)S(1)}, u32[]{:S(2)}) copy-start(bf16[2,48,512]{2,1,0:T(8,128)(2,1)S(1)} %collective-permute-done.4.refs_3_) | copy-start | bytes 294916
  118.2 6.0 %collective-permute-start.5 = (bf16[2,48,512]{2,1,0:T(8,128)(2,1)}, bf16[2,48,512]{2,1,0:T(8,128)(2,1)S(1)}, u32[]{:S(2)}, u32[]{:S(2)}) collective-permute-start(bf16[2,48,512]{2,1,0:T(8,128)(2,1)} %get-tuple-element.46), channel_id=1, source_target_pairs={{0,2},{1,3},{2,0},{3,1},{4,6},{5,7},{6,4},{7,5},{8,10},{9,11},{10,... | collective-permute-start | bytes 294920 | tf_op jit(solution)/shard_map/ppermute | solution.py:490
  118.3 6.0 %collective-permute-start.6 = (bf16[2,48,512]{2,1,0:T(8,128)(2,1)}, bf16[2,48,512]{2,1,0:T(8,128)(2,1)S(1)}, u32[]{:S(2)}, u32[]{:S(2)}) collective-permute-start(bf16[2,48,512]{2,1,0:T(8,128)(2,1)} %get-tuple-element.47), channel_id=1, source_target_pairs={{0,4},{1,5},{2,6},{3,7},{4,0},{5,1},{6,2},{7,3},{8,12},{9,13},{10,... | collective-permute-start | bytes 294920 | tf_op jit(solution)/shard_map/ppermute | solution.py:490
  118.4 13.9 %collective-permute-start.7 = (bf16[2,48,512]{2,1,0:T(8,128)(2,1)}, bf16[2,48,512]{2,1,0:T(8,128)(2,1)S(1)}, u32[]{:S(2)}, u32[]{:S(2)}) collective-permute-start(bf16[2,48,512]{2,1,0:T(8,128)(2,1)} %get-tuple-element.48), channel_id=1, source_target_pairs={{0,6},{1,7},{2,4},{3,5},{4,2},{5,3},{6,0},{7,1},{8,14},{9,15},{10,... | collective-permute-start | bytes 294920 | tf_op jit(solution)/shard_map/ppermute | solution.py:490
  121.8 11.1 %collective-permute-start.8 = (bf16[2,48,512]{2,1,0:T(8,128)(2,1)}, bf16[2,48,512]{2,1,0:T(8,128)(2,1)S(1)}, u32[]{:S(2)}, u32[]{:S(2)}) collective-permute-start(bf16[2,48,512]{2,1,0:T(8,128)(2,1)} %get-tuple-element.49), channel_id=1, source_target_pairs={{0,8},{1,9},{2,10},{3,11},{4,12},{5,13},{6,14},{7,15},{8,0},{9,1},... | collective-permute-start | bytes 294920 | tf_op jit(solution)/shard_map/ppermute | solution.py:490
  121.8 12.9 %collective-permute-start.9 = (bf16[2,48,512]{2,1,0:T(8,128)(2,1)}, bf16[2,48,512]{2,1,0:T(8,128)(2,1)S(1)}, u32[]{:S(2)}, u32[]{:S(2)}) collective-permute-start(bf16[2,48,512]{2,1,0:T(8,128)(2,1)} %get-tuple-element.50), channel_id=1, source_target_pairs={{0,10},{1,11},{2,8},{3,9},{4,14},{5,15},{6,12},{7,13},{8,2},{9,3},... | collective-permute-start | bytes 294920 | tf_op jit(solution)/shard_map/ppermute | solution.py:490
  124.3 10.5 %collective-permute-start.10 = (bf16[2,48,512]{2,1,0:T(8,128)(2,1)}, bf16[2,48,512]{2,1,0:T(8,128)(2,1)S(1)}, u32[]{:S(2)}, u32[]{:S(2)}) collective-permute-start(bf16[2,48,512]{2,1,0:T(8,128)(2,1)} %get-tuple-element.51), channel_id=1, source_target_pairs={{0,12},{1,13},{2,14},{3,15},{4,8},{5,9},{6,10},{7,11},{8,4},{9,5},... | collective-permute-start | bytes 294920 | tf_op jit(solution)/shard_map/ppermute | solution.py:490
  124.4 10.4 %collective-permute-start.11 = (bf16[2,48,512]{2,1,0:T(8,128)(2,1)}, bf16[2,48,512]{2,1,0:T(8,128)(2,1)S(1)}, u32[]{:S(2)}, u32[]{:S(2)}) collective-permute-start(bf16[2,48,512]{2,1,0:T(8,128)(2,1)} %get-tuple-element.52), channel_id=1, source_target_pairs={{0,14},{1,15},{2,12},{3,13},{4,10},{5,11},{6,8},{7,9},{8,6},{9,7},... | collective-permute-start | bytes 294920 | tf_op jit(solution)/shard_map/ppermute | solution.py:490
  (16 other events, 71.5 us)
